TPU v7x, 256 devices: a whole 4x4x8 slice. The times are simulated.
256 devices in a mesh: gx: 16 (over z, x_hi), gy: 16 (over x_lo, y, core).
Axes of the slice: x: 4 (x_hi: 2, x_lo: 2; x = x_hi * 2 + x_lo), y: 4, z: 8, core: 2. Of those that a mesh axis runs over, the one named last changes fastest.
Arguments:
- electric: float32 [2, 3, 512, 32768], P(None, None, 'gx', 'gy'), may hold values from -6 to 6
- magnetic: float32 [2, 3, 512, 32768], P(None, None, 'gx', 'gy'), may hold values from -6 to 6
- permittivity: float32 [512, 32768], P('gx', 'gy'), may hold values from 1 to 12
- source_profile: float32 [2, 512, 1024], P(None, 'gx', 'gy'), may hold values from -6 to 6
- source_plane: int32 [2, 512], P(None, 'gx'), may hold values from 0 to 31
- block_owner: int32 [16, 16, 16, 1], P('gx', 'gy'), may hold values from 0 to 15; in each aligned block of 16 rows (0 to 15, 16 to 31, ..., all dimensions but the last counted through in order) at most 2 rows name the same one
- design_slot: int32 [16, 16, 16], P('gx', 'gy'), may hold values from 0 to 3
- filter_matrix: float32 [128, 128], replicated, may hold values from -0.5 to 0.5
Outputs:
- electric_out: float32 [2, 3, 512, 32768], P(None, None, 'gx', 'gy')
- magnetic_out: float32 [2, 3, 512, 32768], P(None, None, 'gx', 'gy')
- design_grad: float32 [16, 64, 128], P('gx', 'gy')
Inputs may be any that keep to these rules, and one draw needn't show every extreme that they name: `block_owner`: among the 16 blocks of one device no owner appears more than 2 times, and some owner appears exactly 2 times on some device.
All inputs are finite; a program needn't handle non-finite values.
Results may differ from a plain program's by a relative error of at most 0.00016.
Values sent between devices are 32-bit elements; how exact they have to be, the bound alone decides.
No kernel may reach another device: no remote copies, remote signals or barrier semaphores. Data moves between devices by JAX's collectives and lax.ppermute only.
A program may use at most 192 MiB of HBM per device.

v0:
```python
import jax
import jax.numpy as jnp
from jax import lax
from jax.sharding import PartitionSpec as P

NZ = 32
STEPS = 12
BROWS = 2
DB_DEV = 4


time_step = 0.5
omega_source = 1.3


def shifted(array, axis, by):
    count = lax.axis_size(axis)
    return lax.ppermute(array, axis, [(i, (i + by) % count) for i in range(count)])


def upper_z(field, keep):
    return jnp.where(
        keep, jnp.concatenate([field[..., 1:], jnp.zeros_like(field[..., :1])], -1), 0.0
    )


def lower_z(field, keep):
    return jnp.where(
        keep, jnp.concatenate([jnp.zeros_like(field[..., :1]), field[..., :-1]], -1), 0.0
    )


def update_electric(
    ex,
    ey,
    ez,
    hx,
    hy,
    hz,
    hy_prev_x,
    hz_prev_x,
    hx_prev_y,
    hz_prev_y,
    inverse,
    source,
    step,
    keep_down,
):
    cx = hz - hz_prev_y - (hy - lower_z(hy, keep_down))
    cy = hx - lower_z(hx, keep_down) - (hz - hz_prev_x)
    cz = hy - hy_prev_x - (hx - hx_prev_y)
    wave = jnp.sin(jnp.asarray(step + 1).astype(jnp.float32) * (omega_source * time_step))
    new_x = ex + time_step * inverse * cx + time_step * wave * source
    new_y = ey + time_step * inverse * cy
    new_z = ez + time_step * inverse * cz
    return (new_x, new_y, new_z)


def per_device(
    electric,
    magnetic,
    permittivity,
    source_profile,
    source_plane,
    block_owner,
    design_slot,
    filter_matrix,
):
    rows = electric.shape[2]
    length = electric.shape[3]
    depth = NZ
    columns = length // depth
    position = jnp.arange(length, dtype=jnp.int32) % depth
    keep_up = position != depth - 1
    keep_down = position != 0
    inverse = 1.0 / permittivity
    level = jnp.arange(depth, dtype=jnp.int32)
    source = (
        source_profile[:, :, :, None]
        * (level[None, None, None, :] == source_plane[:, :, None, None]).astype(jnp.float32)
    ).reshape(2, rows, length)

    def advance(step, carry):
        ex, ey, ez, hx, hy, hz, accum = carry
        front = shifted((ey[:, 0:1], ez[:, 0:1]), "gx", -1)
        beside = shifted((ex[:, :, 0:depth], ez[:, :, 0:depth]), "gy", -1)
        ey_next_x = jnp.concatenate([ey[:, 1:], front[0]], 1)
        ez_next_x = jnp.concatenate([ez[:, 1:], front[1]], 1)
        ex_next_y = jnp.concatenate([ex[:, :, depth:], beside[0]], -1)
        ez_next_y = jnp.concatenate([ez[:, :, depth:], beside[1]], -1)
        curl_x = ez_next_y - ez - (upper_z(ey, keep_up) - ey)
        curl_y = upper_z(ex, keep_up) - ex - (ez_next_x - ez)
        curl_z = ey_next_x - ey - (ex_next_y - ex)
        hx = hx - time_step * curl_x
        hy = hy - time_step * curl_y
        hz = hz - time_step * curl_z
        behind = shifted((hy[:, rows - 1 : rows], hz[:, rows - 1 : rows]), "gx", 1)
        below = shifted((hx[:, :, length - depth :], hz[:, :, length - depth :]), "gy", 1)
        hy_prev_x = jnp.concatenate([behind[0], hy[:, :-1]], 1)
        hz_prev_x = jnp.concatenate([behind[1], hz[:, :-1]], 1)
        hx_prev_y = jnp.concatenate([below[0], hx[:, :, :-depth]], -1)
        hz_prev_y = jnp.concatenate([below[1], hz[:, :, :-depth]], -1)
        new_x, new_y, new_z = update_electric(
            ex,
            ey,
            ez,
            hx,
            hy,
            hz,
            hy_prev_x,
            hz_prev_x,
            hx_prev_y,
            hz_prev_y,
            inverse,
            source,
            step,
            keep_down,
        )
        accum = accum + (new_x[0] * new_x[1] + new_y[0] * new_y[1] + new_z[0] * new_z[1])
        return (new_x, new_y, new_z, hx, hy, hz, accum)

    start = (
        electric[:, 0],
        electric[:, 1],
        electric[:, 2],
        magnetic[:, 0],
        magnetic[:, 1],
        magnetic[:, 2],
        jnp.zeros((rows, length), jnp.float32),
    )
    ex, ey, ez, hx, hy, hz, accum = lax.fori_loop(0, STEPS, advance, start)
    field_e = jnp.stack([ex, ey, ez], 1)
    field_h = jnp.stack([hx, hy, hz], 1)
    total = accum.reshape(rows, columns, depth).sum(-1) / (STEPS * depth)
    count = rows // BROWS
    blocks = total.reshape(count, BROWS * columns)
    owner = block_owner[0, 0, :, 0]
    slot = design_slot[0, 0, :]
    owners = lax.axis_size("gy")
    capacity = max(2, (count + owners - 1) // owners)
    index = jnp.arange(count, dtype=jnp.int32)
    earlier = (
        ((owner[:, None] == owner[None, :]) & (index[None, :] < index[:, None]))
        .astype(jnp.int32)
        .sum(1)
    )
    target = owner * capacity + earlier
    places = owners * capacity
    select = jnp.arange(places, dtype=jnp.int32)[:, None] == target[None, :]
    packed = jnp.dot(
        select.astype(jnp.float32),
        blocks,
        precision=lax.Precision.HIGHEST,
        preferred_element_type=jnp.float32,
    ).reshape(owners, capacity, BROWS * columns)
    labels = jnp.sum(
        jnp.where(select, (slot[None, :] + 1).astype(jnp.float32), 0.0), axis=1
    ).reshape(owners, capacity)
    received, received_labels = (
        lax.all_to_all(packed, "gy", split_axis=0, concat_axis=0, tiled=True),
        lax.all_to_all(labels, "gy", split_axis=0, concat_axis=0, tiled=True),
    )
    choose = (
        (jnp.arange(DB_DEV, dtype=jnp.int32)[:, None] + 1).astype(jnp.float32)
        == received_labels.reshape(1, places)
    ).astype(jnp.float32)
    design = jnp.dot(
        choose,
        received.reshape(places, BROWS * columns),
        precision=lax.Precision.HIGHEST,
        preferred_element_type=jnp.float32,
    )
    result = jnp.dot(
        design, filter_matrix, precision=lax.Precision.HIGHEST, preferred_element_type=jnp.float32
    )
    return (field_e, field_h, result[None])


def solution(mesh):
    placed = (
        P(None, None, "gx", "gy"),
        P(None, None, "gx", "gy"),
        P("gx", "gy"),
        P(None, "gx", "gy"),
        P(None, "gx"),
        P("gx", "gy", None, None),
        P("gx", "gy", None),
        P(),
    )
    return jax.shard_map(
        per_device,
        mesh=mesh,
        in_specs=placed,
        out_specs=(P(None, None, "gx", "gy"), P(None, None, "gx", "gy"), P("gx", "gy", None)),
        check_vma=False,
    )
```

profile of v0, /device:TPU:1, one launch (start us, length us, event | category | flops | bytes accessed | tf_op | source)
XLA Modules:
  0.0 388.6 jit_solution(10946459047130577718)
XLA Ops:
  3.7 7.1 %all-to-all-start = ((f32[16,1,2]{2,1,0:T(1,128)}), f32[16,1,2]{2,1,0:T(1,128)}, u32[]{:S(2)}, u32[]{:S(2)}) async-start(f32[16,1,2]{2,1,0:T(1,128)} %bitcast.14), calls=%async_computation | async-start | bytes 16384 | tf_op jit(solution)/shard_map/all_to_all | solution.py:161
  15.9 350.9 %while.27 = (s32[]{:T(128)}, f32[2,32,2048]{2,1,0:T(8,128)S(1)}, f32[2,32,2048]{2,1,0:T(8,128)S(1)}, f32[2,32,2048]{2,1,0:T(8,128)S(1)}, f32[2,32,2048]{2,1,0:T(...) while((s32[]{:T(128)}, f32[2,32,2048]{2,1,0:T(8,128)S(1)}, ...), condition=%wide.region_1.2_spmd.clone.clone, body=%wide.region_0.1_spmd.clone.clone.sunk | while | flops 6451206 | bytes 33036920 | solution.py:131
  16.3 7.5 %collective-permute-start.1 = (f32[2,1,2048]{2,1,0:T(1,128)S(1)}, f32[2,1,2048]{2,1,0:T(1,128)S(1)}, u32[]{:S(2)}, u32[]{:S(2)}) collective-permute-start(f32[2,1,2048]{2,1,0:T(1,128)S(1)} %slice.327), channel_id=1, source_target_pairs={{0,240},{16,0},{32,16},{48,32},{64,48},{80,64},{96,80},{112,96},{1... | collective-permute-start | bytes 49160 | tf_op jit(solution)/shard_map/while/body/eval_jaxpr/ppermute | solution.py:18
  23.8 4.0 %collective-permute-start.2 = (f32[2,32,32]{2,1,0:T(8,128)S(1)}, f32[2,32,32]{2,1,0:T(8,128)S(1)}, u32[]{:S(2)}, u32[]{:S(2)}) collective-permute-start(f32[2,32,32]{2,1,0:T(8,128)S(1)} %slice.330), channel_id=1, source_target_pairs={{0,15},{1,0},{2,1},{3,2},{4,3},{5,4},{6,5},{7,6},{8,7},{9,8},{10,9... | collective-permute-start | bytes 24584 | tf_op jit(solution)/shard_map/while/body/eval_jaxpr/ppermute | solution.py:18
  34.3 2.5 collective-permute-start.6
  37.4 3.1 mul.275
  42.3 4.8 %collective-permute-done.4 = f32[2,1,2048]{2,1,0:T(1,128)S(1)} collective-permute-done((f32[2,1,2048]{2,1,0:T(1,128)S(1)}, f32[2,1,2048]{2,1,0:T(1,128)S(1)}, u32[]{:S(2)}, u32[]{:S(2)}) %collective-permute-start.4) | collective-permute-done | bytes 16416 | tf_op jit(solution)/shard_map/while/body/eval_jaxpr/ppermute | solution.py:18
  52.4 2.9 collective-permute-start.2
  64.9 3.1 mul.275
  68.3 2.8 collective-permute-start.4
  72.2 2.3 collective-permute-done.4
  76.4 3.2 collective-permute-start
  81.4 2.9 collective-permute-start.2
  93.9 3.1 mul.275
  97.3 2.7 collective-permute-start.4
  101.2 2.4 collective-permute-done.4
  105.5 3.2 collective-permute-start
  110.5 2.9 collective-permute-start.2
  122.9 3.1 mul.275
  126.3 2.7 collective-permute-start.4
  130.2 2.4 collective-permute-done.4
  134.5 3.2 collective-permute-start
  139.5 2.9 collective-permute-start.2
  151.9 3.1 mul.275
  155.3 2.7 collective-permute-start.4
  159.3 2.4 collective-permute-done.4
  163.5 3.2 collective-permute-start
  168.5 2.9 collective-permute-start.2
  181.0 3.1 mul.275
  184.4 2.7 collective-permute-start.4
  188.3 2.4 collective-permute-done.4
  192.6 3.2 collective-permute-start
  197.6 2.9 collective-permute-start.2
  210.0 3.1 mul.275
  213.4 2.7 collective-permute-start.4
  217.3 2.4 collective-permute-done.4
  221.6 3.2 collective-permute-start
  226.6 2.9 collective-permute-start.2
  239.0 3.1 mul.275
  242.4 2.7 collective-permute-start.4
  246.4 2.4 collective-permute-done.4
  250.6 3.2 collective-permute-start
  255.6 2.9 collective-permute-start.2
  268.1 3.1 mul.275
  271.5 2.7 collective-permute-start.4
  275.4 2.4 collective-permute-done.4
  279.6 3.2 collective-permute-start
  284.7 2.9 collective-permute-start.2
  297.1 3.1 mul.275
  300.5 2.7 collective-permute-start.4
  304.4 2.4 collective-permute-done.4
  308.7 3.2 collective-permute-start
  313.7 2.9 collective-permute-start.2
  326.1 3.1 mul.275
  329.5 2.7 collective-permute-start.4
  333.5 2.4 collective-permute-done.4
  337.7 3.2 collective-permute-start
  342.7 2.9 collective-permute-start.2
  355.2 3.1 mul.275
  358.6 2.7 collective-permute-start.4
  362.5 2.3 collective-permute-done.4
  366.7 2.3 reshape.98
  374.0 7.9 %all-to-all-start.1 = ((f32[16,2,128]{2,1,0:T(2,128)}), f32[16,2,128]{2,1,0:T(2,128)S(1)}, u32[]{:S(2)}, u32[]{:S(2)}) async-start(f32[16,2,128]{2,1,0:T(2,128)} %copy.39), calls=%async_computation.1 | async-start | bytes 32768 | tf_op jit(solution)/shard_map/all_to_all | solution.py:160
  383.9 3.8 all-to-all-done.1
  (539 shorter events, 188.5 us)
Async XLA Ops:
  3.7 370.3 %all-to-all-start = ((f32[16,1,2]{2,1,0:T(1,128)}), f32[16,1,2]{2,1,0:T(1,128)}, u32[]{:S(2)}, u32[]{:S(2)}) async-start(f32[16,1,2]{2,1,0:T(1,128)} %bitcast.14), calls=%async_computation | async-start | bytes 16384 | tf_op jit(solution)/shard_map/all_to_all | solution.py:161
  15.9 16.4 %collective-permute-start = (f32[2,32,32]{2,1,0:T(8,128)S(1)}, f32[2,32,32]{2,1,0:T(8,128)S(1)}, u32[]{:S(2)}, u32[]{:S(2)}) collective-permute-start(f32[2,32,32]{2,1,0:T(8,128)S(1)} %slice.324), channel_id=1, source_target_pairs={{0,15},{1,0},{2,1},{3,2},{4,3},{5,4},{6,5},{7,6},{8,7},{9,8},{10,9... | collective-permute-start | bytes 24584 | tf_op jit(solution)/shard_map/while/body/eval_jaxpr/ppermute | solution.py:18
  16.3 16.0 %collective-permute-start.1 = (f32[2,1,2048]{2,1,0:T(1,128)S(1)}, f32[2,1,2048]{2,1,0:T(1,128)S(1)}, u32[]{:S(2)}, u32[]{:S(2)}) collective-permute-start(f32[2,1,2048]{2,1,0:T(1,128)S(1)} %slice.327), channel_id=1, source_target_pairs={{0,240},{16,0},{32,16},{48,32},{64,48},{80,64},{96,80},{112,96},{1... | collective-permute-start | bytes 49160 | tf_op jit(solution)/shard_map/while/body/eval_jaxpr/ppermute | solution.py:18
  23.8 8.5 %collective-permute-start.2 = (f32[2,32,32]{2,1,0:T(8,128)S(1)}, f32[2,32,32]{2,1,0:T(8,128)S(1)}, u32[]{:S(2)}, u32[]{:S(2)}) collective-permute-start(f32[2,32,32]{2,1,0:T(8,128)S(1)} %slice.330), channel_id=1, source_target_pairs={{0,15},{1,0},{2,1},{3,2},{4,3},{5,4},{6,5},{7,6},{8,7},{9,8},{10,9... | collective-permute-start | bytes 24584 | tf_op jit(solution)/shard_map/while/body/eval_jaxpr/ppermute | solution.py:18
  33.7 7.2 %collective-permute-start.7 = (f32[2,32,32]{2,1,0:T(8,128)}, f32[2,32,32]{2,1,0:T(8,128)}, u32[]{:S(2)}, u32[]{:S(2)}) collective-permute-start(f32[2,32,32]{2,1,0:T(8,128)} %slice.337), channel_id=1, source_target_pairs={{0,1},{1,2},{2,3},{3,4},{4,5},{5,6},{6,7},{7,8},{8,9},{9,10},{10,1... | collective-permute-start | bytes 24584 | tf_op jit(solution)/shard_map/while/body/eval_jaxpr/ppermute | solution.py:18
  34.3 6.5 %collective-permute-start.6 = (f32[2,1,2048]{2,1,0:T(1,128)}, f32[2,1,2048]{2,1,0:T(1,128)S(1)}, u32[]{:S(2)}, u32[]{:S(2)}) collective-permute-start(f32[2,1,2048]{2,1,0:T(1,128)} %slice.336), channel_id=1, source_target_pairs={{0,16},{16,32},{32,48},{48,64},{64,80},{80,96},{96,112},{112,128},... | collective-permute-start | bytes 49160 | tf_op jit(solution)/shard_map/while/body/eval_jaxpr/ppermute | solution.py:18
  40.8 6.3 %collective-permute-start.4 = (f32[2,1,2048]{2,1,0:T(1,128)S(1)}, f32[2,1,2048]{2,1,0:T(1,128)S(1)}, u32[]{:S(2)}, u32[]{:S(2)}) collective-permute-start(f32[2,1,2048]{2,1,0:T(1,128)S(1)} %slice.334), channel_id=1, source_target_pairs={{0,16},{16,32},{32,48},{48,64},{64,80},{80,96},{96,112},{112,128},... | collective-permute-start | bytes 49160 | tf_op jit(solution)/shard_map/while/body/eval_jaxpr/ppermute | solution.py:18
  49.0 12.2 %collective-permute-start = (f32[2,32,32]{2,1,0:T(8,128)S(1)}, f32[2,32,32]{2,1,0:T(8,128)S(1)}, u32[]{:S(2)}, u32[]{:S(2)}) collective-permute-start(f32[2,32,32]{2,1,0:T(8,128)S(1)} %slice.324), channel_id=1, source_target_pairs={{0,15},{1,0},{2,1},{3,2},{4,3},{5,4},{6,5},{7,6},{8,7},{9,8},{10,9... | collective-permute-start | bytes 24584 | tf_op jit(solution)/shard_map/while/body/eval_jaxpr/ppermute | solution.py:18
  50.9 10.3 %collective-permute-start.1 = (f32[2,1,2048]{2,1,0:T(1,128)S(1)}, f32[2,1,2048]{2,1,0:T(1,128)S(1)}, u32[]{:S(2)}, u32[]{:S(2)}) collective-permute-start(f32[2,1,2048]{2,1,0:T(1,128)S(1)} %slice.327), channel_id=1, source_target_pairs={{0,240},{16,0},{32,16},{48,32},{64,48},{80,64},{96,80},{112,96},{1... | collective-permute-start | bytes 49160 | tf_op jit(solution)/shard_map/while/body/eval_jaxpr/ppermute | solution.py:18
  52.4 8.8 %collective-permute-start.2 = (f32[2,32,32]{2,1,0:T(8,128)S(1)}, f32[2,32,32]{2,1,0:T(8,128)S(1)}, u32[]{:S(2)}, u32[]{:S(2)}) collective-permute-start(f32[2,32,32]{2,1,0:T(8,128)S(1)} %slice.330), channel_id=1, source_target_pairs={{0,15},{1,0},{2,1},{3,2},{4,3},{5,4},{6,5},{7,6},{8,7},{9,8},{10,9... | collective-permute-start | bytes 24584 | tf_op jit(solution)/shard_map/while/body/eval_jaxpr/ppermute | solution.py:18
  62.6 8.4 %collective-permute-start.7 = (f32[2,32,32]{2,1,0:T(8,128)}, f32[2,32,32]{2,1,0:T(8,128)}, u32[]{:S(2)}, u32[]{:S(2)}) collective-permute-start(f32[2,32,32]{2,1,0:T(8,128)} %slice.337), channel_id=1, source_target_pairs={{0,1},{1,2},{2,3},{3,4},{4,5},{5,6},{6,7},{7,8},{8,9},{9,10},{10,1... | collective-permute-start | bytes 24584 | tf_op jit(solution)/shard_map/while/body/eval_jaxpr/ppermute | solution.py:18
  63.3 7.8 %collective-permute-start.6 = (f32[2,1,2048]{2,1,0:T(1,128)}, f32[2,1,2048]{2,1,0:T(1,128)S(1)}, u32[]{:S(2)}, u32[]{:S(2)}) collective-permute-start(f32[2,1,2048]{2,1,0:T(1,128)} %slice.336), channel_id=1, source_target_pairs={{0,16},{16,32},{32,48},{48,64},{64,80},{80,96},{96,112},{112,128},... | collective-permute-start | bytes 49160 | tf_op jit(solution)/shard_map/while/body/eval_jaxpr/ppermute | solution.py:18
  76.4 13.8 %collective-permute-start = (f32[2,32,32]{2,1,0:T(8,128)S(1)}, f32[2,32,32]{2,1,0:T(8,128)S(1)}, u32[]{:S(2)}, u32[]{:S(2)}) collective-permute-start(f32[2,32,32]{2,1,0:T(8,128)S(1)} %slice.324), channel_id=1, source_target_pairs={{0,15},{1,0},{2,1},{3,2},{4,3},{5,4},{6,5},{7,6},{8,7},{9,8},{10,9... | collective-permute-start | bytes 24584 | tf_op jit(solution)/shard_map/while/body/eval_jaxpr/ppermute | solution.py:18
  79.7 10.5 %collective-permute-start.1 = (f32[2,1,2048]{2,1,0:T(1,128)S(1)}, f32[2,1,2048]{2,1,0:T(1,128)S(1)}, u32[]{:S(2)}, u32[]{:S(2)}) collective-permute-start(f32[2,1,2048]{2,1,0:T(1,128)S(1)} %slice.327), channel_id=1, source_target_pairs={{0,240},{16,0},{32,16},{48,32},{64,48},{80,64},{96,80},{112,96},{1... | collective-permute-start | bytes 49160 | tf_op jit(solution)/shard_map/while/body/eval_jaxpr/ppermute | solution.py:18
  81.4 8.8 %collective-permute-start.2 = (f32[2,32,32]{2,1,0:T(8,128)S(1)}, f32[2,32,32]{2,1,0:T(8,128)S(1)}, u32[]{:S(2)}, u32[]{:S(2)}) collective-permute-start(f32[2,32,32]{2,1,0:T(8,128)S(1)} %slice.330), channel_id=1, source_target_pairs={{0,15},{1,0},{2,1},{3,2},{4,3},{5,4},{6,5},{7,6},{8,7},{9,8},{10,9... | collective-permute-start | bytes 24584 | tf_op jit(solution)/shard_map/while/body/eval_jaxpr/ppermute | solution.py:18
  91.7 8.3 %collective-permute-start.7 = (f32[2,32,32]{2,1,0:T(8,128)}, f32[2,32,32]{2,1,0:T(8,128)}, u32[]{:S(2)}, u32[]{:S(2)}) collective-permute-start(f32[2,32,32]{2,1,0:T(8,128)} %slice.337), channel_id=1, source_target_pairs={{0,1},{1,2},{2,3},{3,4},{4,5},{5,6},{6,7},{7,8},{8,9},{9,10},{10,1... | collective-permute-start | bytes 24584 | tf_op jit(solution)/shard_map/while/body/eval_jaxpr/ppermute | solution.py:18
  92.3 7.7 %collective-permute-start.6 = (f32[2,1,2048]{2,1,0:T(1,128)}, f32[2,1,2048]{2,1,0:T(1,128)S(1)}, u32[]{:S(2)}, u32[]{:S(2)}) collective-permute-start(f32[2,1,2048]{2,1,0:T(1,128)} %slice.336), channel_id=1, source_target_pairs={{0,16},{16,32},{32,48},{48,64},{64,80},{80,96},{96,112},{112,128},... | collective-permute-start | bytes 49160 | tf_op jit(solution)/shard_map/while/body/eval_jaxpr/ppermute | solution.py:18
  105.5 13.8 %collective-permute-start = (f32[2,32,32]{2,1,0:T(8,128)S(1)}, f32[2,32,32]{2,1,0:T(8,128)S(1)}, u32[]{:S(2)}, u32[]{:S(2)}) collective-permute-start(f32[2,32,32]{2,1,0:T(8,128)S(1)} %slice.324), channel_id=1, source_target_pairs={{0,15},{1,0},{2,1},{3,2},{4,3},{5,4},{6,5},{7,6},{8,7},{9,8},{10,9... | collective-permute-start | bytes 24584 | tf_op jit(solution)/shard_map/while/body/eval_jaxpr/ppermute | solution.py:18
  108.7 10.5 %collective-permute-start.1 = (f32[2,1,2048]{2,1,0:T(1,128)S(1)}, f32[2,1,2048]{2,1,0:T(1,128)S(1)}, u32[]{:S(2)}, u32[]{:S(2)}) collective-permute-start(f32[2,1,2048]{2,1,0:T(1,128)S(1)} %slice.327), channel_id=1, source_target_pairs={{0,240},{16,0},{32,16},{48,32},{64,48},{80,64},{96,80},{112,96},{1... | collective-permute-start | bytes 49160 | tf_op jit(solution)/shard_map/while/body/eval_jaxpr/ppermute | solution.py:18
  110.5 8.8 %collective-permute-start.2 = (f32[2,32,32]{2,1,0:T(8,128)S(1)}, f32[2,32,32]{2,1,0:T(8,128)S(1)}, u32[]{:S(2)}, u32[]{:S(2)}) collective-permute-start(f32[2,32,32]{2,1,0:T(8,128)S(1)} %slice.330), channel_id=1, source_target_pairs={{0,15},{1,0},{2,1},{3,2},{4,3},{5,4},{6,5},{7,6},{8,7},{9,8},{10,9... | collective-permute-start | bytes 24584 | tf_op jit(solution)/shard_map/while/body/eval_jaxpr/ppermute | solution.py:18
  120.7 8.3 %collective-permute-start.7 = (f32[2,32,32]{2,1,0:T(8,128)}, f32[2,32,32]{2,1,0:T(8,128)}, u32[]{:S(2)}, u32[]{:S(2)}) collective-permute-start(f32[2,32,32]{2,1,0:T(8,128)} %slice.337), channel_id=1, source_target_pairs={{0,1},{1,2},{2,3},{3,4},{4,5},{5,6},{6,7},{7,8},{8,9},{9,10},{10,1... | collective-permute-start | bytes 24584 | tf_op jit(solution)/shard_map/while/body/eval_jaxpr/ppermute | solution.py:18
  121.3 7.7 %collective-permute-start.6 = (f32[2,1,2048]{2,1,0:T(1,128)}, f32[2,1,2048]{2,1,0:T(1,128)S(1)}, u32[]{:S(2)}, u32[]{:S(2)}) collective-permute-start(f32[2,1,2048]{2,1,0:T(1,128)} %slice.336), channel_id=1, source_target_pairs={{0,16},{16,32},{32,48},{48,64},{64,80},{80,96},{96,112},{112,128},... | collective-permute-start | bytes 49160 | tf_op jit(solution)/shard_map/while/body/eval_jaxpr/ppermute | solution.py:18
  126.3 6.3 %collective-permute-start.4 = (f32[2,1,2048]{2,1,0:T(1,128)S(1)}, f32[2,1,2048]{2,1,0:T(1,128)S(1)}, u32[]{:S(2)}, u32[]{:S(2)}) collective-permute-start(f32[2,1,2048]{2,1,0:T(1,128)S(1)} %slice.334), channel_id=1, source_target_pairs={{0,16},{16,32},{32,48},{48,64},{64,80},{80,96},{96,112},{112,128},... | collective-permute-start | bytes 49160 | tf_op jit(solution)/shard_map/while/body/eval_jaxpr/ppermute | solution.py:18
  134.5 13.8 %collective-permute-start = (f32[2,32,32]{2,1,0:T(8,128)S(1)}, f32[2,32,32]{2,1,0:T(8,128)S(1)}, u32[]{:S(2)}, u32[]{:S(2)}) collective-permute-start(f32[2,32,32]{2,1,0:T(8,128)S(1)} %slice.324), channel_id=1, source_target_pairs={{0,15},{1,0},{2,1},{3,2},{4,3},{5,4},{6,5},{7,6},{8,7},{9,8},{10,9... | collective-permute-start | bytes 24584 | tf_op jit(solution)/shard_map/while/body/eval_jaxpr/ppermute | solution.py:18
  137.7 10.5 %collective-permute-start.1 = (f32[2,1,2048]{2,1,0:T(1,128)S(1)}, f32[2,1,2048]{2,1,0:T(1,128)S(1)}, u32[]{:S(2)}, u32[]{:S(2)}) collective-permute-start(f32[2,1,2048]{2,1,0:T(1,128)S(1)} %slice.327), channel_id=1, source_target_pairs={{0,240},{16,0},{32,16},{48,32},{64,48},{80,64},{96,80},{112,96},{1... | collective-permute-start | bytes 49160 | tf_op jit(solution)/shard_map/while/body/eval_jaxpr/ppermute | solution.py:18
  139.5 8.8 %collective-permute-start.2 = (f32[2,32,32]{2,1,0:T(8,128)S(1)}, f32[2,32,32]{2,1,0:T(8,128)S(1)}, u32[]{:S(2)}, u32[]{:S(2)}) collective-permute-start(f32[2,32,32]{2,1,0:T(8,128)S(1)} %slice.330), channel_id=1, source_target_pairs={{0,15},{1,0},{2,1},{3,2},{4,3},{5,4},{6,5},{7,6},{8,7},{9,8},{10,9... | collective-permute-start | bytes 24584 | tf_op jit(solution)/shard_map/while/body/eval_jaxpr/ppermute | solution.py:18
  149.7 8.3 %collective-permute-start.7 = (f32[2,32,32]{2,1,0:T(8,128)}, f32[2,32,32]{2,1,0:T(8,128)}, u32[]{:S(2)}, u32[]{:S(2)}) collective-permute-start(f32[2,32,32]{2,1,0:T(8,128)} %slice.337), channel_id=1, source_target_pairs={{0,1},{1,2},{2,3},{3,4},{4,5},{5,6},{6,7},{7,8},{8,9},{9,10},{10,1... | collective-permute-start | bytes 24584 | tf_op jit(solution)/shard_map/while/body/eval_jaxpr/ppermute | solution.py:18
  150.3 7.7 %collective-permute-start.6 = (f32[2,1,2048]{2,1,0:T(1,128)}, f32[2,1,2048]{2,1,0:T(1,128)S(1)}, u32[]{:S(2)}, u32[]{:S(2)}) collective-permute-start(f32[2,1,2048]{2,1,0:T(1,128)} %slice.336), channel_id=1, source_target_pairs={{0,16},{16,32},{32,48},{48,64},{64,80},{80,96},{96,112},{112,128},... | collective-permute-start | bytes 49160 | tf_op jit(solution)/shard_map/while/body/eval_jaxpr/ppermute | solution.py:18
  163.5 13.8 %collective-permute-start = (f32[2,32,32]{2,1,0:T(8,128)S(1)}, f32[2,32,32]{2,1,0:T(8,128)S(1)}, u32[]{:S(2)}, u32[]{:S(2)}) collective-permute-start(f32[2,32,32]{2,1,0:T(8,128)S(1)} %slice.324), channel_id=1, source_target_pairs={{0,15},{1,0},{2,1},{3,2},{4,3},{5,4},{6,5},{7,6},{8,7},{9,8},{10,9... | collective-permute-start | bytes 24584 | tf_op jit(solution)/shard_map/while/body/eval_jaxpr/ppermute | solution.py:18
  166.8 10.5 %collective-permute-start.1 = (f32[2,1,2048]{2,1,0:T(1,128)S(1)}, f32[2,1,2048]{2,1,0:T(1,128)S(1)}, u32[]{:S(2)}, u32[]{:S(2)}) collective-permute-start(f32[2,1,2048]{2,1,0:T(1,128)S(1)} %slice.327), channel_id=1, source_target_pairs={{0,240},{16,0},{32,16},{48,32},{64,48},{80,64},{96,80},{112,96},{1... | collective-permute-start | bytes 49160 | tf_op jit(solution)/shard_map/while/body/eval_jaxpr/ppermute | solution.py:18
  168.5 8.8 %collective-permute-start.2 = (f32[2,32,32]{2,1,0:T(8,128)S(1)}, f32[2,32,32]{2,1,0:T(8,128)S(1)}, u32[]{:S(2)}, u32[]{:S(2)}) collective-permute-start(f32[2,32,32]{2,1,0:T(8,128)S(1)} %slice.330), channel_id=1, source_target_pairs={{0,15},{1,0},{2,1},{3,2},{4,3},{5,4},{6,5},{7,6},{8,7},{9,8},{10,9... | collective-permute-start | bytes 24584 | tf_op jit(solution)/shard_map/while/body/eval_jaxpr/ppermute | solution.py:18
  178.8 8.3 %collective-permute-start.7 = (f32[2,32,32]{2,1,0:T(8,128)}, f32[2,32,32]{2,1,0:T(8,128)}, u32[]{:S(2)}, u32[]{:S(2)}) collective-permute-start(f32[2,32,32]{2,1,0:T(8,128)} %slice.337), channel_id=1, source_target_pairs={{0,1},{1,2},{2,3},{3,4},{4,5},{5,6},{6,7},{7,8},{8,9},{9,10},{10,1... | collective-permute-start | bytes 24584 | tf_op jit(solution)/shard_map/while/body/eval_jaxpr/ppermute | solution.py:18
  179.4 7.7 %collective-permute-start.6 = (f32[2,1,2048]{2,1,0:T(1,128)}, f32[2,1,2048]{2,1,0:T(1,128)S(1)}, u32[]{:S(2)}, u32[]{:S(2)}) collective-permute-start(f32[2,1,2048]{2,1,0:T(1,128)} %slice.336), channel_id=1, source_target_pairs={{0,16},{16,32},{32,48},{48,64},{64,80},{80,96},{96,112},{112,128},... | collective-permute-start | bytes 49160 | tf_op jit(solution)/shard_map/while/body/eval_jaxpr/ppermute | solution.py:18
  192.6 13.8 %collective-permute-start = (f32[2,32,32]{2,1,0:T(8,128)S(1)}, f32[2,32,32]{2,1,0:T(8,128)S(1)}, u32[]{:S(2)}, u32[]{:S(2)}) collective-permute-start(f32[2,32,32]{2,1,0:T(8,128)S(1)} %slice.324), channel_id=1, source_target_pairs={{0,15},{1,0},{2,1},{3,2},{4,3},{5,4},{6,5},{7,6},{8,7},{9,8},{10,9... | collective-permute-start | bytes 24584 | tf_op jit(solution)/shard_map/while/body/eval_jaxpr/ppermute | solution.py:18
  195.8 10.5 %collective-permute-start.1 = (f32[2,1,2048]{2,1,0:T(1,128)S(1)}, f32[2,1,2048]{2,1,0:T(1,128)S(1)}, u32[]{:S(2)}, u32[]{:S(2)}) collective-permute-start(f32[2,1,2048]{2,1,0:T(1,128)S(1)} %slice.327), channel_id=1, source_target_pairs={{0,240},{16,0},{32,16},{48,32},{64,48},{80,64},{96,80},{112,96},{1... | collective-permute-start | bytes 49160 | tf_op jit(solution)/shard_map/while/body/eval_jaxpr/ppermute | solution.py:18
  197.6 8.8 %collective-permute-start.2 = (f32[2,32,32]{2,1,0:T(8,128)S(1)}, f32[2,32,32]{2,1,0:T(8,128)S(1)}, u32[]{:S(2)}, u32[]{:S(2)}) collective-permute-start(f32[2,32,32]{2,1,0:T(8,128)S(1)} %slice.330), channel_id=1, source_target_pairs={{0,15},{1,0},{2,1},{3,2},{4,3},{5,4},{6,5},{7,6},{8,7},{9,8},{10,9... | collective-permute-start | bytes 24584 | tf_op jit(solution)/shard_map/while/body/eval_jaxpr/ppermute | solution.py:18
  207.8 8.3 %collective-permute-start.7 = (f32[2,32,32]{2,1,0:T(8,128)}, f32[2,32,32]{2,1,0:T(8,128)}, u32[]{:S(2)}, u32[]{:S(2)}) collective-permute-start(f32[2,32,32]{2,1,0:T(8,128)} %slice.337), channel_id=1, source_target_pairs={{0,1},{1,2},{2,3},{3,4},{4,5},{5,6},{6,7},{7,8},{8,9},{9,10},{10,1... | collective-permute-start | bytes 24584 | tf_op jit(solution)/shard_map/while/body/eval_jaxpr/ppermute | solution.py:18
  208.4 7.7 %collective-permute-start.6 = (f32[2,1,2048]{2,1,0:T(1,128)}, f32[2,1,2048]{2,1,0:T(1,128)S(1)}, u32[]{:S(2)}, u32[]{:S(2)}) collective-permute-start(f32[2,1,2048]{2,1,0:T(1,128)} %slice.336), channel_id=1, source_target_pairs={{0,16},{16,32},{32,48},{48,64},{64,80},{80,96},{96,112},{112,128},... | collective-permute-start | bytes 49160 | tf_op jit(solution)/shard_map/while/body/eval_jaxpr/ppermute | solution.py:18
  221.6 13.8 %collective-permute-start = (f32[2,32,32]{2,1,0:T(8,128)S(1)}, f32[2,32,32]{2,1,0:T(8,128)S(1)}, u32[]{:S(2)}, u32[]{:S(2)}) collective-permute-start(f32[2,32,32]{2,1,0:T(8,128)S(1)} %slice.324), channel_id=1, source_target_pairs={{0,15},{1,0},{2,1},{3,2},{4,3},{5,4},{6,5},{7,6},{8,7},{9,8},{10,9... | collective-permute-start | bytes 24584 | tf_op jit(solution)/shard_map/while/body/eval_jaxpr/ppermute | solution.py:18
  224.8 10.5 %collective-permute-start.1 = (f32[2,1,2048]{2,1,0:T(1,128)S(1)}, f32[2,1,2048]{2,1,0:T(1,128)S(1)}, u32[]{:S(2)}, u32[]{:S(2)}) collective-permute-start(f32[2,1,2048]{2,1,0:T(1,128)S(1)} %slice.327), channel_id=1, source_target_pairs={{0,240},{16,0},{32,16},{48,32},{64,48},{80,64},{96,80},{112,96},{1... | collective-permute-start | bytes 49160 | tf_op jit(solution)/shard_map/while/body/eval_jaxpr/ppermute | solution.py:18
  226.6 8.8 %collective-permute-start.2 = (f32[2,32,32]{2,1,0:T(8,128)S(1)}, f32[2,32,32]{2,1,0:T(8,128)S(1)}, u32[]{:S(2)}, u32[]{:S(2)}) collective-permute-start(f32[2,32,32]{2,1,0:T(8,128)S(1)} %slice.330), channel_id=1, source_target_pairs={{0,15},{1,0},{2,1},{3,2},{4,3},{5,4},{6,5},{7,6},{8,7},{9,8},{10,9... | collective-permute-start | bytes 24584 | tf_op jit(solution)/shard_map/while/body/eval_jaxpr/ppermute | solution.py:18
  236.8 8.3 %collective-permute-start.7 = (f32[2,32,32]{2,1,0:T(8,128)}, f32[2,32,32]{2,1,0:T(8,128)}, u32[]{:S(2)}, u32[]{:S(2)}) collective-permute-start(f32[2,32,32]{2,1,0:T(8,128)} %slice.337), channel_id=1, source_target_pairs={{0,1},{1,2},{2,3},{3,4},{4,5},{5,6},{6,7},{7,8},{8,9},{9,10},{10,1... | collective-permute-start | bytes 24584 | tf_op jit(solution)/shard_map/while/body/eval_jaxpr/ppermute | solution.py:18
  237.4 7.7 %collective-permute-start.6 = (f32[2,1,2048]{2,1,0:T(1,128)}, f32[2,1,2048]{2,1,0:T(1,128)S(1)}, u32[]{:S(2)}, u32[]{:S(2)}) collective-permute-start(f32[2,1,2048]{2,1,0:T(1,128)} %slice.336), channel_id=1, source_target_pairs={{0,16},{16,32},{32,48},{48,64},{64,80},{80,96},{96,112},{112,128},... | collective-permute-start | bytes 49160 | tf_op jit(solution)/shard_map/while/body/eval_jaxpr/ppermute | solution.py:18
  250.6 13.8 %collective-permute-start = (f32[2,32,32]{2,1,0:T(8,128)S(1)}, f32[2,32,32]{2,1,0:T(8,128)S(1)}, u32[]{:S(2)}, u32[]{:S(2)}) collective-permute-start(f32[2,32,32]{2,1,0:T(8,128)S(1)} %slice.324), channel_id=1, source_target_pairs={{0,15},{1,0},{2,1},{3,2},{4,3},{5,4},{6,5},{7,6},{8,7},{9,8},{10,9... | collective-permute-start | bytes 24584 | tf_op jit(solution)/shard_map/while/body/eval_jaxpr/ppermute | solution.py:18
  253.9 10.5 %collective-permute-start.1 = (f32[2,1,2048]{2,1,0:T(1,128)S(1)}, f32[2,1,2048]{2,1,0:T(1,128)S(1)}, u32[]{:S(2)}, u32[]{:S(2)}) collective-permute-start(f32[2,1,2048]{2,1,0:T(1,128)S(1)} %slice.327), channel_id=1, source_target_pairs={{0,240},{16,0},{32,16},{48,32},{64,48},{80,64},{96,80},{112,96},{1... | collective-permute-start | bytes 49160 | tf_op jit(solution)/shard_map/while/body/eval_jaxpr/ppermute | solution.py:18
  255.6 8.8 %collective-permute-start.2 = (f32[2,32,32]{2,1,0:T(8,128)S(1)}, f32[2,32,32]{2,1,0:T(8,128)S(1)}, u32[]{:S(2)}, u32[]{:S(2)}) collective-permute-start(f32[2,32,32]{2,1,0:T(8,128)S(1)} %slice.330), channel_id=1, source_target_pairs={{0,15},{1,0},{2,1},{3,2},{4,3},{5,4},{6,5},{7,6},{8,7},{9,8},{10,9... | collective-permute-start | bytes 24584 | tf_op jit(solution)/shard_map/while/body/eval_jaxpr/ppermute | solution.py:18
  265.9 8.3 %collective-permute-start.7 = (f32[2,32,32]{2,1,0:T(8,128)}, f32[2,32,32]{2,1,0:T(8,128)}, u32[]{:S(2)}, u32[]{:S(2)}) collective-permute-start(f32[2,32,32]{2,1,0:T(8,128)} %slice.337), channel_id=1, source_target_pairs={{0,1},{1,2},{2,3},{3,4},{4,5},{5,6},{6,7},{7,8},{8,9},{9,10},{10,1... | collective-permute-start | bytes 24584 | tf_op jit(solution)/shard_map/while/body/eval_jaxpr/ppermute | solution.py:18
  266.5 7.7 %collective-permute-start.6 = (f32[2,1,2048]{2,1,0:T(1,128)}, f32[2,1,2048]{2,1,0:T(1,128)S(1)}, u32[]{:S(2)}, u32[]{:S(2)}) collective-permute-start(f32[2,1,2048]{2,1,0:T(1,128)} %slice.336), channel_id=1, source_target_pairs={{0,16},{16,32},{32,48},{48,64},{64,80},{80,96},{96,112},{112,128},... | collective-permute-start | bytes 49160 | tf_op jit(solution)/shard_map/while/body/eval_jaxpr/ppermute | solution.py:18
  279.6 13.8 %collective-permute-start = (f32[2,32,32]{2,1,0:T(8,128)S(1)}, f32[2,32,32]{2,1,0:T(8,128)S(1)}, u32[]{:S(2)}, u32[]{:S(2)}) collective-permute-start(f32[2,32,32]{2,1,0:T(8,128)S(1)} %slice.324), channel_id=1, source_target_pairs={{0,15},{1,0},{2,1},{3,2},{4,3},{5,4},{6,5},{7,6},{8,7},{9,8},{10,9... | collective-permute-start | bytes 24584 | tf_op jit(solution)/shard_map/while/body/eval_jaxpr/ppermute | solution.py:18
  282.9 10.5 %collective-permute-start.1 = (f32[2,1,2048]{2,1,0:T(1,128)S(1)}, f32[2,1,2048]{2,1,0:T(1,128)S(1)}, u32[]{:S(2)}, u32[]{:S(2)}) collective-permute-start(f32[2,1,2048]{2,1,0:T(1,128)S(1)} %slice.327), channel_id=1, source_target_pairs={{0,240},{16,0},{32,16},{48,32},{64,48},{80,64},{96,80},{112,96},{1... | collective-permute-start | bytes 49160 | tf_op jit(solution)/shard_map/while/body/eval_jaxpr/ppermute | solution.py:18
  284.7 8.8 %collective-permute-start.2 = (f32[2,32,32]{2,1,0:T(8,128)S(1)}, f32[2,32,32]{2,1,0:T(8,128)S(1)}, u32[]{:S(2)}, u32[]{:S(2)}) collective-permute-start(f32[2,32,32]{2,1,0:T(8,128)S(1)} %slice.330), channel_id=1, source_target_pairs={{0,15},{1,0},{2,1},{3,2},{4,3},{5,4},{6,5},{7,6},{8,7},{9,8},{10,9... | collective-permute-start | bytes 24584 | tf_op jit(solution)/shard_map/while/body/eval_jaxpr/ppermute | solution.py:18
  294.9 8.3 %collective-permute-start.7 = (f32[2,32,32]{2,1,0:T(8,128)}, f32[2,32,32]{2,1,0:T(8,128)}, u32[]{:S(2)}, u32[]{:S(2)}) collective-permute-start(f32[2,32,32]{2,1,0:T(8,128)} %slice.337), channel_id=1, source_target_pairs={{0,1},{1,2},{2,3},{3,4},{4,5},{5,6},{6,7},{7,8},{8,9},{9,10},{10,1... | collective-permute-start | bytes 24584 | tf_op jit(solution)/shard_map/while/body/eval_jaxpr/ppermute | solution.py:18
  295.5 7.7 %collective-permute-start.6 = (f32[2,1,2048]{2,1,0:T(1,128)}, f32[2,1,2048]{2,1,0:T(1,128)S(1)}, u32[]{:S(2)}, u32[]{:S(2)}) collective-permute-start(f32[2,1,2048]{2,1,0:T(1,128)} %slice.336), channel_id=1, source_target_pairs={{0,16},{16,32},{32,48},{48,64},{64,80},{80,96},{96,112},{112,128},... | collective-permute-start | bytes 49160 | tf_op jit(solution)/shard_map/while/body/eval_jaxpr/ppermute | solution.py:18
  308.7 13.8 %collective-permute-start = (f32[2,32,32]{2,1,0:T(8,128)S(1)}, f32[2,32,32]{2,1,0:T(8,128)S(1)}, u32[]{:S(2)}, u32[]{:S(2)}) collective-permute-start(f32[2,32,32]{2,1,0:T(8,128)S(1)} %slice.324), channel_id=1, source_target_pairs={{0,15},{1,0},{2,1},{3,2},{4,3},{5,4},{6,5},{7,6},{8,7},{9,8},{10,9... | collective-permute-start | bytes 24584 | tf_op jit(solution)/shard_map/while/body/eval_jaxpr/ppermute | solution.py:18
  311.9 10.5 %collective-permute-start.1 = (f32[2,1,2048]{2,1,0:T(1,128)S(1)}, f32[2,1,2048]{2,1,0:T(1,128)S(1)}, u32[]{:S(2)}, u32[]{:S(2)}) collective-permute-start(f32[2,1,2048]{2,1,0:T(1,128)S(1)} %slice.327), channel_id=1, source_target_pairs={{0,240},{16,0},{32,16},{48,32},{64,48},{80,64},{96,80},{112,96},{1... | collective-permute-start | bytes 49160 | tf_op jit(solution)/shard_map/while/body/eval_jaxpr/ppermute | solution.py:18
  313.7 8.8 %collective-permute-start.2 = (f32[2,32,32]{2,1,0:T(8,128)S(1)}, f32[2,32,32]{2,1,0:T(8,128)S(1)}, u32[]{:S(2)}, u32[]{:S(2)}) collective-permute-start(f32[2,32,32]{2,1,0:T(8,128)S(1)} %slice.330), channel_id=1, source_target_pairs={{0,15},{1,0},{2,1},{3,2},{4,3},{5,4},{6,5},{7,6},{8,7},{9,8},{10,9... | collective-permute-start | bytes 24584 | tf_op jit(solution)/shard_map/while/body/eval_jaxpr/ppermute | solution.py:18
  323.9 8.3 %collective-permute-start.7 = (f32[2,32,32]{2,1,0:T(8,128)}, f32[2,32,32]{2,1,0:T(8,128)}, u32[]{:S(2)}, u32[]{:S(2)}) collective-permute-start(f32[2,32,32]{2,1,0:T(8,128)} %slice.337), channel_id=1, source_target_pairs={{0,1},{1,2},{2,3},{3,4},{4,5},{5,6},{6,7},{7,8},{8,9},{9,10},{10,1... | collective-permute-start | bytes 24584 | tf_op jit(solution)/shard_map/while/body/eval_jaxpr/ppermute | solution.py:18
  324.5 7.7 %collective-permute-start.6 = (f32[2,1,2048]{2,1,0:T(1,128)}, f32[2,1,2048]{2,1,0:T(1,128)S(1)}, u32[]{:S(2)}, u32[]{:S(2)}) collective-permute-start(f32[2,1,2048]{2,1,0:T(1,128)} %slice.336), channel_id=1, source_target_pairs={{0,16},{16,32},{32,48},{48,64},{64,80},{80,96},{96,112},{112,128},... | collective-permute-start | bytes 49160 | tf_op jit(solution)/shard_map/while/body/eval_jaxpr/ppermute | solution.py:18
  337.7 13.8 %collective-permute-start = (f32[2,32,32]{2,1,0:T(8,128)S(1)}, f32[2,32,32]{2,1,0:T(8,128)S(1)}, u32[]{:S(2)}, u32[]{:S(2)}) collective-permute-start(f32[2,32,32]{2,1,0:T(8,128)S(1)} %slice.324), channel_id=1, source_target_pairs={{0,15},{1,0},{2,1},{3,2},{4,3},{5,4},{6,5},{7,6},{8,7},{9,8},{10,9... | collective-permute-start | bytes 24584 | tf_op jit(solution)/shard_map/while/body/eval_jaxpr/ppermute | solution.py:18
  341.0 10.5 %collective-permute-start.1 = (f32[2,1,2048]{2,1,0:T(1,128)S(1)}, f32[2,1,2048]{2,1,0:T(1,128)S(1)}, u32[]{:S(2)}, u32[]{:S(2)}) collective-permute-start(f32[2,1,2048]{2,1,0:T(1,128)S(1)} %slice.327), channel_id=1, source_target_pairs={{0,240},{16,0},{32,16},{48,32},{64,48},{80,64},{96,80},{112,96},{1... | collective-permute-start | bytes 49160 | tf_op jit(solution)/shard_map/while/body/eval_jaxpr/ppermute | solution.py:18
  342.7 8.8 %collective-permute-start.2 = (f32[2,32,32]{2,1,0:T(8,128)S(1)}, f32[2,32,32]{2,1,0:T(8,128)S(1)}, u32[]{:S(2)}, u32[]{:S(2)}) collective-permute-start(f32[2,32,32]{2,1,0:T(8,128)S(1)} %slice.330), channel_id=1, source_target_pairs={{0,15},{1,0},{2,1},{3,2},{4,3},{5,4},{6,5},{7,6},{8,7},{9,8},{10,9... | collective-permute-start | bytes 24584 | tf_op jit(solution)/shard_map/while/body/eval_jaxpr/ppermute | solution.py:18
  352.9 8.3 %collective-permute-start.7 = (f32[2,32,32]{2,1,0:T(8,128)}, f32[2,32,32]{2,1,0:T(8,128)}, u32[]{:S(2)}, u32[]{:S(2)}) collective-permute-start(f32[2,32,32]{2,1,0:T(8,128)} %slice.337), channel_id=1, source_target_pairs={{0,1},{1,2},{2,3},{3,4},{4,5},{5,6},{6,7},{7,8},{8,9},{9,10},{10,1... | collective-permute-start | bytes 24584 | tf_op jit(solution)/shard_map/while/body/eval_jaxpr/ppermute | solution.py:18
  353.6 7.7 %collective-permute-start.6 = (f32[2,1,2048]{2,1,0:T(1,128)}, f32[2,1,2048]{2,1,0:T(1,128)S(1)}, u32[]{:S(2)}, u32[]{:S(2)}) collective-permute-start(f32[2,1,2048]{2,1,0:T(1,128)} %slice.336), channel_id=1, source_target_pairs={{0,16},{16,32},{32,48},{48,64},{64,80},{80,96},{96,112},{112,128},... | collective-permute-start | bytes 49160 | tf_op jit(solution)/shard_map/while/body/eval_jaxpr/ppermute | solution.py:18
  374.0 13.7 %all-to-all-start.1 = ((f32[16,2,128]{2,1,0:T(2,128)}), f32[16,2,128]{2,1,0:T(2,128)S(1)}, u32[]{:S(2)}, u32[]{:S(2)}) async-start(f32[16,2,128]{2,1,0:T(2,128)} %copy.39), calls=%async_computation.1 | async-start | bytes 32768 | tf_op jit(solution)/shard_map/all_to_all | solution.py:160
  (87 other events, 681.3 us)
where the time goes:
time: 390 us; the launch traced here: 389 us
  starting transfers between devices  179 us (46%)
  other arithmetic  85.3 us (22%)
  local copies, waits for them, and re-layouts  84.8 us (22%)
  waiting for transfers between devices  34.9 us (9%)
    ppermute x96, starting transfers between devices, shifted(): lax.ppermute(array, axis, [(i, (i + by) % count) for i in range(count)])  164 us
    mul x12, local copies, waits for them, and re-layouts, per_device(): source_profile[:, :, :, None]  37.5 us
    ppermute x96, waiting for transfers between devices, shifted(): lax.ppermute(array, axis, [(i, (i + by) % count) for i in range(count)])  31.1 us
    mul x12, other arithmetic, per_device(): source_profile[:, :, :, None]  23.2 us
    add x12, other arithmetic, update_electric(): new_z = ez + time_step * inverse * cz  14.3 us
    while x96, local copies, waits for them, and re-layouts  13.2 us
    mul x12, other arithmetic, update_electric(): new_x = ex + time_step * inverse * cx + time_step * wave * source  11.6 us
    sub x12, other arithmetic, advance(): hx = hx - time_step * curl_x  9.06 us
  transfers between devices with their start and end apart: 98, of which 14 were waited for; matrix products, arithmetic and copies ran while one was open for 40% of the time, Pallas kernels for 0%

commit v1 on v0

v1 whole, which is shorter than its diff:
```python
import functools

import jax
import jax.numpy as jnp
import numpy as np
from jax import lax
from jax.experimental import pallas as pl
from jax.experimental.pallas import tpu as pltpu
from jax.sharding import PartitionSpec as P

NZ = 32
STEPS = 12
BROWS = 2
DB_DEV = 4

time_step = 0.5
omega_source = 1.3

ROWS = 32
TILES = 16
HALO = STEPS
XR = ROWS + 2 * HALO
HT = HALO // 4
YV = 24
PAD = 8
NARR = 14
NEAR = 8
FAR = 4
FARW = TILES + HT + 1
LANES = 128
HIGH = lax.Precision.HIGHEST
VLIM = pltpu.CompilerParams(vmem_limit_bytes=60 * 1024 * 1024)


def shifted(array, axis, by):
    count = lax.axis_size(axis)
    return lax.ppermute(array, axis, [(i, (i + by) % count) for i in range(count)])


def planes(e, h, eps, aux):
    out = [e.at[r, c] for r in range(2) for c in range(3)]
    out += [h.at[r, c] for r in range(2) for c in range(3)]
    return out + [eps, aux]


def pack_near(e, h, eps, aux, to_prev, to_next, to_left, to_right):
    edge = HT * LANES
    length = TILES * LANES
    for a, src in enumerate(planes(e, h, eps, aux)):
        to_prev[a] = src[0:NEAR, :]
        to_next[a] = src[ROWS - NEAR : ROWS, :]
        to_left[a] = src[:, 0:edge]
        to_right[a] = src[:, length - edge : length]


def pack_far(e, h, eps, aux, left, right, to_prev, to_next):
    edge = HT * LANES
    length = TILES * LANES
    lo, hi = NEAR, ROWS - NEAR - FAR
    for a, src in enumerate(planes(e, h, eps, aux)):
        p, q = a // 2, pl.ds(FAR * (a % 2), FAR)
        to_prev[p, q, 0:edge] = left[a, lo : lo + FAR, :]
        to_prev[p, q, edge : edge + length] = src[lo : lo + FAR, :]
        to_prev[p, q, edge + length :] = right[a, lo : lo + FAR, 0:LANES]
        to_next[p, q, 0:LANES] = left[a, hi : hi + FAR, edge - LANES : edge]
        to_next[p, q, LANES : LANES + length] = src[hi : hi + FAR, :]
        to_next[p, q, LANES + length :] = right[a, hi : hi + FAR, :]


def pack_corner(behind, ahead, to_left, to_right):
    edge = HT * LANES
    length = TILES * LANES
    for a in range(NARR):
        to_left[a, 0:NEAR, :] = behind[a, :, 0:edge]
        to_left[a, NEAR:, :] = ahead[a, :, 0:edge]
        to_right[a, 0:NEAR, :] = behind[a, :, length - edge : length]
        to_right[a, NEAR:, :] = ahead[a, :, length - edge : length]


def at(a, x, v=0):
    return PAD + (a * XR + x) * YV + v


def place(dst, a, x, v, value):
    dst[pl.ds(at(a, x, v), value.shape[0], stride=YV), :] = value


def stepping(
    waves,
    e,
    h,
    eps,
    aux,
    left,
    right,
    near_b,
    near_a,
    far_b,
    far_a,
    corner_l,
    corner_r,
    select,
    marks,
    e_out,
    h_out,
    packed,
    we,
    wh,
    wc,
    ws,
    wa,
    acc,
):
    def unpack(dst, a, n, own, fix):
        for j in range(TILES):
            cols = pl.ds(j * LANES, LANES)
            for i in range(ROWS // 8):
                place(dst, a, HALO + 8 * i, HT + j, fix(own[pl.ds(8 * i, 8), cols]))
            place(dst, a, FAR, HT + j, fix(near_b[n, :, cols]))
            place(dst, a, HALO + ROWS, HT + j, fix(near_a[n, :, cols]))
        for j in range(HT):
            cols = pl.ds(j * LANES, LANES)
            for i in range(ROWS // 8):
                place(dst, a, HALO + 8 * i, j, fix(left[n, pl.ds(8 * i, 8), cols]))
                place(dst, a, HALO + 8 * i, HT + TILES + j, fix(right[n, pl.ds(8 * i, 8), cols]))
            for src, v in ((corner_l, j), (corner_r, HT + TILES + j)):
                place(dst, a, FAR, v, fix(src[n, 0:NEAR, cols]))
                place(dst, a, HALO + ROWS, v, fix(src[n, NEAR : 2 * NEAR, cols]))
        for j in range(FARW):
            cols = pl.ds(j * LANES, LANES)
            q = pl.ds(FAR * (n % 2), FAR)
            place(dst, a, 0, HT - 1 + j, fix(far_b[n // 2, q, cols]))
            place(dst, a, XR - FAR, j, fix(far_a[n // 2, q, cols]))

    for a in range(6):
        unpack(we, a, a, e.at[a // 3, a % 3], lambda t: t)
        unpack(wh, a, 6 + a, h.at[a // 3, a % 3], lambda t: t * 2.0)
    unpack(wc, 0, 12, eps, lambda t: 0.25 / t)
    unpack(wa, 0, 13, aux, lambda t: t)

    lane = lax.broadcasted_iota(jnp.int32, (YV, LANES), 1)
    level = lane % NZ
    up_keep = level != NZ - 1
    down_keep = level != 0
    first = lane < NZ
    last = lane >= LANES - NZ

    rows_i = lax.broadcasted_iota(jnp.int32, (LANES, LANES), 0)
    cols_i = lax.broadcasted_iota(jnp.int32, (LANES, LANES), 1)

    def spread(k):
        return (rows_i == (cols_i // NZ) * NZ + k).astype(jnp.float32)

    held = wa[pl.ds(PAD, XR * YV), :]
    lev = lax.broadcasted_iota(jnp.int32, (XR * YV, LANES), 1) % NZ
    held = jnp.where(lev < 4, held, 0.0)
    for r in range(2):
        strength = jnp.dot(held, spread(r), precision=HIGH, preferred_element_type=jnp.float32)
        where = jnp.dot(held, spread(2 + r), precision=HIGH, preferred_element_type=jnp.float32)
        ws[pl.ds(PAD + r * XR * YV, XR * YV), :] = jnp.where(
            lev.astype(jnp.float32) == where, strength, 0.0
        )
    acc[...] = jnp.zeros_like(acc)

    def up_z(t):
        return jnp.where(up_keep, pltpu.roll(t, LANES - 1, 1), 0.0)

    def down_z(t):
        return jnp.where(down_keep, pltpu.roll(t, 1, 1), 0.0)

    def up_y(t, after):
        return pltpu.roll(jnp.where(first, after, t), LANES - NZ, 1)

    def down_y(t, before):
        return pltpu.roll(jnp.where(last, before, t), NZ, 1)

    def row(ref, a, x):
        return ref[pl.ds(pl.multiple_of(at(a, x), 8), YV), :]

    def off(ref, a, x, by):
        return ref[pl.ds(at(a, x) + by, YV), :]

    def put(ref, a, x, value):
        ref[pl.ds(pl.multiple_of(at(a, x), 8), YV), :] = value

    def magnetic_row(r, x):
        ex, ey, ez = (row(we, 3 * r + c, x) for c in range(3))
        hx, hy, hz = (row(wh, 3 * r + c, x) for c in range(3))
        ey_x, ez_x = (row(we, 3 * r + c, x + 1) for c in (1, 2))
        ex_y = up_y(ex, off(we, 3 * r, x, 1))
        ez_y = up_y(ez, off(we, 3 * r + 2, x, 1))
        hx = hx - ((ez_y - ez) - (up_z(ey) - ey))
        hy = hy - ((up_z(ex) - ex) - (ez_x - ez))
        hz = hz - ((ey_x - ey) - (ex_y - ex))
        return (hx, hy, hz)

    def electric_row(r, x, c, wave):
        hx, hy, hz = (row(wh, 3 * r + k, x) for k in range(3))
        hy_x, hz_x = (row(wh, 3 * r + k, x - 1) for k in (1, 2))
        hx_y = down_y(hx, off(wh, 3 * r, x, -1))
        hz_y = down_y(hz, off(wh, 3 * r + 2, x, -1))
        ex, ey, ez = (row(we, 3 * r + k, x) for k in range(3))
        ex = ex + c * ((hz - hz_y) - (hy - down_z(hy))) + wave * row(ws, r, x)
        ey = ey + c * ((hx - down_z(hx)) - (hz - hz_x))
        ez = ez + c * ((hy - hy_x) - (hx - hx_y))
        return (ex, ey, ez)

    def magnetic_group(x, count):
        for r in range(2):
            done = [magnetic_row(r, x + i) for i in range(count)]
            for i in range(count):
                for k in range(3):
                    put(wh, 3 * r + k, x + i, done[i][k])

    def electric_group(x, count, wave):
        for i in range(count):
            c = row(wc, 0, x + i)
            f = electric_row(0, x + i, c, wave)
            g = electric_row(1, x + i, c, wave)
            total = row(acc, 0, x + i) + (f[0] * g[0] + f[1] * g[1] + f[2] * g[2])
            put(acc, 0, x + i, total)
            for k in range(3):
                put(we, k, x + i, f[k])
                put(we, 3 + k, x + i, g[k])

    unroll = 2

    def step(n, _):
        wave = waves[n]
        groups = (XR - n) // unroll - n // unroll

        def hgroup(g, _):
            magnetic_group((n // unroll + g) * unroll, unroll)
            return 0

        def egroup(g, _):
            electric_group((n // unroll + g) * unroll, unroll, wave)
            return 0

        lax.fori_loop(0, groups, hgroup, 0)
        lax.fori_loop(0, groups, egroup, 0)
        return 0

    lax.fori_loop(0, STEPS, step, 0)

    for a in range(6):
        for i in range(ROWS // 8):
            for j in range(TILES):
                src = pl.ds(at(a, HALO + 8 * i, HT + j), 8, stride=YV)
                dst = (a // 3, a % 3, pl.ds(8 * i, 8), pl.ds(j * LANES, LANES))
                e_out[dst] = we[src, :]
                h_out[dst] = wh[src, :] * 0.5

    group = (rows_i // NZ == cols_i % 4).astype(jnp.float32)
    mine = acc[pl.ds(at(0, HALO), ROWS * YV), :]
    sums = jnp.dot(mine, group, precision=HIGH, preferred_element_type=jnp.float32)
    per = BROWS * YV
    place_i = lax.broadcasted_iota(jnp.int32, (per, LANES), 0)
    cell_i = lax.broadcasted_iota(jnp.int32, (per, LANES), 1)
    keep = (place_i // YV == cell_i // (LANES // BROWS)) & (
        (cell_i % (LANES // BROWS)) // 4 == place_i % YV - HT
    )
    blocks = jnp.sum(
        jnp.where(keep[None], sums.reshape(ROWS // BROWS, per, LANES), 0.0), axis=1
    ) / (STEPS * NZ)
    packed[...] = (
        jnp.dot(select[...], blocks, precision=HIGH, preferred_element_type=jnp.float32)
        + marks[...]
    )


def collect(received, filter_matrix, out):
    rec = received[...]
    places = rec.shape[0]
    p = lax.broadcasted_iota(jnp.int32, (places, places), 0)
    q = lax.broadcasted_iota(jnp.int32, (places, places), 1)
    pick = (q == (p // 3) * 3 + 2).astype(jnp.float32)
    labels = jnp.dot(pick, rec, precision=HIGH, preferred_element_type=jnp.float32)
    pr = lax.broadcasted_iota(jnp.int32, (places, LANES), 0)
    ln = lax.broadcasted_iota(jnp.int32, (places, LANES), 1)
    label = jnp.sum(jnp.where((ln == pr % 3) & (pr % 3 < 2), labels, 0.0), axis=1, keepdims=True)
    want = lax.broadcasted_iota(jnp.int32, (places, 8), 1) + 1
    choose = (label == want.astype(jnp.float32)).astype(jnp.float32)
    design = lax.dot_general(
        choose, rec, (((0,), (0,)), ((), ())), precision=HIGH, preferred_element_type=jnp.float32
    )
    result = jnp.dot(
        design, filter_matrix[...], precision=HIGH, preferred_element_type=jnp.float32
    )
    out[...] = result[0:DB_DEV]


def call(kernel, out_shape, count, **kwargs):
    def struct(shape):
        return jax.ShapeDtypeStruct(shape, jnp.float32)

    specs = [pl.BlockSpec(memory_space=pltpu.VMEM)] * count
    outs = tuple(struct(s) for s in out_shape)
    return pl.pallas_call(
        kernel,
        in_specs=kwargs.pop("in_specs", specs),
        out_specs=tuple(pl.BlockSpec(memory_space=pltpu.VMEM) for _ in outs),
        out_shape=outs,
        compiler_params=VLIM,
        **kwargs,
    )


def per_device(
    electric,
    magnetic,
    permittivity,
    source_profile,
    source_plane,
    block_owner,
    design_slot,
    filter_matrix,
):
    length = TILES * LANES
    columns = length // NZ
    edge = HT * LANES
    cell = jnp.arange(length, dtype=jnp.int32)
    column = jnp.arange(columns, dtype=jnp.int32)
    run = jnp.arange(2, dtype=jnp.int32)
    spread = (
        (cell[None, None, :] // NZ == column[None, :, None])
        & (cell[None, None, :] % NZ == run[:, None, None])
    ).astype(jnp.float32)
    mark = (cell[None, :] % NZ == run[:, None] + 2).astype(jnp.float32)
    aux = jnp.einsum("krc,kcl->rl", source_profile, spread, precision=HIGH)
    aux = aux + jnp.einsum("kr,kl->rl", source_plane.astype(jnp.float32), mark, precision=HIGH)

    x_near = (NARR, NEAR, length)
    y_own = (NARR, ROWS, edge)
    own = (electric, magnetic, permittivity, aux)
    to_prev, to_next, to_left, to_right = call(pack_near, (x_near, x_near, y_own, y_own), 4)(*own)
    near_b = shifted(to_next, "gx", 1)
    near_a = shifted(to_prev, "gx", -1)
    left = shifted(to_right, "gy", 1)
    right = shifted(to_left, "gy", -1)

    x_far = (NARR // 2, 2 * FAR, FARW * LANES)
    far_prev, far_next = call(pack_far, (x_far, x_far), 6)(*own, left, right)
    far_b = shifted(far_next, "gx", 1)
    far_a = shifted(far_prev, "gx", -1)

    y_corner = (NARR, 2 * NEAR, edge)
    corner_left, corner_right = call(pack_corner, (y_corner, y_corner), 2)(near_b, near_a)
    corner_l = shifted(corner_right, "gy", 1)
    corner_r = shifted(corner_left, "gy", -1)

    count = ROWS // BROWS
    owner = block_owner[0, 0, :, 0]
    slot = design_slot[0, 0, :]
    owners = lax.axis_size("gy")
    index = jnp.arange(count, dtype=jnp.int32)
    earlier = (
        ((owner[:, None] == owner[None, :]) & (index[None, :] < index[:, None]))
        .astype(jnp.int32)
        .sum(1)
    )
    places = jnp.arange(3 * owners, dtype=jnp.int32)
    chosen = (places[:, None] == (owner * 3 + earlier)[None, :]).astype(jnp.float32)
    lane = jnp.arange(LANES, dtype=jnp.int32)
    holder = (places[:, None] == (owner * 3 + 2)[None, :]).astype(jnp.float32)
    tags = (lane[None, :] == earlier[:, None]).astype(jnp.float32) * (slot + 1).astype(
        jnp.float32
    )[:, None]
    marks = jnp.dot(holder, tags, precision=HIGH)

    waves = jnp.asarray(
        time_step
        * np.sin(np.arange(1, STEPS + 1).astype(np.float32) * np.float32(omega_source * time_step)),
        jnp.float32,
    )
    field = (2, 3, ROWS, length)
    many = XR * YV
    vmem = pl.BlockSpec(memory_space=pltpu.VMEM)
    field_e, field_h, packed = call(
        stepping,
        (field, field, (3 * owners, LANES)),
        15,
        in_specs=[pl.BlockSpec(memory_space=pltpu.SMEM)] + [vmem] * 14,
        scratch_shapes=[
            pltpu.VMEM((6 * many + PAD + YV, LANES), jnp.float32),
            pltpu.VMEM((6 * many + PAD + YV, LANES), jnp.float32),
            pltpu.VMEM((many + 2 * PAD, LANES), jnp.float32),
            pltpu.VMEM((2 * many + 2 * PAD, LANES), jnp.float32),
            pltpu.VMEM((many + 2 * PAD, LANES), jnp.float32),
            pltpu.VMEM((many + 2 * PAD, LANES), jnp.float32),
        ],
    )(
        waves,
        *own,
        left,
        right,
        near_b,
        near_a,
        far_b,
        far_a,
        corner_l,
        corner_r,
        chosen,
        marks,
    )
    received = lax.all_to_all(
        packed.reshape(owners, 3, LANES), "gy", split_axis=0, concat_axis=0, tiled=True
    )
    (result,) = call(collect, ((DB_DEV, LANES),), 2)(
        received.reshape(3 * owners, LANES), filter_matrix
    )
    return (field_e, field_h, result[None])


def solution(mesh):
    placed = (
        P(None, None, "gx", "gy"),
        P(None, None, "gx", "gy"),
        P("gx", "gy"),
        P(None, "gx", "gy"),
        P(None, "gx"),
        P("gx", "gy", None, None),
        P("gx", "gy", None),
        P(),
    )
    return jax.shard_map(
        per_device,
        mesh=mesh,
        in_specs=placed,
        out_specs=(P(None, None, "gx", "gy"), P(None, None, "gx", "gy"), P("gx", "gy", None)),
        check_vma=False,
    )
```

time: 390 us -> 197 us (0.51)
  starting transfers between devices: 179 us -> 46.4 us
  Pallas kernels: 0 us -> 90.8 us
  other arithmetic: 85.3 us -> 0.89 us
  local copies, waits for them, and re-layouts: 84.8 us -> 5.58 us
  blocking collectives: 0 us -> 18.2 us
    ppermute x96 -> x8, starting transfers between devices: 164 us -> 46.4 us  [shifted(): lax.ppermute(array, axis, [(i, (i + by) % count) for i in range(count)])]
    pallas_call x0 -> x5, Pallas kernels: none -> 90.8 us  [the longest x1 79 us: per_device(): call(stepping, (field, field, (3 * owners, LANES)), 15, in_specs=[pl.Bloc...]
    mul x12 -> x0, local copies, waits for them, and re-layouts: 37.5 us -> none  [per_device(): source_profile[:, :, :, None]]
    mul x24 -> x0, other arithmetic: 34.8 us -> none  [the longest x12 23.2 us: per_device(): source_profile[:, :, :, None]]
    slice x168 -> x0, local copies, waits for them, and re-layouts: 27.7 us -> none  [the longest x12 8.13 us: advance(): hx[:, :, length - depth:]]
    add x37 -> x2, other arithmetic: 24.2 us -> 0.01 us  [the longest x1 0.01 us: per_device(): holder = (places[:, None] == (owner * 3 + 2)[None, :]).astype(jnp.float32)]
    all_to_all x0 -> x1, blocking collectives: none -> 18.2 us  [per_device(): lax.all_to_all(packed.reshape(owners, 3, LANES), 'gy', split_axis=0, conc...]
    all_to_all x2 -> x0, starting transfers between devices: 15 us -> none  [the longest x1 7.91 us: per_device(): lax.all_to_all(packed, 'gy', split_axis=0, concat_axis=0, tiled=True)]
  transfers between devices with their start and end apart: 98 -> 8, of which waited for: 14 -> 6; matrix products, arithmetic and copies ran while one was open for 40% -> 1% of each run, Pallas kernels for 0% -> 3%
where the time goes in v1:
time: 197 us
  Pallas kernels  90.8 us (46%)
  starting transfers between devices  46.4 us (24%)
  waiting for transfers between devices  31.3 us (16%)
  blocking collectives  18.2 us (9%)
  local copies, waits for them, and re-layouts  5.58 us (3%)
  matrix products  2.99 us (2%)
    pallas_call x1, Pallas kernels, per_device(): call(stepping, (field, field, (3 * owners, LANES)), 15, in_specs=[pl.Bloc...  79 us
    ppermute x8, starting transfers between devices, shifted(): lax.ppermute(array, axis, [(i, (i + by) % count) for i in range(count)])  46.4 us
    ppermute x8, waiting for transfers between devices, shifted(): lax.ppermute(array, axis, [(i, (i + by) % count) for i in range(count)])  31.3 us
    all_to_all x1, blocking collectives, per_device(): lax.all_to_all(packed.reshape(owners, 3, LANES), 'gy', split_axis=0, conc...  18.2 us
    unnamed x22, local copies, waits for them, and re-layouts  4.21 us
  transfers between devices with their start and end apart: 8, of which 6 were waited for; matrix products, arithmetic and copies ran while one was open for 1% of the time, Pallas kernels for 3%

profile of v1, /device:TPU:1, one launch (start us, length us, event | category | flops | bytes accessed | tf_op | source)
XLA Modules:
  0.0 196.9 jit_solution(3337592785863014370)
XLA Ops:
  0.6 0.0 copy-start
  0.7 0.1 iota_compare_fusion
  0.8 0.6 copy-done
  1.4 0.4 convolution_bitcast_fusion
  1.8 1.7 fusion.aux
  3.6 0.0 copy-start.9
  3.6 3.8 %shard_map.112 = (f32[14,8,2048]{2,1,0:T(8,128)}, f32[14,8,2048]{2,1,0:T(8,128)}, f32[14,32,384]{2,1,0:T(8,128)}, f32[14,32,384]{2,1,0:T(8,128)}) custom-call(f32[2,3,32,2048]{3,2,1,0:T(8,128)} %e.5, f32[2,3,32,2048]{3,2,1,0:T(8,128)} %h.5, f32[32,2048]{1,0:T(8,128)} %eps.5, f32[32,2048]{1,0:T(8,128)} %fusion.aux), custom_call_target="tpu_custom_call" | custom-call | tf_op jit(solution)/shard_map/pallas_call | solution.py:336
  7.3 3.6 %collective-permute-start.2 = (f32[14,8,2048]{2,1,0:T(8,128)}, f32[14,8,2048]{2,1,0:T(8,128)S(1)}, u32[]{:S(2)}, u32[]{:S(2)}) collective-permute-start(f32[14,8,2048]{2,1,0:T(8,128)} %get-tuple-element.16), channel_id=1, source_target_pairs={{0,16},{16,32},{32,48},{48,64},{64,80},{80,96},{96,112},{112,128},... | collective-permute-start | bytes 2752520 | tf_op jit(solution)/shard_map/ppermute | solution.py:37
  10.9 5.3 %collective-permute-start.3 = (f32[14,8,2048]{2,1,0:T(8,128)}, f32[14,8,2048]{2,1,0:T(8,128)S(1)}, u32[]{:S(2)}, u32[]{:S(2)}) collective-permute-start(f32[14,8,2048]{2,1,0:T(8,128)} %get-tuple-element.17), channel_id=1, source_target_pairs={{0,240},{16,0},{32,16},{48,32},{64,48},{80,64},{96,80},{112,96},{1... | collective-permute-start | bytes 2752520 | tf_op jit(solution)/shard_map/ppermute | solution.py:37
  16.2 2.1 %collective-permute-start = (f32[14,32,384]{2,1,0:T(8,128)}, f32[14,32,384]{2,1,0:T(8,128)S(1)}, u32[]{:S(2)}, u32[]{:S(2)}) collective-permute-start(f32[14,32,384]{2,1,0:T(8,128)} %get-tuple-element.14), channel_id=1, source_target_pairs={{0,1},{1,2},{2,3},{3,4},{4,5},{5,6},{6,7},{7,8},{8,9},{9,10},{10,1... | collective-permute-start | bytes 2064392 | tf_op jit(solution)/shard_map/ppermute | solution.py:37
  18.3 0.0 collective-permute-start.1
  18.3 0.0 copy-done.9
  18.4 0.2 convert_reduce_fusion
  18.5 8.0 %collective-permute-done.left = f32[14,32,384]{2,1,0:T(8,128)S(1)} collective-permute-done((f32[14,32,384]{2,1,0:T(8,128)}, f32[14,32,384]{2,1,0:T(8,128)S(1)}, u32[]{:S(2)}, u32[]{:S(2)}) %collective-permute-start) | collective-permute-done | bytes 688160 | tf_op jit(solution)/shard_map/ppermute | solution.py:37
  26.5 0.0 copy-start.3
  26.5 2.7 %collective-permute-done.1.right = f32[14,32,384]{2,1,0:T(8,128)S(1)} collective-permute-done((f32[14,32,384]{2,1,0:T(8,128)}, f32[14,32,384]{2,1,0:T(8,128)S(1)}, u32[]{:S(2)}, u32[]{:S(2)}) %collective-permute-start.1) | collective-permute-done | bytes 688160 | tf_op jit(solution)/shard_map/ppermute | solution.py:37
  29.2 0.0 copy-done.3
  29.2 0.0 copy-start.4
  29.2 0.9 copy-done.4
  30.1 3.6 %shard_map.113 = (f32[7,8,2560]{2,1,0:T(8,128)}, f32[7,8,2560]{2,1,0:T(8,128)}) custom-call(f32[2,3,32,2048]{3,2,1,0:T(8,128)} %e.5, f32[2,3,32,2048]{3,2,1,0:T(8,128)} %h.5, f32[32,2048]{1,0:T(8,128)} %eps.5, f32[32,2048]{1,0:T(8,128)} %fusion.aux, f32[14,32,384]{2,1,0:T(8,128)} %copy-done.3, f32[14,32,384]{2,1,0:T(8,128)} %copy-done.4), custom_call_target="tpu_custom_call" | custom-call | tf_op jit(solution)/shard_map/pallas_call | solution.py:343
  33.7 0.0 copy-start.10
  33.7 0.0 collective-permute-start.4
  33.7 5.1 %collective-permute-start.5 = (f32[7,8,2560]{2,1,0:T(8,128)}, f32[7,8,2560]{2,1,0:T(8,128)S(1)}, u32[]{:S(2)}, u32[]{:S(2)}) collective-permute-start(f32[7,8,2560]{2,1,0:T(8,128)} %get-tuple-element.19), channel_id=1, source_target_pairs={{0,240},{16,0},{32,16},{48,32},{64,48},{80,64},{96,80},{112,96},{1... | collective-permute-start | bytes 1720328 | tf_op jit(solution)/shard_map/ppermute | solution.py:37
  38.8 0.6 fusion.5.select
  39.4 16.7 %collective-permute-done.2.behind.near_b = f32[14,8,2048]{2,1,0:T(8,128)S(1)} collective-permute-done((f32[14,8,2048]{2,1,0:T(8,128)}, f32[14,8,2048]{2,1,0:T(8,128)S(1)}, u32[]{:S(2)}, u32[]{:S(2)}) %collective-permute-start.2) | collective-permute-done | bytes 917536 | tf_op jit(solution)/shard_map/ppermute | solution.py:37
  56.1 0.0 copy-start.1
  56.1 3.3 %collective-permute-done.3.ahead.near_a = f32[14,8,2048]{2,1,0:T(8,128)S(1)} collective-permute-done((f32[14,8,2048]{2,1,0:T(8,128)}, f32[14,8,2048]{2,1,0:T(8,128)S(1)}, u32[]{:S(2)}, u32[]{:S(2)}) %collective-permute-start.3) | collective-permute-done | bytes 917536 | tf_op jit(solution)/shard_map/ppermute | solution.py:37
  59.3 0.0 copy-done.1
  59.3 0.0 copy-start.2
  59.3 1.0 copy-done.2
  60.3 2.3 %shard_map.114 = (f32[14,16,384]{2,1,0:T(8,128)}, f32[14,16,384]{2,1,0:T(8,128)}) custom-call(f32[14,8,2048]{2,1,0:T(8,128)} %copy-done.1, f32[14,8,2048]{2,1,0:T(8,128)} %copy-done.2), custom_call_target="tpu_custom_call" | custom-call | tf_op jit(solution)/shard_map/pallas_call | solution.py:348
  62.7 10.7 %collective-permute-start.6 = (f32[14,16,384]{2,1,0:T(8,128)}, f32[14,16,384]{2,1,0:T(8,128)S(1)}, u32[]{:S(2)}, u32[]{:S(2)}) collective-permute-start(f32[14,16,384]{2,1,0:T(8,128)} %get-tuple-element.20), channel_id=1, source_target_pairs={{0,1},{1,2},{2,3},{3,4},{4,5},{5,6},{6,7},{7,8},{8,9},{9,10},{10,1... | collective-permute-start | bytes 1032200 | tf_op jit(solution)/shard_map/ppermute | solution.py:37
  73.3 19.7 %collective-permute-start.7 = (f32[14,16,384]{2,1,0:T(8,128)}, f32[14,16,384]{2,1,0:T(8,128)S(1)}, u32[]{:S(2)}, u32[]{:S(2)}) collective-permute-start(f32[14,16,384]{2,1,0:T(8,128)} %get-tuple-element.21), channel_id=1, source_target_pairs={{0,15},{1,0},{2,1},{3,2},{4,3},{5,4},{6,5},{7,6},{8,7},{9,8},{10,9... | collective-permute-start | bytes 1032200 | tf_op jit(solution)/shard_map/ppermute | solution.py:37
  93.0 0.0 copy-done.10
  93.0 0.8 fusion.6.marks
  93.8 0.5 collective-permute-done.6.corner_l
  94.4 0.0 copy-start.7
  94.4 0.1 collective-permute-done.7.corner_r
  94.5 0.0 copy-start.8
  94.5 0.0 collective-permute-done.4.far_b
  94.5 0.0 copy-start.5
  94.5 0.0 collective-permute-done.5.far_a
  94.5 0.6 copy-done.7
  95.1 0.1 copy-done.8
  95.2 0.2 copy-done.5
  95.5 0.0 copy-start.6
  95.5 0.8 copy-done.6
  96.3 79.0 %shard_map.115 = (f32[2,3,32,2048]{3,2,1,0:T(8,128)}, f32[2,3,32,2048]{3,2,1,0:T(8,128)}, f32[48,128]{1,0:T(8,128)}) custom-call(f32[12]{0:T(128)} %constant.51.clone.waves, f32[2,3,32,2048]{3,2,1,0:T(8,128)} %e.5, f32[2,3,32,2048]{3,2,1,0:T(8,128)} %h.5, f32[32,2048]{1,0:T(8,128)} %eps.5, f32[32,2048]{1,0:T(8,128)} %fusion.aux, f32[14,32,384]{2,1,0:T(8,128)} %copy-done.3, ...), custom_call_target="tpu_custom_call" | custom-call | tf_op jit(solution)/shard_map/pallas_call | solution.py:379
  175.2 0.8 reshape.154
  176.0 18.2 %all_to_all.5 = f32[16,3,128]{2,1,0:T(4,128)S(1)} all-to-all(f32[16,3,128]{2,1,0:T(4,128)S(1)} %reshape.154), channel_id=1, replica_groups=mesh['gx'=16,'gy'=16] {'gy'}, dimensions={0} | all-to-all | bytes 49152 | tf_op jit(solution)/shard_map/all_to_all | solution.py:406
  194.2 0.6 reshape.155.received
  194.8 2.1 %shard_map.116 = f32[4,128]{1,0:T(4,128)} custom-call(f32[48,128]{1,0:T(8,128)} %reshape.155.received, f32[128,128]{1,0:T(8,128)} %filter_matrix.1), custom_call_target="tpu_custom_call" | custom-call | tf_op jit(solution)/shard_map/pallas_call | solution.py:409
  (6 shorter events, 0.0 us)
Async XLA Ops:
  0.6 0.8 copy-start
  3.6 14.8 %copy-start.9 = (s32[1,1,16,1]{2,3,1,0:T(1,128)S(1)}, s32[1,1,16,1]{2,3,1,0:T(1,128)}, u32[]{:S(2)}) copy-start(s32[1,1,16,1]{2,3,1,0:T(1,128)} %param.14) | copy-start | bytes 196
  7.3 48.7 %collective-permute-start.2 = (f32[14,8,2048]{2,1,0:T(8,128)}, f32[14,8,2048]{2,1,0:T(8,128)S(1)}, u32[]{:S(2)}, u32[]{:S(2)}) collective-permute-start(f32[14,8,2048]{2,1,0:T(8,128)} %get-tuple-element.16), channel_id=1, source_target_pairs={{0,16},{16,32},{32,48},{48,64},{64,80},{80,96},{96,112},{112,128},... | collective-permute-start | bytes 2752520 | tf_op jit(solution)/shard_map/ppermute | solution.py:37
  10.9 48.4 %collective-permute-start.3 = (f32[14,8,2048]{2,1,0:T(8,128)}, f32[14,8,2048]{2,1,0:T(8,128)S(1)}, u32[]{:S(2)}, u32[]{:S(2)}) collective-permute-start(f32[14,8,2048]{2,1,0:T(8,128)} %get-tuple-element.17), channel_id=1, source_target_pairs={{0,240},{16,0},{32,16},{48,32},{64,48},{80,64},{96,80},{112,96},{1... | collective-permute-start | bytes 2752520 | tf_op jit(solution)/shard_map/ppermute | solution.py:37
  16.2 10.3 %collective-permute-start = (f32[14,32,384]{2,1,0:T(8,128)}, f32[14,32,384]{2,1,0:T(8,128)S(1)}, u32[]{:S(2)}, u32[]{:S(2)}) collective-permute-start(f32[14,32,384]{2,1,0:T(8,128)} %get-tuple-element.14), channel_id=1, source_target_pairs={{0,1},{1,2},{2,3},{3,4},{4,5},{5,6},{6,7},{7,8},{8,9},{9,10},{10,1... | collective-permute-start | bytes 2064392 | tf_op jit(solution)/shard_map/ppermute | solution.py:37
  18.3 10.9 %collective-permute-start.1 = (f32[14,32,384]{2,1,0:T(8,128)}, f32[14,32,384]{2,1,0:T(8,128)S(1)}, u32[]{:S(2)}, u32[]{:S(2)}) collective-permute-start(f32[14,32,384]{2,1,0:T(8,128)} %get-tuple-element.15), channel_id=1, source_target_pairs={{0,15},{1,0},{2,1},{3,2},{4,3},{5,4},{6,5},{7,6},{8,7},{9,8},{10,9... | collective-permute-start | bytes 2064392 | tf_op jit(solution)/shard_map/ppermute | solution.py:37
  26.5 2.7 %copy-start.3 = (f32[14,32,384]{2,1,0:T(8,128)}, f32[14,32,384]{2,1,0:T(8,128)S(1)}, u32[]{:S(2)}) copy-start(f32[14,32,384]{2,1,0:T(8,128)S(1)} %collective-permute-done.left) | copy-start | bytes 2064388
  29.2 0.9 copy-start.4
  33.7 59.3 %copy-start.10 = (s32[1,1,16]{2,1,0:T(1,128)S(1)}, s32[1,1,16]{2,1,0:T(1,128)}, u32[]{:S(2)}) copy-start(s32[1,1,16]{2,1,0:T(1,128)} %param.15) | copy-start | bytes 196
  33.7 60.8 %collective-permute-start.4 = (f32[7,8,2560]{2,1,0:T(8,128)}, f32[7,8,2560]{2,1,0:T(8,128)S(1)}, u32[]{:S(2)}, u32[]{:S(2)}) collective-permute-start(f32[7,8,2560]{2,1,0:T(8,128)} %get-tuple-element.18), channel_id=1, source_target_pairs={{0,16},{16,32},{32,48},{48,64},{64,80},{80,96},{96,112},{112,128},... | collective-permute-start | bytes 1720328 | tf_op jit(solution)/shard_map/ppermute | solution.py:37
  33.7 60.8 %collective-permute-start.5 = (f32[7,8,2560]{2,1,0:T(8,128)}, f32[7,8,2560]{2,1,0:T(8,128)S(1)}, u32[]{:S(2)}, u32[]{:S(2)}) collective-permute-start(f32[7,8,2560]{2,1,0:T(8,128)} %get-tuple-element.19), channel_id=1, source_target_pairs={{0,240},{16,0},{32,16},{48,32},{64,48},{80,64},{96,80},{112,96},{1... | collective-permute-start | bytes 1720328 | tf_op jit(solution)/shard_map/ppermute | solution.py:37
  56.1 3.3 %copy-start.1 = (f32[14,8,2048]{2,1,0:T(8,128)}, f32[14,8,2048]{2,1,0:T(8,128)S(1)}, u32[]{:S(2)}) copy-start(f32[14,8,2048]{2,1,0:T(8,128)S(1)} %collective-permute-done.2.behind.near_b) | copy-start | bytes 2752516
  59.3 1.0 copy-start.2
  62.7 31.7 %collective-permute-start.6 = (f32[14,16,384]{2,1,0:T(8,128)}, f32[14,16,384]{2,1,0:T(8,128)S(1)}, u32[]{:S(2)}, u32[]{:S(2)}) collective-permute-start(f32[14,16,384]{2,1,0:T(8,128)} %get-tuple-element.20), channel_id=1, source_target_pairs={{0,1},{1,2},{2,3},{3,4},{4,5},{5,6},{6,7},{7,8},{8,9},{9,10},{10,1... | collective-permute-start | bytes 1032200 | tf_op jit(solution)/shard_map/ppermute | solution.py:37
  73.3 21.2 %collective-permute-start.7 = (f32[14,16,384]{2,1,0:T(8,128)}, f32[14,16,384]{2,1,0:T(8,128)S(1)}, u32[]{:S(2)}, u32[]{:S(2)}) collective-permute-start(f32[14,16,384]{2,1,0:T(8,128)} %get-tuple-element.21), channel_id=1, source_target_pairs={{0,15},{1,0},{2,1},{3,2},{4,3},{5,4},{6,5},{7,6},{8,7},{9,8},{10,9... | collective-permute-start | bytes 1032200 | tf_op jit(solution)/shard_map/ppermute | solution.py:37
  94.4 0.7 copy-start.7
  94.5 0.7 copy-start.8
  94.5 0.9 copy-start.5
  95.5 0.8 copy-start.6

commit v2 on v1

v2 whole, which is shorter than its diff:
```python
import functools

import jax
import jax.numpy as jnp
import numpy as np
from jax import lax
from jax.experimental import pallas as pl
from jax.experimental.pallas import tpu as pltpu
from jax.sharding import PartitionSpec as P

NZ = 32
STEPS = 12
BROWS = 2
DB_DEV = 4

time_step = 0.5
omega_source = 1.3

ROWS = 32
TILES = 16
HALO = STEPS
XR = ROWS + 2 * HALO
HT = HALO // 4
YV = 24
PAD = 8
NARR = 14
NEAR = 8
FAR = 4
FARW = TILES + HT + 1
LANES = 128
HIGH = lax.Precision.HIGHEST


def shifted(array, axis, by):
    count = lax.axis_size(axis)
    return lax.ppermute(array, axis, [(i, (i + by) % count) for i in range(count)])


def dot(a, b):
    return jnp.dot(a, b, precision=HIGH, preferred_element_type=jnp.float32)


def iota(shape, axis):
    return lax.broadcasted_iota(jnp.int32, shape, axis)


def planes(e, h, eps, aux=None):
    out = [e.at[r, c] for r in range(2) for c in range(3)]
    out += [h.at[r, c] for r in range(2) for c in range(3)] + [eps]
    return out + ([] if aux is None else [aux])


def source_tags(profile, plane):
    half = LANES // 2
    c, l = iota((half, LANES), 0), iota((half, LANES), 1)
    strength = dot(profile[0], (l == c).astype(jnp.float32))
    strength = strength + dot(profile[1], (l == c + half).astype(jnp.float32))
    pick = (iota((2, LANES), 0) == iota((2, LANES), 1)).astype(jnp.float32)
    where = lax.dot_general(
        plane[...], pick, (((0,), (0,)), ((), ())), precision=HIGH, preferred_element_type=jnp.float32
    )
    return strength, where


def source_rows(strength, where):
    length = TILES * LANES
    half = LANES // 2
    c, l = iota((LANES, length), 0), iota((LANES, length), 1)
    spread = ((l // NZ == c % half) & (l % NZ == c // half)).astype(jnp.float32)
    level = iota((strength.shape[0], length), 1) % NZ
    out = dot(strength, spread)
    out = jnp.where(level == 2, where[:, 0:1], out)
    return jnp.where(level == 3, where[:, 1:2], out)


def pack_side(e, h, eps, profile, plane, to_left, to_right, aux):
    edge = HT * LANES
    length = TILES * LANES
    aux[...] = source_rows(*source_tags(profile, plane))
    for a, src in enumerate(planes(e, h, eps, aux)):
        to_left[a] = src[:, 0:edge]
        to_right[a] = src[:, length - edge : length]


def pack_near(e, h, eps, profile, plane, to_prev, to_next):
    length = TILES * LANES
    for a, src in enumerate(planes(e, h, eps)):
        to_prev[:, a * length : (a + 1) * length] = src[0:NEAR, :]
        to_next[:, a * length : (a + 1) * length] = src[ROWS - NEAR : ROWS, :]
    for k, tag in enumerate(source_tags(profile, plane)):
        cols = pl.ds((NARR - 1) * length + k * LANES, LANES)
        to_prev[:, cols] = tag[0:NEAR, :]
        to_next[:, cols] = tag[ROWS - NEAR : ROWS, :]


def near_source(ref):
    base = (NARR - 1) * TILES * LANES
    return source_rows(ref[:, base : base + LANES], ref[:, base + LANES : base + 2 * LANES])


def pack_far(e, h, eps, aux, left, right, to_prev, to_next):
    edge = HT * LANES
    length = TILES * LANES
    lo, hi = NEAR, ROWS - NEAR - FAR
    for a, src in enumerate(planes(e, h, eps, aux)):
        p, q = a // 2, pl.ds(FAR * (a % 2), FAR)
        to_prev[p, q, 0:edge] = left[a, lo : lo + FAR, :]
        to_prev[p, q, edge : edge + length] = src[lo : lo + FAR, :]
        to_prev[p, q, edge + length :] = right[a, lo : lo + FAR, 0:LANES]
        to_next[p, q, 0:LANES] = left[a, hi : hi + FAR, edge - LANES : edge]
        to_next[p, q, LANES : LANES + length] = src[hi : hi + FAR, :]
        to_next[p, q, LANES + length :] = right[a, hi : hi + FAR, :]


def pack_corner(behind, ahead, to_left, to_right, made):
    edge = HT * LANES
    length = TILES * LANES
    for k, src in enumerate((behind, ahead)):
        made[...] = near_source(src)
        rows = pl.ds(NEAR * k, NEAR)
        for a in range(NARR):
            part = made if a == NARR - 1 else src.at[:, pl.ds(a * length, length)]
            to_left[a, rows, :] = part[:, 0:edge]
            to_right[a, rows, :] = part[:, length - edge : length]


def at(a, x, v=0):
    return PAD + (a * XR + x) * YV + v


def place(dst, a, x, v, value):
    dst[pl.ds(at(a, x, v), value.shape[0], stride=YV), :] = value


def row(ref, a, x):
    return ref[pl.ds(pl.multiple_of(at(a, x), 8), YV), :]


def off(ref, a, x, by):
    return ref[pl.ds(at(a, x) + by, YV), :]


def put(ref, a, x, value):
    ref[pl.ds(pl.multiple_of(at(a, x), 8), YV), :] = value


def fill_sources(wa, ws, x, count):
    size = count * YV
    level = iota((size, LANES), 1) % NZ
    held = wa[pl.ds(at(0, x), size), :]
    held = jnp.where(level < 4, held, 0.0)
    i, j = iota((LANES, LANES), 0), iota((LANES, LANES), 1)
    for r in range(2):
        strength = dot(held, (i == (j // NZ) * NZ + r).astype(jnp.float32))
        where = dot(held, (i == (j // NZ) * NZ + 2 + r).astype(jnp.float32))
        ws[pl.ds(at(r, x), size), :] = jnp.where(level.astype(jnp.float32) == where, strength, 0.0)


def kinds(we, wh, wc, wa):
    def same(t):
        return t

    out = [(we, a, same) for a in range(6)]
    out += [(wh, a, lambda t: t * 2.0) for a in range(6)]
    return out + [(wc, 0, lambda t: 0.25 / t), (wa, 0, same)]


class Stepper:
    def __init__(self, waves, we, wh, wc, ws, acc):
        self.waves, self.we, self.wh, self.wc, self.ws, self.acc = waves, we, wh, wc, ws, acc
        lane = iota((YV, LANES), 1)
        self.up_keep = lane % NZ != NZ - 1
        self.down_keep = lane % NZ != 0
        self.first = lane < NZ
        self.last = lane >= LANES - NZ

    def up_z(self, t):
        return jnp.where(self.up_keep, pltpu.roll(t, LANES - 1, 1), 0.0)

    def down_z(self, t):
        return jnp.where(self.down_keep, pltpu.roll(t, 1, 1), 0.0)

    def up_y(self, t, after):
        return pltpu.roll(jnp.where(self.first, after, t), LANES - NZ, 1)

    def down_y(self, t, before):
        return pltpu.roll(jnp.where(self.last, before, t), NZ, 1)

    def magnetic_row(self, r, x):
        we, wh = self.we, self.wh
        ex, ey, ez = (row(we, 3 * r + c, x) for c in range(3))
        hx, hy, hz = (row(wh, 3 * r + c, x) for c in range(3))
        ey_x, ez_x = (row(we, 3 * r + c, x + 1) for c in (1, 2))
        ex_y = self.up_y(ex, off(we, 3 * r, x, 1))
        ez_y = self.up_y(ez, off(we, 3 * r + 2, x, 1))
        hx = hx - ((ez_y - ez) - (self.up_z(ey) - ey))
        hy = hy - ((self.up_z(ex) - ex) - (ez_x - ez))
        hz = hz - ((ey_x - ey) - (ex_y - ex))
        return (hx, hy, hz)

    def electric_row(self, r, x, c, wave):
        we, wh = self.we, self.wh
        hx, hy, hz = (row(wh, 3 * r + k, x) for k in range(3))
        hy_x, hz_x = (row(wh, 3 * r + k, x - 1) for k in (1, 2))
        hx_y = self.down_y(hx, off(wh, 3 * r, x, -1))
        hz_y = self.down_y(hz, off(wh, 3 * r + 2, x, -1))
        ex, ey, ez = (row(we, 3 * r + k, x) for k in range(3))
        ex = ex + c * ((hz - hz_y) - (hy - self.down_z(hy))) + wave * row(self.ws, r, x)
        ey = ey + c * ((hx - self.down_z(hx)) - (hz - hz_x))
        ez = ez + c * ((hy - hy_x) - (hx - hx_y))
        return (ex, ey, ez)

    def magnetic(self, x):
        for r in range(2):
            for k, value in enumerate(self.magnetic_row(r, x)):
                put(self.wh, 3 * r + k, x, value)

    def electric(self, x, wave):
        c = row(self.wc, 0, x)
        f = self.electric_row(0, x, c, wave)
        g = self.electric_row(1, x, c, wave)
        put(self.acc, 0, x, row(self.acc, 0, x) + (f[0] * g[0] + f[1] * g[1] + f[2] * g[2]))
        for k in range(3):
            put(self.we, k, x, f[k])
            put(self.we, 3 + k, x, g[k])

    def edges(self, low, high, count):
        def step(n, _):
            wave = self.waves[n]
            for i in range(count):
                self.magnetic(low + n + i)
                self.magnetic(high - n + i)
            for i in range(count):
                self.electric(low + 1 + n + i, wave)
                self.electric(high - n + i, wave)
            return 0

        lax.fori_loop(0, STEPS, step, 0)

    def inside(self, low, high):
        def sweep(one, x, count):
            def group(g, _):
                for i in range(8):
                    one(x + g * 8 + i)
                return 0

            lax.fori_loop(0, count // 8, group, 0)
            for size in (4, 2, 1):
                begin = x + count // (2 * size) * (2 * size)

                @pl.when(count % (2 * size) >= size)
                def _(size=size, begin=begin):
                    for i in range(size):
                        one(begin + i)

        def step(n, _):
            wave = self.waves[n]
            sweep(self.magnetic, low + n, high - low - 2 * n)
            sweep(lambda x: self.electric(x, wave), low + 1 + n, high - low - 1 - 2 * n)
            return 0

        lax.fori_loop(0, STEPS, step, 0)


def run_inside(waves, e, h, eps, aux, left, right, we, wh, wc, ws, acc, wa):
    own = planes(e, h, eps, aux)
    for n, (dst, a, fix) in enumerate(kinds(we, wh, wc, wa)):
        for i in range(ROWS // 8):
            rows = pl.ds(8 * i, 8)
            for j in range(TILES):
                place(dst, a, HALO + 8 * i, HT + j, fix(own[n][rows, pl.ds(j * LANES, LANES)]))
            for j in range(HT):
                cols = pl.ds(j * LANES, LANES)
                place(dst, a, HALO + 8 * i, j, fix(left[n, rows, cols]))
                place(dst, a, HALO + 8 * i, HT + TILES + j, fix(right[n, rows, cols]))
    fill_sources(wa, ws, HALO, ROWS)
    acc[...] = jnp.zeros_like(acc)
    Stepper(waves, we, wh, wc, ws, acc).inside(HALO, HALO + ROWS - 1)


def run_near(waves, _e, _h, _c, _s, _t, near_b, near_a, corner_l, corner_r, we, wh, wc, ws, acc, wa, made):
    length = TILES * LANES
    for k, (src, x) in enumerate(((near_b, FAR), (near_a, HALO + ROWS))):
        made[...] = near_source(src)
        rows = pl.ds(NEAR * k, NEAR)
        for n, (dst, a, fix) in enumerate(kinds(we, wh, wc, wa)):
            for j in range(TILES):
                cols = pl.ds(j * LANES, LANES)
                value = made[:, cols] if n == NARR - 1 else src[:, pl.ds(n * length + j * LANES, LANES)]
                place(dst, a, x, HT + j, fix(value))
            for j in range(HT):
                cols = pl.ds(j * LANES, LANES)
                place(dst, a, x, j, fix(corner_l[n, rows, cols]))
                place(dst, a, x, HT + TILES + j, fix(corner_r[n, rows, cols]))
        fill_sources(wa, ws, x, NEAR)
    Stepper(waves, we, wh, wc, ws, acc).edges(FAR, HALO + ROWS - 1, NEAR)


def run_far(
    waves, _e, _h, _c, _s, _t, far_b, far_a, select, marks, e_out, h_out, packed, we, wh, wc, ws, acc, wa
):
    for n, (dst, a, fix) in enumerate(kinds(we, wh, wc, wa)):
        q = pl.ds(FAR * (n % 2), FAR)
        for j in range(FARW):
            cols = pl.ds(j * LANES, LANES)
            place(dst, a, 0, HT - 1 + j, fix(far_b[n // 2, q, cols]))
            place(dst, a, XR - FAR, j, fix(far_a[n // 2, q, cols]))
    fill_sources(wa, ws, 0, FAR)
    fill_sources(wa, ws, XR - FAR, FAR)
    Stepper(waves, we, wh, wc, ws, acc).edges(0, XR - FAR - 1, FAR)

    for a in range(6):
        for i in range(ROWS // 8):
            for j in range(TILES):
                src = pl.ds(at(a, HALO + 8 * i, HT + j), 8, stride=YV)
                dst = (a // 3, a % 3, pl.ds(8 * i, 8), pl.ds(j * LANES, LANES))
                e_out[dst] = we[src, :]
                h_out[dst] = wh[src, :] * 0.5

    i, j = iota((LANES, LANES), 0), iota((LANES, LANES), 1)
    sums = dot(acc[pl.ds(at(0, HALO), ROWS * YV), :], (i // NZ == j % 4).astype(jnp.float32))
    per = BROWS * YV
    p, q = iota((per, LANES), 0), iota((per, LANES), 1)
    half = LANES // BROWS
    keep = (p // YV == q // half) & ((q % half) // 4 == p % YV - HT)
    blocks = jnp.sum(
        jnp.where(keep[None], sums.reshape(ROWS // BROWS, per, LANES), 0.0), axis=1
    ) / (STEPS * NZ)
    packed[...] = dot(select[...], blocks) + marks[...]


def collect(received, filter_matrix, out):
    rec = received[...]
    places = rec.shape[0]
    p = lax.broadcasted_iota(jnp.int32, (places, places), 0)
    q = lax.broadcasted_iota(jnp.int32, (places, places), 1)
    pick = (q == (p // 3) * 3 + 2).astype(jnp.float32)
    labels = jnp.dot(pick, rec, precision=HIGH, preferred_element_type=jnp.float32)
    pr = lax.broadcasted_iota(jnp.int32, (places, LANES), 0)
    ln = lax.broadcasted_iota(jnp.int32, (places, LANES), 1)
    label = jnp.sum(jnp.where((ln == pr % 3) & (pr % 3 < 2), labels, 0.0), axis=1, keepdims=True)
    want = lax.broadcasted_iota(jnp.int32, (places, 8), 1) + 1
    choose = (label == want.astype(jnp.float32)).astype(jnp.float32)
    design = lax.dot_general(
        choose, rec, (((0,), (0,)), ((), ())), precision=HIGH, preferred_element_type=jnp.float32
    )
    result = jnp.dot(
        design, filter_matrix[...], precision=HIGH, preferred_element_type=jnp.float32
    )
    out[...] = result[0:DB_DEV]


def call(kernel, out_shape, count, micros, limit=32, **kwargs):
    vmem = pl.BlockSpec(memory_space=pltpu.VMEM)
    outs = tuple(jax.ShapeDtypeStruct(shape, jnp.float32) for shape in out_shape)
    return pl.pallas_call(
        kernel,
        in_specs=kwargs.pop("in_specs", [vmem] * count),
        out_specs=(vmem,) * len(outs),
        out_shape=outs,
        compiler_params=pltpu.CompilerParams(vmem_limit_bytes=limit * 1024 * 1024),
        name=kernel.__name__,
        cost_estimate=pl.CostEstimate(
            flops=0, transcendentals=0, bytes_accessed=micros * 3_000_000
        ),
        **kwargs,
    )


def per_device(
    electric,
    magnetic,
    permittivity,
    source_profile,
    source_plane,
    block_owner,
    design_slot,
    filter_matrix,
):
    length = TILES * LANES
    edge = HT * LANES
    plane = source_plane.astype(jnp.float32)
    raw = (electric, magnetic, permittivity, source_profile, plane)

    x_near = (NEAR, (NARR - 1) * length + 2 * LANES)
    to_prev, to_next = call(pack_near, (x_near, x_near), 5, 2)(*raw)
    to_prev, to_next, raw = lax.optimization_barrier((to_prev, to_next, raw))
    near_b = shifted(to_next, "gx", 1)
    near_a = shifted(to_prev, "gx", -1)

    y_own = (NARR, ROWS, edge)
    to_left, to_right, aux = call(pack_side, (y_own, y_own, (ROWS, length)), 5, 3)(*raw)
    left = shifted(to_right, "gy", 1)
    right = shifted(to_left, "gy", -1)

    y_corner = (NARR, 2 * NEAR, edge)
    made = pltpu.VMEM((NEAR, length), jnp.float32)
    corner_left, corner_right = call(
        pack_corner, (y_corner, y_corner), 2, 2, scratch_shapes=[made]
    )(near_b, near_a)
    corner_l = shifted(corner_right, "gy", 1)
    corner_r = shifted(corner_left, "gy", -1)

    own = (electric, magnetic, permittivity, aux)
    x_far = (NARR // 2, 2 * FAR, FARW * LANES)
    far_prev, far_next = call(pack_far, (x_far, x_far), 6, 2)(*own, left, right)
    far_prev, far_next, corner_l, corner_r, left, right = lax.optimization_barrier(
        (far_prev, far_next, corner_l, corner_r, left, right)
    )
    far_b = shifted(far_next, "gx", 1)
    far_a = shifted(far_prev, "gx", -1)

    waves = jnp.asarray(
        time_step
        * np.sin(np.arange(1, STEPS + 1).astype(np.float32) * np.float32(omega_source * time_step)),
        jnp.float32,
    )
    field = (2, 3, ROWS, length)
    many = XR * YV
    tail = PAD + YV
    vmem = pl.BlockSpec(memory_space=pltpu.VMEM)
    smem = pl.BlockSpec(memory_space=pltpu.SMEM)
    held = tuple((k * many + tail, LANES) for k in (6, 6, 1, 2, 1))
    tags = pltpu.VMEM((many + tail, LANES), jnp.float32)
    state = call(run_inside, held, 7, 15, in_specs=[smem] + [vmem] * 6, scratch_shapes=[tags])(
        waves, *own, left, right
    )

    count = ROWS // BROWS
    owner = block_owner[0, 0, :, 0]
    slot = design_slot[0, 0, :]
    owners = lax.axis_size("gy")
    index = jnp.arange(count, dtype=jnp.int32)
    earlier = (
        ((owner[:, None] == owner[None, :]) & (index[None, :] < index[:, None]))
        .astype(jnp.int32)
        .sum(1)
    )
    places = jnp.arange(3 * owners, dtype=jnp.int32)
    chosen = (places[:, None] == (owner * 3 + earlier)[None, :]).astype(jnp.float32)
    lane = jnp.arange(LANES, dtype=jnp.int32)
    holder = (places[:, None] == (owner * 3 + 2)[None, :]).astype(jnp.float32)
    named = (lane[None, :] == earlier[:, None]).astype(jnp.float32) * (slot + 1).astype(
        jnp.float32
    )[:, None]
    marks = jnp.dot(holder, named, precision=HIGH)

    state = call(
        run_near,
        held,
        10,
        12,
        in_specs=[smem] + [vmem] * 9,
        scratch_shapes=[tags, made],
        input_output_aliases={1 + k: k for k in range(5)},
    )(waves, *state, near_b, near_a, corner_l, corner_r)
    out = call(
        run_far,
        (field, field, (3 * owners, LANES)) + held,
        10,
        8,
        in_specs=[smem] + [vmem] * 9,
        scratch_shapes=[tags],
        input_output_aliases={1 + k: 3 + k for k in range(5)},
    )(waves, *state, far_b, far_a, chosen, marks)
    field_e, field_h, packed = out[:3]
    received = lax.all_to_all(
        packed.reshape(owners, 3, LANES), "gy", split_axis=0, concat_axis=0, tiled=True
    )
    (result,) = call(collect, ((DB_DEV, LANES),), 2, 1)(
        received.reshape(3 * owners, LANES), filter_matrix
    )
    return (field_e, field_h, result[None])


def solution(mesh):
    placed = (
        P(None, None, "gx", "gy"),
        P(None, None, "gx", "gy"),
        P("gx", "gy"),
        P(None, "gx", "gy"),
        P(None, "gx"),
        P("gx", "gy", None, None),
        P("gx", "gy", None),
        P(),
    )
    return jax.shard_map(
        per_device,
        mesh=mesh,
        in_specs=placed,
        out_specs=(P(None, None, "gx", "gy"), P(None, None, "gx", "gy"), P("gx", "gy", None)),
        check_vma=False,
    )
```

time: 197 us -> 128 us (0.65)
  Pallas kernels: 90.8 us -> 50.8 us
  starting transfers between devices: 46.4 us -> 19.7 us
  waiting for transfers between devices: 31.3 us -> 37.7 us
  blocking collectives: 18.2 us -> 13 us
  matrix products: 2.99 us -> 0.2 us
    pallas_call x5 -> x8, Pallas kernels: 90.8 us -> 50.8 us  [the longest x1 21.5 us: per_device(): call(run_inside, held, 7, 15, in_specs=[smem] + [vmem] * 6, scratch_shape...]
    ppermute x8, starting transfers between devices: 46.4 us -> 19.7 us  [shifted(): lax.ppermute(array, axis, [(i, (i + by) % count) for i in range(count)])]
    ppermute x8, waiting for transfers between devices: 31.3 us -> 37.7 us  [shifted(): lax.ppermute(array, axis, [(i, (i + by) % count) for i in range(count)])]
    all_to_all x1, blocking collectives: 18.2 us -> 13 us  [per_device(): lax.all_to_all(packed.reshape(owners, 3, LANES), 'gy', split_axis=0, conc...]
    dot_general x3 -> x1, matrix products: 2.99 us -> 0.2 us  [per_device(): marks = jnp.dot(holder, named, precision=HIGH)]
    unnamed x22 -> x20, local copies, waits for them, and re-layouts: 4.21 us -> 4.56 us
  transfers between devices with their start and end apart: 8 -> 8, of which waited for: 6 -> 4; matrix products, arithmetic and copies ran while one was open for 1% -> 0% of each run, Pallas kernels for 3% -> 30%
where the time goes in v2:
time: 128 us
  Pallas kernels  50.8 us (40%)
  waiting for transfers between devices  37.7 us (29%)
  starting transfers between devices  19.7 us (15%)
  blocking collectives  13 us (10%)
  local copies, waits for them, and re-layouts  4.59 us (4%)
    ppermute x8, waiting for transfers between devices, shifted(): lax.ppermute(array, axis, [(i, (i + by) % count) for i in range(count)])  37.7 us
    pallas_call x1, Pallas kernels, per_device(): call(run_inside, held, 7, 15, in_specs=[smem] + [vmem] * 6, scratch_shape...  21.5 us
    ppermute x8, starting transfers between devices, shifted(): lax.ppermute(array, axis, [(i, (i + by) % count) for i in range(count)])  19.7 us
    pallas_call x1, Pallas kernels, per_device(): call(run_near, held, 10, 12, in_specs=[smem] + [vmem] * 9, scratch_shapes...  15.3 us
    all_to_all x1, blocking collectives, per_device(): lax.all_to_all(packed.reshape(owners, 3, LANES), 'gy', split_axis=0, conc...  13 us
    pallas_call x1, Pallas kernels, per_device(): call(run_far, (field, field, (3 * owners, LANES)) + held, 10, 8, in_specs...  11 us
    unnamed x20, local copies, waits for them, and re-layouts  4.56 us
  transfers between devices with their start and end apart: 8, of which 4 were waited for; matrix products, arithmetic and copies ran while one was open for 0% of the time, Pallas kernels for 30%

profile of v2, /device:TPU:1, one launch (start us, length us, event | category | flops | bytes accessed | tf_op | source)
XLA Modules:
  0.0 127.8 jit_solution(5826065178229557623)
XLA Ops:
  0.6 0.7 convert_element_type.21.plane
  1.3 0.0 copy-start
  1.3 1.4 %copy-done = f32[2,3,32,2048]{3,2,1,0:T(8,128)S(1)} copy-done((f32[2,3,32,2048]{3,2,1,0:T(8,128)S(1)}, f32[2,3,32,2048]{3,2,1,0:T(8,128)}, u32[]{:S(2)}) %copy-start) | copy-done | bytes 1572888
  2.7 0.0 copy-start.2
  2.7 1.4 %copy-done.2 = f32[2,3,32,2048]{3,2,1,0:T(8,128)S(1)} copy-done((f32[2,3,32,2048]{3,2,1,0:T(8,128)S(1)}, f32[2,3,32,2048]{3,2,1,0:T(8,128)}, u32[]{:S(2)}) %copy-start.2) | copy-done | bytes 1572888
  4.1 0.0 copy-start.4
  4.1 0.9 copy-done.4
  5.1 0.0 copy-start.5
  5.1 0.8 copy-done.5
  5.8 0.2 pack_near.1
  6.0 3.6 %collective-permute-start.2 = (f32[8,26880]{1,0:T(8,128)S(1)}, f32[8,26880]{1,0:T(8,128)S(1)}, u32[]{:S(2)}, u32[]{:S(2)}) collective-permute-start(f32[8,26880]{1,0:T(8,128)S(1)} %get-tuple-element.50), channel_id=1, source_target_pairs={{0,16},{16,32},{32,48},{48,64},{64,80},{80,96},{96,112},{112,128},... | collective-permute-start | bytes 2580488 | tf_op jit(solution)/shard_map/ppermute | solution.py:36
  9.7 5.4 %collective-permute-start.3 = (f32[8,26880]{1,0:T(8,128)S(1)}, f32[8,26880]{1,0:T(8,128)S(1)}, u32[]{:S(2)}, u32[]{:S(2)}) collective-permute-start(f32[8,26880]{1,0:T(8,128)S(1)} %get-tuple-element.51), channel_id=1, source_target_pairs={{0,240},{16,0},{32,16},{48,32},{64,48},{80,64},{96,80},{112,96},{1... | collective-permute-start | bytes 2580488 | tf_op jit(solution)/shard_map/ppermute | solution.py:36
  15.0 0.0 copy-start.3
  15.1 0.7 pack_side.1
  15.8 0.0 copy-start.8
  15.8 0.0 copy-start.1
  15.8 2.2 %collective-permute-start = (f32[14,32,384]{2,1,0:T(8,128)S(1)}, f32[14,32,384]{2,1,0:T(8,128)S(1)}, u32[]{:S(2)}, u32[]{:S(2)}) collective-permute-start(f32[14,32,384]{2,1,0:T(8,128)S(1)} %get-tuple-element.46), channel_id=1, source_target_pairs={{0,1},{1,2},{2,3},{3,4},{4,5},{5,6},{6,7},{7,8},{8,9},{9,10},{10,1... | collective-permute-start | bytes 2064392 | tf_op jit(solution)/shard_map/ppermute | solution.py:36
  18.0 0.0 collective-permute-start.1
  18.0 27.9 %collective-permute-done.2.behind.near_b = f32[8,26880]{1,0:T(8,128)S(1)} collective-permute-done((f32[8,26880]{1,0:T(8,128)S(1)}, f32[8,26880]{1,0:T(8,128)S(1)}, u32[]{:S(2)}, u32[]{:S(2)}) %collective-permute-start.2) | collective-permute-done | bytes 860192 | tf_op jit(solution)/shard_map/ppermute | solution.py:36
  45.9 3.4 %collective-permute-done.3.ahead.near_a = f32[8,26880]{1,0:T(8,128)S(1)} collective-permute-done((f32[8,26880]{1,0:T(8,128)S(1)}, f32[8,26880]{1,0:T(8,128)S(1)}, u32[]{:S(2)}, u32[]{:S(2)}) %collective-permute-start.3) | collective-permute-done | bytes 860192 | tf_op jit(solution)/shard_map/ppermute | solution.py:36
  49.3 0.7 pack_corner.1
  50.0 3.2 %collective-permute-start.4 = (f32[14,16,384]{2,1,0:T(8,128)S(1)}, f32[14,16,384]{2,1,0:T(8,128)S(1)}, u32[]{:S(2)}, u32[]{:S(2)}) collective-permute-start(f32[14,16,384]{2,1,0:T(8,128)S(1)} %get-tuple-element.52), channel_id=1, source_target_pairs={{0,1},{1,2},{2,3},{3,4},{4,5},{5,6},{6,7},{7,8},{8,9},{9,10},{10,1... | collective-permute-start | bytes 1032200 | tf_op jit(solution)/shard_map/ppermute | solution.py:36
  53.2 0.0 collective-permute-start.5
  53.2 0.0 copy-done.8
  53.2 0.2 convert_reduce_fusion
  53.4 0.0 collective-permute-done.left
  53.4 0.0 collective-permute-done.1.right
  53.4 0.0 copy-done.3
  53.4 0.0 copy-done.1
  53.4 0.0 copy-start.9
  53.4 0.0 copy-start.7
  53.4 0.2 pack_far.1
  53.6 3.7 %collective-permute-done.4.corner_l = f32[14,16,384]{2,1,0:T(8,128)S(1)} collective-permute-done((f32[14,16,384]{2,1,0:T(8,128)S(1)}, f32[14,16,384]{2,1,0:T(8,128)S(1)}, u32[]{:S(2)}, u32[]{:S(2)}) %collective-permute-start.4) | collective-permute-done | bytes 344096 | tf_op jit(solution)/shard_map/ppermute | solution.py:36
  57.4 2.8 %collective-permute-done.5.corner_r = f32[14,16,384]{2,1,0:T(8,128)S(1)} collective-permute-done((f32[14,16,384]{2,1,0:T(8,128)S(1)}, f32[14,16,384]{2,1,0:T(8,128)S(1)}, u32[]{:S(2)}, u32[]{:S(2)}) %collective-permute-start.5) | collective-permute-done | bytes 344096 | tf_op jit(solution)/shard_map/ppermute | solution.py:36
  60.1 0.0 collective-permute-start.6
  60.1 5.3 %collective-permute-start.7 = (f32[7,8,2560]{2,1,0:T(8,128)S(1)}, f32[7,8,2560]{2,1,0:T(8,128)S(1)}, u32[]{:S(2)}, u32[]{:S(2)}) collective-permute-start(f32[7,8,2560]{2,1,0:T(8,128)S(1)} %get-tuple-element.69), channel_id=1, source_target_pairs={{0,240},{16,0},{32,16},{48,32},{64,48},{80,64},{96,80},{112,96},{1... | collective-permute-start | bytes 1720328 | tf_op jit(solution)/shard_map/ppermute | solution.py:36
  65.4 0.0 copy-done.9
  65.4 0.2 fusion.1.marks
  65.7 0.0 copy-done.7
  65.7 21.5 %run_inside.1 = (f32[8096,128]{1,0:T(8,128)S(1)}, f32[8096,128]{1,0:T(8,128)S(1)}, f32[1376,128]{1,0:T(8,128)S(1)}, f32[2720,128]{1,0:T(8,128)S(1)}, f32[1376,128]{1,0:T(8,128)S(1)}) custom-call(f32[12]{0:T(128)S(1)} %copy-done.7, f32[2,3,32,2048]{3,2,1,0:T(8,128)S(1)} %copy-done.1, f32[2,3,32,2048]{3,2,1,0:T(8,128)S(1)} %copy-done.3, ...), custom_call_target="tpu_custom_call" | custom-call | bytes 45000000 | tf_op jit(solution)/shard_map/run_inside/pallas_call | solution.py:425
  87.1 15.3 %run_near.1 = (f32[8096,128]{1,0:T(8,128)S(1)}, f32[8096,128]{1,0:T(8,128)S(1)}, f32[1376,128]{1,0:T(8,128)S(1)}, f32[2720,128]{1,0:T(8,128)S(1)}, f32[1376,128]{1,0:T(8,128)S(1)}) custom-call(f32[12]{0:T(128)S(1)} %copy-done.7, ...), custom_call_target="tpu_custom_call", output_to_operand_aliasing={{0}: (1, {}), {1}: (2, {}), {2}: (3, {}), {3}: (4, {}), {4}... | custom-call | bytes 36000000 | tf_op jit(solution)/shard_map/run_near/pallas_call | solution.py:448
  102.4 0.0 collective-permute-done.6.far_b
  102.4 0.0 collective-permute-done.7.far_a
  102.4 0.0 copy-start.6
  102.4 11.0 %run_far.1 = (f32[2,3,32,2048]{3,2,1,0:T(8,128)}, f32[2,3,32,2048]{3,2,1,0:T(8,128)}, f32[48,128]{1,0:T(8,128)S(1)}, f32[8096,128]{1,0:T(8,128)S(1)}, f32[8096,1...) custom-call(f32[12]{0:T(128)S(1)} %copy-done.7, ...), custom_call_target="tpu_custom_call", output_to_operand_aliasing={{3}: (1, {}), {4}: (2, {}), {5}: (3, {}), {6}: (4, {}), {7}... | custom-call | bytes 24000000 | tf_op jit(solution)/shard_map/run_far/pallas_call | solution.py:457
  113.5 13.0 %all_to_all.5 = f32[16,3,128]{2,1,0:T(4,128)S(1)} all-to-all(f32[16,3,128]{2,1,0:T(4,128)S(1)} %reshape.36), channel_id=1, replica_groups=mesh['gx'=16,'gy'=16] {'gy'}, dimensions={0} | all-to-all | bytes 49152 | tf_op jit(solution)/shard_map/all_to_all | solution.py:467
  126.6 0.0 copy-done.6
  126.6 1.2 collect.1
  (5 shorter events, 0.0 us)
Async XLA Ops:
  1.3 1.4 %copy-start = (f32[2,3,32,2048]{3,2,1,0:T(8,128)S(1)}, f32[2,3,32,2048]{3,2,1,0:T(8,128)}, u32[]{:S(2)}) copy-start(f32[2,3,32,2048]{3,2,1,0:T(8,128)} %e.6) | copy-start | bytes 4718596
  2.7 1.4 %copy-start.2 = (f32[2,3,32,2048]{3,2,1,0:T(8,128)S(1)}, f32[2,3,32,2048]{3,2,1,0:T(8,128)}, u32[]{:S(2)}) copy-start(f32[2,3,32,2048]{3,2,1,0:T(8,128)} %h.6) | copy-start | bytes 4718596
  4.1 0.9 copy-start.4
  5.1 0.8 copy-start.5
  6.0 39.9 %collective-permute-start.2 = (f32[8,26880]{1,0:T(8,128)S(1)}, f32[8,26880]{1,0:T(8,128)S(1)}, u32[]{:S(2)}, u32[]{:S(2)}) collective-permute-start(f32[8,26880]{1,0:T(8,128)S(1)} %get-tuple-element.50), channel_id=1, source_target_pairs={{0,16},{16,32},{32,48},{48,64},{64,80},{80,96},{96,112},{112,128},... | collective-permute-start | bytes 2580488 | tf_op jit(solution)/shard_map/ppermute | solution.py:36
  9.7 39.6 %collective-permute-start.3 = (f32[8,26880]{1,0:T(8,128)S(1)}, f32[8,26880]{1,0:T(8,128)S(1)}, u32[]{:S(2)}, u32[]{:S(2)}) collective-permute-start(f32[8,26880]{1,0:T(8,128)S(1)} %get-tuple-element.51), channel_id=1, source_target_pairs={{0,240},{16,0},{32,16},{48,32},{64,48},{80,64},{96,80},{112,96},{1... | collective-permute-start | bytes 2580488 | tf_op jit(solution)/shard_map/ppermute | solution.py:36
  15.0 38.3 %copy-start.3 = (f32[2,3,32,2048]{3,2,1,0:T(8,128)S(1)}, f32[2,3,32,2048]{3,2,1,0:T(8,128)}, u32[]{:S(2)}) copy-start(f32[2,3,32,2048]{3,2,1,0:T(8,128)} %h.6) | copy-start | bytes 4718596
  15.8 37.4 %copy-start.8 = (s32[1,1,16,1]{2,3,1,0:T(1,128)S(1)}, s32[1,1,16,1]{2,3,1,0:T(1,128)}, u32[]{:S(2)}) copy-start(s32[1,1,16,1]{2,3,1,0:T(1,128)} %param.14) | copy-start | bytes 196
  15.8 37.6 %copy-start.1 = (f32[2,3,32,2048]{3,2,1,0:T(8,128)S(1)}, f32[2,3,32,2048]{3,2,1,0:T(8,128)}, u32[]{:S(2)}) copy-start(f32[2,3,32,2048]{3,2,1,0:T(8,128)} %e.6) | copy-start | bytes 4718596
  15.8 37.5 %collective-permute-start = (f32[14,32,384]{2,1,0:T(8,128)S(1)}, f32[14,32,384]{2,1,0:T(8,128)S(1)}, u32[]{:S(2)}, u32[]{:S(2)}) collective-permute-start(f32[14,32,384]{2,1,0:T(8,128)S(1)} %get-tuple-element.46), channel_id=1, source_target_pairs={{0,1},{1,2},{2,3},{3,4},{4,5},{5,6},{6,7},{7,8},{8,9},{9,10},{10,1... | collective-permute-start | bytes 2064392 | tf_op jit(solution)/shard_map/ppermute | solution.py:36
  18.0 35.3 %collective-permute-start.1 = (f32[14,32,384]{2,1,0:T(8,128)S(1)}, f32[14,32,384]{2,1,0:T(8,128)S(1)}, u32[]{:S(2)}, u32[]{:S(2)}) collective-permute-start(f32[14,32,384]{2,1,0:T(8,128)S(1)} %get-tuple-element.47), channel_id=1, source_target_pairs={{0,15},{1,0},{2,1},{3,2},{4,3},{5,4},{6,5},{7,6},{8,7},{9,8},{10,9... | collective-permute-start | bytes 2064392 | tf_op jit(solution)/shard_map/ppermute | solution.py:36
  50.0 7.4 %collective-permute-start.4 = (f32[14,16,384]{2,1,0:T(8,128)S(1)}, f32[14,16,384]{2,1,0:T(8,128)S(1)}, u32[]{:S(2)}, u32[]{:S(2)}) collective-permute-start(f32[14,16,384]{2,1,0:T(8,128)S(1)} %get-tuple-element.52), channel_id=1, source_target_pairs={{0,1},{1,2},{2,3},{3,4},{4,5},{5,6},{6,7},{7,8},{8,9},{9,10},{10,1... | collective-permute-start | bytes 1032200 | tf_op jit(solution)/shard_map/ppermute | solution.py:36
  53.2 7.0 %collective-permute-start.5 = (f32[14,16,384]{2,1,0:T(8,128)S(1)}, f32[14,16,384]{2,1,0:T(8,128)S(1)}, u32[]{:S(2)}, u32[]{:S(2)}) collective-permute-start(f32[14,16,384]{2,1,0:T(8,128)S(1)} %get-tuple-element.53), channel_id=1, source_target_pairs={{0,15},{1,0},{2,1},{3,2},{4,3},{5,4},{6,5},{7,6},{8,7},{9,8},{10,9... | collective-permute-start | bytes 1032200 | tf_op jit(solution)/shard_map/ppermute | solution.py:36
  53.4 12.0 %copy-start.9 = (s32[1,1,16]{2,1,0:T(1,128)S(1)}, s32[1,1,16]{2,1,0:T(1,128)}, u32[]{:S(2)}) copy-start(s32[1,1,16]{2,1,0:T(1,128)} %param.15) | copy-start | bytes 196
  53.4 12.3 %copy-start.7 = (f32[12]{0:T(128)S(1)}, f32[12]{0:T(128)}, u32[]{:S(2)}) copy-start(f32[12]{0:T(128)} %constant.12.clone.waves) | copy-start | bytes 148
  60.1 42.3 %collective-permute-start.6 = (f32[7,8,2560]{2,1,0:T(8,128)S(1)}, f32[7,8,2560]{2,1,0:T(8,128)S(1)}, u32[]{:S(2)}, u32[]{:S(2)}) collective-permute-start(f32[7,8,2560]{2,1,0:T(8,128)S(1)} %get-tuple-element.68), channel_id=1, source_target_pairs={{0,16},{16,32},{32,48},{48,64},{64,80},{80,96},{96,112},{112,128},... | collective-permute-start | bytes 1720328 | tf_op jit(solution)/shard_map/ppermute | solution.py:36
  60.1 42.3 %collective-permute-start.7 = (f32[7,8,2560]{2,1,0:T(8,128)S(1)}, f32[7,8,2560]{2,1,0:T(8,128)S(1)}, u32[]{:S(2)}, u32[]{:S(2)}) collective-permute-start(f32[7,8,2560]{2,1,0:T(8,128)S(1)} %get-tuple-element.69), channel_id=1, source_target_pairs={{0,240},{16,0},{32,16},{48,32},{64,48},{80,64},{96,80},{112,96},{1... | collective-permute-start | bytes 1720328 | tf_op jit(solution)/shard_map/ppermute | solution.py:36
  102.4 24.1 %copy-start.6 = (f32[128,128]{1,0:T(8,128)S(1)}, f32[128,128]{1,0:T(8,128)}, u32[]{:S(2)}) copy-start(f32[128,128]{1,0:T(8,128)} %filter_matrix.1) | copy-start | bytes 196612

commit v3 on v2

--- a/solution.py
+++ b/solution.py
@@ -57,7 +57,7 @@
     strength = strength + dot(profile[1], (l == c + half).astype(jnp.float32))
     pick = (iota((2, LANES), 0) == iota((2, LANES), 1)).astype(jnp.float32)
     where = lax.dot_general(
-        plane[...], pick, (((0,), (0,)), ((), ())), precision=HIGH, preferred_element_type=jnp.float32
+        plane[...].astype(jnp.float32), pick, (((0,), (0,)), ((), ())), precision=HIGH, preferred_element_type=jnp.float32
     )
     return strength, where
 
@@ -73,24 +73,49 @@
     return jnp.where(level == 3, where[:, 1:2], out)
 
 
-def pack_side(e, h, eps, profile, plane, to_left, to_right, aux):
+def moves(e, h, eps, view, put_at, sems, base):
+    srcs = planes(e, h, eps)
+    return [
+        pltpu.make_async_copy(src.at[view], put_at(a), sems.at[base + a])
+        for a, src in enumerate(srcs)
+    ]
+
+
+def pack_side(e, h, eps, profile, plane, to_left, to_right, aux, sems):
     edge = HT * LANES
     length = TILES * LANES
-    aux[...] = source_rows(*source_tags(profile, plane))
-    for a, src in enumerate(planes(e, h, eps, aux)):
-        to_left[a] = src[:, 0:edge]
-        to_right[a] = src[:, length - edge : length]
-
-
-def pack_near(e, h, eps, profile, plane, to_prev, to_next):
-    length = TILES * LANES
-    for a, src in enumerate(planes(e, h, eps)):
-        to_prev[:, a * length : (a + 1) * length] = src[0:NEAR, :]
-        to_next[:, a * length : (a + 1) * length] = src[ROWS - NEAR : ROWS, :]
+    first = (slice(None), pl.ds(0, edge))
+    final = (slice(None), pl.ds(length - edge, edge))
+    copies = moves(e, h, eps, first, lambda a: to_left.at[a], sems, 0)
+    copies += moves(e, h, eps, final, lambda a: to_right.at[a], sems, NARR - 1)
+    for copy in copies:
+        copy.start()
+    made = source_rows(*source_tags(profile, plane))
+    aux[...] = made
+    to_left[NARR - 1] = made[:, 0:edge]
+    to_right[NARR - 1] = made[:, length - edge : length]
+    for copy in copies:
+        copy.wait()
+
+
+def pack_near(e, h, eps, profile, plane, to_prev, to_next, sems):
+    length = TILES * LANES
+
+    def spot(ref):
+        return lambda a: ref.at[:, pl.ds(a * length, length)]
+
+    first = (pl.ds(0, NEAR), slice(None))
+    final = (pl.ds(ROWS - NEAR, NEAR), slice(None))
+    copies = moves(e, h, eps, first, spot(to_prev), sems, 0)
+    copies += moves(e, h, eps, final, spot(to_next), sems, NARR - 1)
+    for copy in copies:
+        copy.start()
     for k, tag in enumerate(source_tags(profile, plane)):
         cols = pl.ds((NARR - 1) * length + k * LANES, LANES)
         to_prev[:, cols] = tag[0:NEAR, :]
         to_next[:, cols] = tag[ROWS - NEAR : ROWS, :]
+    for copy in copies:
+        copy.wait()
 
 
 def near_source(ref):
@@ -278,7 +303,24 @@
     Stepper(waves, we, wh, wc, ws, acc).inside(HALO, HALO + ROWS - 1)
 
 
-def run_near(waves, _e, _h, _c, _s, _t, near_b, near_a, corner_l, corner_r, we, wh, wc, ws, acc, wa, made):
+def store_rows(we, wh, stage, e_out, h_out, sems, x, count):
+    copies = []
+    for a in range(6):
+        for k, (src, out, scale) in enumerate(((we, e_out, None), (wh, h_out, 0.5))):
+            for i in range(count // 8):
+                for j in range(TILES):
+                    value = src[pl.ds(at(a, HALO + x + 8 * i, HT + j), 8, stride=YV), :]
+                    value = value if scale is None else value * scale
+                    stage[6 * k + a, pl.ds(8 * i, 8), pl.ds(j * LANES, LANES)] = value
+            copy = pltpu.make_async_copy(
+                stage.at[6 * k + a], out.at[a // 3, a % 3, pl.ds(x, count), :], sems.at[6 * k + a]
+            )
+            copy.start()
+            copies.append(copy)
+    return copies
+
+
+def run_near(waves, _e, _h, _c, _s, _t, near_b, near_a, corner_l, corner_r, e_out, h_out, we, wh, wc, ws, acc, wa, made, stage, sems):
     length = TILES * LANES
     for k, (src, x) in enumerate(((near_b, FAR), (near_a, HALO + ROWS))):
         made[...] = near_source(src)
@@ -294,10 +336,12 @@
                 place(dst, a, x, HT + TILES + j, fix(corner_r[n, rows, cols]))
         fill_sources(wa, ws, x, NEAR)
     Stepper(waves, we, wh, wc, ws, acc).edges(FAR, HALO + ROWS - 1, NEAR)
+    for copy in store_rows(we, wh, stage, e_out, h_out, sems, 8, 16):
+        copy.wait()
 
 
 def run_far(
-    waves, _e, _h, _c, _s, _t, far_b, far_a, select, marks, e_out, h_out, packed, we, wh, wc, ws, acc, wa
+    waves, _e, _h, _c, _s, _t, _x, _y, far_b, far_a, select, marks, e_out, h_out, packed, we, wh, wc, ws, acc, wa, stage_lo, stage_hi, sems
 ):
     for n, (dst, a, fix) in enumerate(kinds(we, wh, wc, wa)):
         q = pl.ds(FAR * (n % 2), FAR)
@@ -309,14 +353,8 @@
     fill_sources(wa, ws, XR - FAR, FAR)
     Stepper(waves, we, wh, wc, ws, acc).edges(0, XR - FAR - 1, FAR)
 
-    for a in range(6):
-        for i in range(ROWS // 8):
-            for j in range(TILES):
-                src = pl.ds(at(a, HALO + 8 * i, HT + j), 8, stride=YV)
-                dst = (a // 3, a % 3, pl.ds(8 * i, 8), pl.ds(j * LANES, LANES))
-                e_out[dst] = we[src, :]
-                h_out[dst] = wh[src, :] * 0.5
-
+    stores = store_rows(we, wh, stage_lo, e_out, h_out, sems, 0, 8)
+    stores += store_rows(we, wh, stage_hi, e_out, h_out, sems.at[pl.ds(12, 12)], 24, 8)
     i, j = iota((LANES, LANES), 0), iota((LANES, LANES), 1)
     sums = dot(acc[pl.ds(at(0, HALO), ROWS * YV), :], (i // NZ == j % 4).astype(jnp.float32))
     per = BROWS * YV
@@ -327,6 +365,8 @@
         jnp.where(keep[None], sums.reshape(ROWS // BROWS, per, LANES), 0.0), axis=1
     ) / (STEPS * NZ)
     packed[...] = dot(select[...], blocks) + marks[...]
+    for copy in stores:
+        copy.wait()
 
 
 def collect(received, filter_matrix, out):
@@ -356,7 +396,7 @@
     return pl.pallas_call(
         kernel,
         in_specs=kwargs.pop("in_specs", [vmem] * count),
-        out_specs=(vmem,) * len(outs),
+        out_specs=kwargs.pop("out_specs", (vmem,) * len(outs)),
         out_shape=outs,
         compiler_params=pltpu.CompilerParams(vmem_limit_bytes=limit * 1024 * 1024),
         name=kernel.__name__,
@@ -379,19 +419,46 @@
 ):
     length = TILES * LANES
     edge = HT * LANES
-    plane = source_plane.astype(jnp.float32)
-    raw = (electric, magnetic, permittivity, source_profile, plane)
+    raw = (electric, magnetic, permittivity, source_profile, source_plane)
+    vmem = pl.BlockSpec(memory_space=pltpu.VMEM)
+    smem = pl.BlockSpec(memory_space=pltpu.SMEM)
+    hbm = pl.BlockSpec(memory_space=pltpu.HBM)
+    fixed = tuple(pltpu.with_memory_space_constraint(t, pltpu.HBM) for t in raw[:3])
+    raw = fixed + raw[3:]
+    packing = dict(
+        in_specs=[hbm] * 3 + [vmem] * 2,
+        scratch_shapes=[pltpu.SemaphoreType.DMA((2 * (NARR - 1),))],
+    )
+
+    y_own = (NARR, ROWS, edge)
+    to_left, to_right, aux = call(pack_side, (y_own, y_own, (ROWS, length)), 5, 3, **packing)(*raw)
+    left = shifted(to_right, "gy", 1)
+    right = shifted(to_left, "gy", -1)
 
     x_near = (NEAR, (NARR - 1) * length + 2 * LANES)
-    to_prev, to_next = call(pack_near, (x_near, x_near), 5, 2)(*raw)
-    to_prev, to_next, raw = lax.optimization_barrier((to_prev, to_next, raw))
+    to_prev, to_next = call(pack_near, (x_near, x_near), 5, 2, **packing)(*raw)
+    left, right, to_prev, to_next = lax.optimization_barrier((left, right, to_prev, to_next))
     near_b = shifted(to_next, "gx", 1)
     near_a = shifted(to_prev, "gx", -1)
 
-    y_own = (NARR, ROWS, edge)
-    to_left, to_right, aux = call(pack_side, (y_own, y_own, (ROWS, length)), 5, 3)(*raw)
-    left = shifted(to_right, "gy", 1)
-    right = shifted(to_left, "gy", -1)
+    own = (electric, magnetic, permittivity, aux)
+    x_far = (NARR // 2, 2 * FAR, FARW * LANES)
+    far_prev, far_next = call(pack_far, (x_far, x_far), 6, 2)(*own, left, right)
+    far_prev, far_next, left, right = lax.optimization_barrier((far_prev, far_next, left, right))
+    waves = jnp.asarray(
+        time_step
+        * np.sin(np.arange(1, STEPS + 1).astype(np.float32) * np.float32(omega_source * time_step)),
+        jnp.float32,
+    )
+    field = (2, 3, ROWS, length)
+    many = XR * YV
+    tail = PAD + YV
+    held = tuple((k * many + tail, LANES) for k in (6, 6, 1, 2, 1))
+    tags = pltpu.VMEM((many + tail, LANES), jnp.float32)
+    state = call(run_inside, held, 7, 15, in_specs=[smem] + [vmem] * 6, scratch_shapes=[tags])(
+        waves, *own, left, right
+    )
+    state, near_b, near_a = lax.optimization_barrier((state, near_b, near_a))
 
     y_corner = (NARR, 2 * NEAR, edge)
     made = pltpu.VMEM((NEAR, length), jnp.float32)
@@ -401,30 +468,11 @@
     corner_l = shifted(corner_right, "gy", 1)
     corner_r = shifted(corner_left, "gy", -1)
 
-    own = (electric, magnetic, permittivity, aux)
-    x_far = (NARR // 2, 2 * FAR, FARW * LANES)
-    far_prev, far_next = call(pack_far, (x_far, x_far), 6, 2)(*own, left, right)
-    far_prev, far_next, corner_l, corner_r, left, right = lax.optimization_barrier(
-        (far_prev, far_next, corner_l, corner_r, left, right)
+    far_prev, far_next, corner_l, corner_r = lax.optimization_barrier(
+        (far_prev, far_next, corner_l, corner_r)
     )
     far_b = shifted(far_next, "gx", 1)
     far_a = shifted(far_prev, "gx", -1)
-
-    waves = jnp.asarray(
-        time_step
-        * np.sin(np.arange(1, STEPS + 1).astype(np.float32) * np.float32(omega_source * time_step)),
-        jnp.float32,
-    )
-    field = (2, 3, ROWS, length)
-    many = XR * YV
-    tail = PAD + YV
-    vmem = pl.BlockSpec(memory_space=pltpu.VMEM)
-    smem = pl.BlockSpec(memory_space=pltpu.SMEM)
-    held = tuple((k * many + tail, LANES) for k in (6, 6, 1, 2, 1))
-    tags = pltpu.VMEM((many + tail, LANES), jnp.float32)
-    state = call(run_inside, held, 7, 15, in_specs=[smem] + [vmem] * 6, scratch_shapes=[tags])(
-        waves, *own, left, right
-    )
 
     count = ROWS // BROWS
     owner = block_owner[0, 0, :, 0]
@@ -445,24 +493,28 @@
     )[:, None]
     marks = jnp.dot(holder, named, precision=HIGH)
 
+    copy_sem = pltpu.SemaphoreType.DMA
     state = call(
         run_near,
-        held,
+        (field, field) + held,
         10,
         12,
         in_specs=[smem] + [vmem] * 9,
-        scratch_shapes=[tags, made],
-        input_output_aliases={1 + k: k for k in range(5)},
+        out_specs=(hbm,) * 2 + (vmem,) * 5,
+        scratch_shapes=[tags, made, pltpu.VMEM((12, 16, length), jnp.float32), copy_sem((12,))],
+        input_output_aliases={1 + k: 2 + k for k in range(5)},
     )(waves, *state, near_b, near_a, corner_l, corner_r)
+    stage = pltpu.VMEM((12, 8, length), jnp.float32)
     out = call(
         run_far,
         (field, field, (3 * owners, LANES)) + held,
-        10,
+        12,
         8,
-        in_specs=[smem] + [vmem] * 9,
-        scratch_shapes=[tags],
-        input_output_aliases={1 + k: 3 + k for k in range(5)},
-    )(waves, *state, far_b, far_a, chosen, marks)
+        in_specs=[smem] + [vmem] * 5 + [hbm] * 2 + [vmem] * 4,
+        out_specs=(hbm,) * 2 + (vmem,) * 6,
+        scratch_shapes=[tags, stage, stage, copy_sem((24,))],
+        input_output_aliases={6: 0, 7: 1} | {1 + k: 3 + k for k in range(5)},
+    )(waves, *state[2:], *state[:2], far_b, far_a, chosen, marks)
     field_e, field_h, packed = out[:3]
     received = lax.all_to_all(
         packed.reshape(owners, 3, LANES), "gy", split_axis=0, concat_axis=0, tiled=True

time: 128 us -> 120 us (0.938)
  waiting for transfers between devices: 37.7 us -> 31.7 us
  Pallas kernels: 50.8 us -> 54 us
  local copies, waits for them, and re-layouts: 4.59 us -> 1.9 us
    ppermute x8, waiting for transfers between devices: 37.7 us -> 31.7 us  [shifted(): lax.ppermute(array, axis, [(i, (i + by) % count) for i in range(count)])]
    pallas_call x4, Pallas kernels: 27.2 us -> 30.4 us  [the longest x1 16.5 us: per_device(): call(run_near, (field, field) + held, 10, 12, in_specs=[smem] + [vmem] *...]
    unnamed x20 -> x18, local copies, waits for them, and re-layouts: 4.56 us -> 1.87 us
  transfers between devices with their start and end apart: 8 -> 8, of which waited for: 4 -> 8; matrix products, arithmetic and copies ran while one was open for 0% -> 0% of each run, Pallas kernels for 30% -> 34%
where the time goes in v3:
time: 120 us; the launch traced here: 119 us
  Pallas kernels  54 us (45%)
  waiting for transfers between devices  31.7 us (26%)
  starting transfers between devices  18.6 us (16%)
  blocking collectives  11.9 us (10%)
  local copies, waits for them, and re-layouts  1.9 us (2%)
    ppermute x8, waiting for transfers between devices, shifted(): lax.ppermute(array, axis, [(i, (i + by) % count) for i in range(count)])  31.7 us
    pallas_call x1, Pallas kernels, per_device(): call(run_inside, held, 7, 15, in_specs=[smem] + [vmem] * 6, scratch_shape...  21.4 us
    ppermute x8, starting transfers between devices, shifted(): lax.ppermute(array, axis, [(i, (i + by) % count) for i in range(count)])  18.6 us
    pallas_call x1, Pallas kernels, per_device(): call(run_near, (field, field) + held, 10, 12, in_specs=[smem] + [vmem] *...  16.5 us
    all_to_all x1, blocking collectives, per_device(): lax.all_to_all(packed.reshape(owners, 3, LANES), 'gy', split_axis=0, conc...  11.9 us
    pallas_call x1, Pallas kernels, per_device(): call(run_far, (field, field, (3 * owners, LANES)) + held, 12, 8, in_specs...  10.4 us
  transfers between devices with their start and end apart: 8, of which 8 were waited for; matrix products, arithmetic and copies ran while one was open for 0% of the time, Pallas kernels for 34%

profile of v3, /device:TPU:1, one launch (start us, length us, event | category | flops | bytes accessed | tf_op | source)
XLA Modules:
  0.0 119.2 jit_solution(10626561326026773896)
XLA Ops:
  0.6 0.0 copy-start.3
  0.6 0.7 copy-done.3
  1.4 0.0 copy-start.6
  1.4 0.7 copy-done.6
  2.1 1.5 %pack_side.1 = (f32[14,32,384]{2,1,0:T(8,128)S(1)}, f32[14,32,384]{2,1,0:T(8,128)S(1)}, f32[32,2048]{1,0:T(8,128)S(1)}) custom-call(f32[2,3,32,2048]{3,2,1,0:T(8,128)} %e.7, f32[2,3,32,2048]{3,2,1,0:T(8,128)} %h.7, f32[32,2048]{1,0:T(8,128)} %eps.7, f32[2,32,64]{2,1,0:T(8,128)S(1)} %copy-done.3, s32[2,32]{1,0:T(2,128)S(1)} %copy-done.6), custom_call_target="tpu_custom_call" | custom-call | bytes 9000000 | tf_op jit(solution)/shard_map/pack_side/pallas_call | solution.py:434
  3.6 2.8 %collective-permute-start = (f32[14,32,384]{2,1,0:T(8,128)S(1)}, f32[14,32,384]{2,1,0:T(8,128)S(1)}, u32[]{:S(2)}, u32[]{:S(2)}) collective-permute-start(f32[14,32,384]{2,1,0:T(8,128)S(1)} %get-tuple-element.47), channel_id=1, source_target_pairs={{0,1},{1,2},{2,3},{3,4},{4,5},{5,6},{6,7},{7,8},{8,9},{9,10},{10,1... | collective-permute-start | bytes 2064392 | tf_op jit(solution)/shard_map/ppermute | solution.py:36
  6.4 0.0 copy-start
  6.4 0.0 copy-start.1
  6.4 0.0 copy-start.2
  6.4 0.7 collective-permute-start.1
  7.0 2.0 %pack_near.1 = (f32[8,26880]{1,0:T(8,128)S(1)}, f32[8,26880]{1,0:T(8,128)S(1)}) custom-call(f32[2,3,32,2048]{3,2,1,0:T(8,128)} %e.7, f32[2,3,32,2048]{3,2,1,0:T(8,128)} %h.7, f32[32,2048]{1,0:T(8,128)} %eps.7, f32[2,32,64]{2,1,0:T(8,128)S(1)} %copy-done.3, s32[2,32]{1,0:T(2,128)S(1)} %copy-done.6), custom_call_target="tpu_custom_call" | custom-call | bytes 6000000 | tf_op jit(solution)/shard_map/pack_near/pallas_call | solution.py:439
  9.0 5.2 %collective-permute-done.left = f32[14,32,384]{2,1,0:T(8,128)S(1)} collective-permute-done((f32[14,32,384]{2,1,0:T(8,128)S(1)}, f32[14,32,384]{2,1,0:T(8,128)S(1)}, u32[]{:S(2)}, u32[]{:S(2)}) %collective-permute-start) | collective-permute-done | bytes 688160 | tf_op jit(solution)/shard_map/ppermute | solution.py:36
  14.2 2.8 %collective-permute-done.1.right = f32[14,32,384]{2,1,0:T(8,128)S(1)} collective-permute-done((f32[14,32,384]{2,1,0:T(8,128)S(1)}, f32[14,32,384]{2,1,0:T(8,128)S(1)}, u32[]{:S(2)}, u32[]{:S(2)}) %collective-permute-start.1) | collective-permute-done | bytes 688160 | tf_op jit(solution)/shard_map/ppermute | solution.py:36
  17.0 2.7 %collective-permute-start.2 = (f32[8,26880]{1,0:T(8,128)S(1)}, f32[8,26880]{1,0:T(8,128)S(1)}, u32[]{:S(2)}, u32[]{:S(2)}) collective-permute-start(f32[8,26880]{1,0:T(8,128)S(1)} %get-tuple-element.62), channel_id=1, source_target_pairs={{0,16},{16,32},{32,48},{48,64},{64,80},{80,96},{96,112},{112,128},... | collective-permute-start | bytes 2580488 | tf_op jit(solution)/shard_map/ppermute | solution.py:36
  19.8 5.3 %collective-permute-start.3 = (f32[8,26880]{1,0:T(8,128)S(1)}, f32[8,26880]{1,0:T(8,128)S(1)}, u32[]{:S(2)}, u32[]{:S(2)}) collective-permute-start(f32[8,26880]{1,0:T(8,128)S(1)} %get-tuple-element.63), channel_id=1, source_target_pairs={{0,240},{16,0},{32,16},{48,32},{64,48},{80,64},{96,80},{112,96},{1... | collective-permute-start | bytes 2580488 | tf_op jit(solution)/shard_map/ppermute | solution.py:36
  25.1 0.0 copy-done
  25.1 0.0 copy-done.1
  25.1 0.0 copy-done.2
  25.1 0.0 copy-start.5
  25.1 0.2 pack_far.1
  25.3 0.4 copy-done.5
  25.7 21.4 %run_inside.1 = (f32[8096,128]{1,0:T(8,128)S(1)}, f32[8096,128]{1,0:T(8,128)S(1)}, f32[1376,128]{1,0:T(8,128)S(1)}, f32[2720,128]{1,0:T(8,128)S(1)}, f32[1376,128]{1,0:T(8,128)S(1)}) custom-call(f32[12]{0:T(128)S(1)} %copy-done.5, f32[2,3,32,2048]{3,2,1,0:T(8,128)S(1)} %copy-done, f32[2,3,32,2048]{3,2,1,0:T(8,128)S(1)} %copy-done.1, ...), custom_call_target="tpu_custom_call" | custom-call | bytes 45000000 | tf_op jit(solution)/shard_map/run_inside/pallas_call | solution.py:458
  47.2 0.0 copy-start.7
  47.2 0.0 copy-start.8
  47.2 8.8 %collective-permute-done.2.behind.near_b = f32[8,26880]{1,0:T(8,128)S(1)} collective-permute-done((f32[8,26880]{1,0:T(8,128)S(1)}, f32[8,26880]{1,0:T(8,128)S(1)}, u32[]{:S(2)}, u32[]{:S(2)}) %collective-permute-start.2) | collective-permute-done | bytes 860192 | tf_op jit(solution)/shard_map/ppermute | solution.py:36
  56.0 3.4 %collective-permute-done.3.ahead.near_a = f32[8,26880]{1,0:T(8,128)S(1)} collective-permute-done((f32[8,26880]{1,0:T(8,128)S(1)}, f32[8,26880]{1,0:T(8,128)S(1)}, u32[]{:S(2)}, u32[]{:S(2)}) %collective-permute-start.3) | collective-permute-done | bytes 860192 | tf_op jit(solution)/shard_map/ppermute | solution.py:36
  59.4 0.7 pack_corner.1
  60.1 2.0 %collective-permute-start.4 = (f32[14,16,384]{2,1,0:T(8,128)S(1)}, f32[14,16,384]{2,1,0:T(8,128)S(1)}, u32[]{:S(2)}, u32[]{:S(2)}) collective-permute-start(f32[14,16,384]{2,1,0:T(8,128)S(1)} %get-tuple-element.73), channel_id=1, source_target_pairs={{0,1},{1,2},{2,3},{3,4},{4,5},{5,6},{6,7},{7,8},{8,9},{9,10},{10,1... | collective-permute-start | bytes 1032200 | tf_op jit(solution)/shard_map/ppermute | solution.py:36
  62.1 0.0 collective-permute-start.5
  62.2 0.0 copy-done.7
  62.2 0.2 convert_reduce_fusion
  62.3 4.0 %collective-permute-done.4.corner_l = f32[14,16,384]{2,1,0:T(8,128)S(1)} collective-permute-done((f32[14,16,384]{2,1,0:T(8,128)S(1)}, f32[14,16,384]{2,1,0:T(8,128)S(1)}, u32[]{:S(2)}, u32[]{:S(2)}) %collective-permute-start.4) | collective-permute-done | bytes 344096 | tf_op jit(solution)/shard_map/ppermute | solution.py:36
  66.3 2.8 %collective-permute-done.5.corner_r = f32[14,16,384]{2,1,0:T(8,128)S(1)} collective-permute-done((f32[14,16,384]{2,1,0:T(8,128)S(1)}, f32[14,16,384]{2,1,0:T(8,128)S(1)}, u32[]{:S(2)}, u32[]{:S(2)}) %collective-permute-start.5) | collective-permute-done | bytes 344096 | tf_op jit(solution)/shard_map/ppermute | solution.py:36
  69.1 0.0 collective-permute-start.6
  69.1 5.1 %collective-permute-start.7 = (f32[7,8,2560]{2,1,0:T(8,128)S(1)}, f32[7,8,2560]{2,1,0:T(8,128)S(1)}, u32[]{:S(2)}, u32[]{:S(2)}) collective-permute-start(f32[7,8,2560]{2,1,0:T(8,128)S(1)} %get-tuple-element.85), channel_id=1, source_target_pairs={{0,240},{16,0},{32,16},{48,32},{64,48},{80,64},{96,80},{112,96},{1... | collective-permute-start | bytes 1720328 | tf_op jit(solution)/shard_map/ppermute | solution.py:36
  74.2 0.0 copy-done.8
  74.2 0.2 fusion.1.marks
  74.4 16.5 %run_near.1 = (f32[2,3,32,2048]{3,2,1,0:T(8,128)}, f32[2,3,32,2048]{3,2,1,0:T(8,128)}, f32[8096,128]{1,0:T(8,128)S(1)}, f32[8096,128]{1,0:T(8,128)S(1)}, f32[137...) custom-call(f32[12]{0:T(128)S(1)} %copy-done.5, ...), custom_call_target="tpu_custom_call", output_to_operand_aliasing={{2}: (1, {}), {3}: (2, {}), {4}: (3, {}), {5}: (4, {}), {6}... | custom-call | bytes 36000000 | tf_op jit(solution)/shard_map/run_near/pallas_call | solution.py:497
  91.0 2.2 %collective-permute-done.6.far_b = f32[7,8,2560]{2,1,0:T(8,128)S(1)} collective-permute-done((f32[7,8,2560]{2,1,0:T(8,128)S(1)}, f32[7,8,2560]{2,1,0:T(8,128)S(1)}, u32[]{:S(2)}, u32[]{:S(2)}) %collective-permute-start.6) | collective-permute-done | bytes 573472 | tf_op jit(solution)/shard_map/ppermute | solution.py:36
  93.1 2.5 %collective-permute-done.7.far_a = f32[7,8,2560]{2,1,0:T(8,128)S(1)} collective-permute-done((f32[7,8,2560]{2,1,0:T(8,128)S(1)}, f32[7,8,2560]{2,1,0:T(8,128)S(1)}, u32[]{:S(2)}, u32[]{:S(2)}) %collective-permute-start.7) | collective-permute-done | bytes 573472 | tf_op jit(solution)/shard_map/ppermute | solution.py:36
  95.6 0.0 copy-start.4
  95.6 10.4 %run_far.1 = (f32[2,3,32,2048]{3,2,1,0:T(8,128)}, f32[2,3,32,2048]{3,2,1,0:T(8,128)}, f32[48,128]{1,0:T(8,128)S(1)}, f32[8096,128]{1,0:T(8,128)S(1)}, f32[8096,1...) custom-call(f32[12]{0:T(128)S(1)} %copy-done.5, ...), custom_call_target="tpu_custom_call", output_to_operand_aliasing={{0}: (6, {}), {1}: (7, {}), {3}: (1, {}), {4}: (2, {}), {5}... | custom-call | bytes 24000000 | tf_op jit(solution)/shard_map/run_far/pallas_call | solution.py:508
  106.1 11.9 %all_to_all.5 = f32[16,3,128]{2,1,0:T(4,128)S(1)} all-to-all(f32[16,3,128]{2,1,0:T(4,128)S(1)} %reshape.36), channel_id=1, replica_groups=mesh['gx'=16,'gy'=16] {'gy'}, dimensions={0} | all-to-all | bytes 49152 | tf_op jit(solution)/shard_map/all_to_all | solution.py:519
  118.0 0.0 copy-done.4
  118.0 1.2 %collect.1 = f32[4,128]{1,0:T(4,128)} custom-call(f32[48,128]{1,0:T(8,128)S(1)} %reshape.37.received, f32[128,128]{1,0:T(8,128)S(1)} %copy-done.4), custom_call_target="tpu_custom_call" | custom-call | bytes 3000000 | tf_op jit(solution)/shard_map/collect/pallas_call | solution.py:522
  (5 shorter events, 0.0 us)
Async XLA Ops:
  0.6 0.8 copy-start.3
  1.4 0.7 copy-start.6
  3.6 10.6 %collective-permute-start = (f32[14,32,384]{2,1,0:T(8,128)S(1)}, f32[14,32,384]{2,1,0:T(8,128)S(1)}, u32[]{:S(2)}, u32[]{:S(2)}) collective-permute-start(f32[14,32,384]{2,1,0:T(8,128)S(1)} %get-tuple-element.47), channel_id=1, source_target_pairs={{0,1},{1,2},{2,3},{3,4},{4,5},{5,6},{6,7},{7,8},{8,9},{9,10},{10,1... | collective-permute-start | bytes 2064392 | tf_op jit(solution)/shard_map/ppermute | solution.py:36
  6.4 18.7 %copy-start = (f32[2,3,32,2048]{3,2,1,0:T(8,128)S(1)}, f32[2,3,32,2048]{3,2,1,0:T(8,128)}, u32[]{:S(2)}) copy-start(f32[2,3,32,2048]{3,2,1,0:T(8,128)} %e.7) | copy-start | bytes 4718596
  6.4 18.7 %copy-start.1 = (f32[2,3,32,2048]{3,2,1,0:T(8,128)S(1)}, f32[2,3,32,2048]{3,2,1,0:T(8,128)}, u32[]{:S(2)}) copy-start(f32[2,3,32,2048]{3,2,1,0:T(8,128)} %h.7) | copy-start | bytes 4718596
  6.4 18.7 %copy-start.2 = (f32[32,2048]{1,0:T(8,128)S(1)}, f32[32,2048]{1,0:T(8,128)}, u32[]{:S(2)}) copy-start(f32[32,2048]{1,0:T(8,128)} %eps.7) | copy-start | bytes 786436
  6.4 10.7 %collective-permute-start.1 = (f32[14,32,384]{2,1,0:T(8,128)S(1)}, f32[14,32,384]{2,1,0:T(8,128)S(1)}, u32[]{:S(2)}, u32[]{:S(2)}) collective-permute-start(f32[14,32,384]{2,1,0:T(8,128)S(1)} %get-tuple-element.48), channel_id=1, source_target_pairs={{0,15},{1,0},{2,1},{3,2},{4,3},{5,4},{6,5},{7,6},{8,7},{9,8},{10,9... | collective-permute-start | bytes 2064392 | tf_op jit(solution)/shard_map/ppermute | solution.py:36
  17.0 39.0 %collective-permute-start.2 = (f32[8,26880]{1,0:T(8,128)S(1)}, f32[8,26880]{1,0:T(8,128)S(1)}, u32[]{:S(2)}, u32[]{:S(2)}) collective-permute-start(f32[8,26880]{1,0:T(8,128)S(1)} %get-tuple-element.62), channel_id=1, source_target_pairs={{0,16},{16,32},{32,48},{48,64},{64,80},{80,96},{96,112},{112,128},... | collective-permute-start | bytes 2580488 | tf_op jit(solution)/shard_map/ppermute | solution.py:36
  19.8 39.7 %collective-permute-start.3 = (f32[8,26880]{1,0:T(8,128)S(1)}, f32[8,26880]{1,0:T(8,128)S(1)}, u32[]{:S(2)}, u32[]{:S(2)}) collective-permute-start(f32[8,26880]{1,0:T(8,128)S(1)} %get-tuple-element.63), channel_id=1, source_target_pairs={{0,240},{16,0},{32,16},{48,32},{64,48},{80,64},{96,80},{112,96},{1... | collective-permute-start | bytes 2580488 | tf_op jit(solution)/shard_map/ppermute | solution.py:36
  25.1 0.7 copy-start.5
  47.2 15.0 %copy-start.7 = (s32[1,1,16,1]{2,3,1,0:T(1,128)S(1)}, s32[1,1,16,1]{2,3,1,0:T(1,128)}, u32[]{:S(2)}) copy-start(s32[1,1,16,1]{2,3,1,0:T(1,128)} %param.14) | copy-start | bytes 196
  47.2 27.0 %copy-start.8 = (s32[1,1,16]{2,1,0:T(1,128)S(1)}, s32[1,1,16]{2,1,0:T(1,128)}, u32[]{:S(2)}) copy-start(s32[1,1,16]{2,1,0:T(1,128)} %param.15) | copy-start | bytes 196
  60.1 6.2 %collective-permute-start.4 = (f32[14,16,384]{2,1,0:T(8,128)S(1)}, f32[14,16,384]{2,1,0:T(8,128)S(1)}, u32[]{:S(2)}, u32[]{:S(2)}) collective-permute-start(f32[14,16,384]{2,1,0:T(8,128)S(1)} %get-tuple-element.73), channel_id=1, source_target_pairs={{0,1},{1,2},{2,3},{3,4},{4,5},{5,6},{6,7},{7,8},{8,9},{9,10},{10,1... | collective-permute-start | bytes 1032200 | tf_op jit(solution)/shard_map/ppermute | solution.py:36
  62.1 7.0 %collective-permute-start.5 = (f32[14,16,384]{2,1,0:T(8,128)S(1)}, f32[14,16,384]{2,1,0:T(8,128)S(1)}, u32[]{:S(2)}, u32[]{:S(2)}) collective-permute-start(f32[14,16,384]{2,1,0:T(8,128)S(1)} %get-tuple-element.74), channel_id=1, source_target_pairs={{0,15},{1,0},{2,1},{3,2},{4,3},{5,4},{6,5},{7,6},{8,7},{9,8},{10,9... | collective-permute-start | bytes 1032200 | tf_op jit(solution)/shard_map/ppermute | solution.py:36
  69.1 24.0 %collective-permute-start.6 = (f32[7,8,2560]{2,1,0:T(8,128)S(1)}, f32[7,8,2560]{2,1,0:T(8,128)S(1)}, u32[]{:S(2)}, u32[]{:S(2)}) collective-permute-start(f32[7,8,2560]{2,1,0:T(8,128)S(1)} %get-tuple-element.84), channel_id=1, source_target_pairs={{0,16},{16,32},{32,48},{48,64},{64,80},{80,96},{96,112},{112,128},... | collective-permute-start | bytes 1720328 | tf_op jit(solution)/shard_map/ppermute | solution.py:36
  69.1 26.5 %collective-permute-start.7 = (f32[7,8,2560]{2,1,0:T(8,128)S(1)}, f32[7,8,2560]{2,1,0:T(8,128)S(1)}, u32[]{:S(2)}, u32[]{:S(2)}) collective-permute-start(f32[7,8,2560]{2,1,0:T(8,128)S(1)} %get-tuple-element.85), channel_id=1, source_target_pairs={{0,240},{16,0},{32,16},{48,32},{64,48},{80,64},{96,80},{112,96},{1... | collective-permute-start | bytes 1720328 | tf_op jit(solution)/shard_map/ppermute | solution.py:36
  95.6 22.4 %copy-start.4 = (f32[128,128]{1,0:T(8,128)S(1)}, f32[128,128]{1,0:T(8,128)}, u32[]{:S(2)}) copy-start(f32[128,128]{1,0:T(8,128)} %filter_matrix.1) | copy-start | bytes 196612

commit v4 on v3

--- a/solution.py
+++ b/solution.py
@@ -73,24 +73,32 @@
     return jnp.where(level == 3, where[:, 1:2], out)
 
 
-def moves(e, h, eps, view, put_at, sems, base):
-    srcs = planes(e, h, eps)
-    return [
-        pltpu.make_async_copy(src.at[view], put_at(a), sems.at[base + a])
-        for a, src in enumerate(srcs)
+def fetch_tags(profile, plane, pv, lv, sems):
+    copies = [
+        pltpu.make_async_copy(profile, pv, sems.at[0]),
+        pltpu.make_async_copy(plane, lv, sems.at[1]),
     ]
-
-
-def pack_side(e, h, eps, profile, plane, to_left, to_right, aux, sems):
+    for copy in copies:
+        copy.start()
+    return copies
+
+
+def pack_side(e, h, eps, profile, plane, to_left, to_right, aux, pv, lv, sems):
     edge = HT * LANES
     length = TILES * LANES
-    first = (slice(None), pl.ds(0, edge))
-    final = (slice(None), pl.ds(length - edge, edge))
-    copies = moves(e, h, eps, first, lambda a: to_left.at[a], sems, 0)
-    copies += moves(e, h, eps, final, lambda a: to_right.at[a], sems, NARR - 1)
-    for copy in copies:
-        copy.start()
-    made = source_rows(*source_tags(profile, plane))
+    tags = fetch_tags(profile, plane, pv, lv, sems)
+    copies = []
+    for part, begin in ((to_left, 0), (to_right, length - edge)):
+        for a, src in enumerate(planes(e, h, eps)):
+            copies.append(
+                pltpu.make_async_copy(
+                    src.at[:, pl.ds(begin, edge)], part.at[a], sems.at[2 + len(copies)]
+                )
+            )
+            copies[-1].start()
+    for copy in tags:
+        copy.wait()
+    made = source_rows(*source_tags(pv, lv))
     aux[...] = made
     to_left[NARR - 1] = made[:, 0:edge]
     to_right[NARR - 1] = made[:, length - edge : length]
@@ -98,28 +106,39 @@
         copy.wait()
 
 
-def pack_near(e, h, eps, profile, plane, to_prev, to_next, sems):
+def pack_near(e, h, eps, profile, plane, edge_p, edge_n, mid_p, mid_n, pv, lv, sems):
+    edge = HT * LANES
     length = TILES * LANES
-
-    def spot(ref):
-        return lambda a: ref.at[:, pl.ds(a * length, length)]
-
-    first = (pl.ds(0, NEAR), slice(None))
-    final = (pl.ds(ROWS - NEAR, NEAR), slice(None))
-    copies = moves(e, h, eps, first, spot(to_prev), sems, 0)
-    copies += moves(e, h, eps, final, spot(to_next), sems, NARR - 1)
-    for copy in copies:
-        copy.start()
-    for k, tag in enumerate(source_tags(profile, plane)):
-        cols = pl.ds((NARR - 1) * length + k * LANES, LANES)
-        to_prev[:, cols] = tag[0:NEAR, :]
-        to_next[:, cols] = tag[ROWS - NEAR : ROWS, :]
+    inner = length - 2 * edge
+    tags = fetch_tags(profile, plane, pv, lv, sems)
+    copies = []
+    for x, side, middle in ((0, edge_p, mid_p), (ROWS - NEAR, edge_n, mid_n)):
+        for a, src in enumerate(planes(e, h, eps)):
+            for part, begin, size, to in (
+                (side, 0, edge, 2 * a * edge),
+                (side, length - edge, edge, (2 * a + 1) * edge),
+                (middle, edge, inner, a * inner),
+            ):
+                copies.append(
+                    pltpu.make_async_copy(
+                        src.at[pl.ds(x, NEAR), pl.ds(begin, size)],
+                        part.at[:, pl.ds(to, size)],
+                        sems.at[2 + len(copies)],
+                    )
+                )
+                copies[-1].start()
+    for copy in tags:
+        copy.wait()
+    for k, tag in enumerate(source_tags(pv, lv)):
+        cols = pl.ds((NARR - 1) * 2 * edge + k * LANES, LANES)
+        edge_p[:, cols] = tag[0:NEAR, :]
+        edge_n[:, cols] = tag[ROWS - NEAR : ROWS, :]
     for copy in copies:
         copy.wait()
 
 
 def near_source(ref):
-    base = (NARR - 1) * TILES * LANES
+    base = (NARR - 1) * 2 * HT * LANES
     return source_rows(ref[:, base : base + LANES], ref[:, base + LANES : base + 2 * LANES])
 
 
@@ -137,16 +156,17 @@
         to_next[p, q, LANES + length :] = right[a, hi : hi + FAR, :]
 
 
-def pack_corner(behind, ahead, to_left, to_right, made):
+def pack_corner(behind, ahead, to_left, to_right):
     edge = HT * LANES
     length = TILES * LANES
     for k, src in enumerate((behind, ahead)):
-        made[...] = near_source(src)
+        made = near_source(src)
         rows = pl.ds(NEAR * k, NEAR)
-        for a in range(NARR):
-            part = made if a == NARR - 1 else src.at[:, pl.ds(a * length, length)]
-            to_left[a, rows, :] = part[:, 0:edge]
-            to_right[a, rows, :] = part[:, length - edge : length]
+        to_left[NARR - 1, rows, :] = made[:, 0:edge]
+        to_right[NARR - 1, rows, :] = made[:, length - edge : length]
+        for a in range(NARR - 1):
+            to_left[a, rows, :] = src[:, 2 * a * edge : (2 * a + 1) * edge]
+            to_right[a, rows, :] = src[:, (2 * a + 1) * edge : (2 * a + 2) * edge]
 
 
 def at(a, x, v=0):
@@ -320,16 +340,26 @@
     return copies
 
 
-def run_near(waves, _e, _h, _c, _s, _t, near_b, near_a, corner_l, corner_r, e_out, h_out, we, wh, wc, ws, acc, wa, made, stage, sems):
-    length = TILES * LANES
-    for k, (src, x) in enumerate(((near_b, FAR), (near_a, HALO + ROWS))):
-        made[...] = near_source(src)
+def run_near(waves, _e, _h, _c, _s, _t, edge_b, edge_a, mid_b, mid_a, corner_l, corner_r, e_out, h_out, we, wh, wc, ws, acc, wa, made, stage, sems):
+    edge = HT * LANES
+    inner = (TILES - 2 * HT) * LANES
+
+    def near_tile(side, middle, n, j):
+        if n == NARR - 1:
+            return made[:, pl.ds(j * LANES, LANES)]
+        if HT <= j < TILES - HT:
+            return middle[:, pl.ds(n * inner + (j - HT) * LANES, LANES)]
+        j = j if j < HT else j - (TILES - 2 * HT)
+        return side[:, pl.ds(2 * n * edge + j * LANES, LANES)]
+
+    for k, (side, middle, x) in enumerate(
+        ((edge_b, mid_b, FAR), (edge_a, mid_a, HALO + ROWS))
+    ):
+        made[...] = near_source(side)
         rows = pl.ds(NEAR * k, NEAR)
         for n, (dst, a, fix) in enumerate(kinds(we, wh, wc, wa)):
             for j in range(TILES):
-                cols = pl.ds(j * LANES, LANES)
-                value = made[:, cols] if n == NARR - 1 else src[:, pl.ds(n * length + j * LANES, LANES)]
-                place(dst, a, x, HT + j, fix(value))
+                place(dst, a, x, HT + j, fix(near_tile(side, middle, n, j)))
             for j in range(HT):
                 cols = pl.ds(j * LANES, LANES)
                 place(dst, a, x, j, fix(corner_l[n, rows, cols]))
@@ -423,23 +453,47 @@
     vmem = pl.BlockSpec(memory_space=pltpu.VMEM)
     smem = pl.BlockSpec(memory_space=pltpu.SMEM)
     hbm = pl.BlockSpec(memory_space=pltpu.HBM)
-    fixed = tuple(pltpu.with_memory_space_constraint(t, pltpu.HBM) for t in raw[:3])
-    raw = fixed + raw[3:]
-    packing = dict(
-        in_specs=[hbm] * 3 + [vmem] * 2,
-        scratch_shapes=[pltpu.SemaphoreType.DMA((2 * (NARR - 1),))],
-    )
+    raw = tuple(pltpu.with_memory_space_constraint(t, pltpu.HBM) for t in raw)
+
+    def packing(copies):
+        return dict(
+            in_specs=[hbm] * 5,
+            scratch_shapes=[
+                pltpu.VMEM(source_profile.shape, jnp.float32),
+                pltpu.VMEM(source_plane.shape, jnp.int32),
+                pltpu.SemaphoreType.DMA((2 + copies,)),
+            ],
+        )
+
+    x_edge = (NEAR, (NARR - 1) * 2 * edge + 2 * LANES)
+    x_mid = (NEAR, (NARR - 1) * (length - 2 * edge))
+    edge_prev, edge_next, mid_prev, mid_next = call(
+        pack_near, (x_edge, x_edge, x_mid, x_mid), 5, 2, **packing(6 * (NARR - 1))
+    )(*raw)
+    edge_prev, edge_next, raw = lax.optimization_barrier((edge_prev, edge_next, raw))
+    edge_b = shifted(edge_next, "gx", 1)
+    edge_a = shifted(edge_prev, "gx", -1)
 
     y_own = (NARR, ROWS, edge)
-    to_left, to_right, aux = call(pack_side, (y_own, y_own, (ROWS, length)), 5, 3, **packing)(*raw)
+    to_left, to_right, aux = call(
+        pack_side, (y_own, y_own, (ROWS, length)), 5, 3, **packing(2 * (NARR - 1))
+    )(*raw)
+    edge_b, edge_a, to_left, to_right = lax.optimization_barrier(
+        (edge_b, edge_a, to_left, to_right)
+    )
     left = shifted(to_right, "gy", 1)
     right = shifted(to_left, "gy", -1)
 
-    x_near = (NEAR, (NARR - 1) * length + 2 * LANES)
-    to_prev, to_next = call(pack_near, (x_near, x_near), 5, 2, **packing)(*raw)
-    left, right, to_prev, to_next = lax.optimization_barrier((left, right, to_prev, to_next))
-    near_b = shifted(to_next, "gx", 1)
-    near_a = shifted(to_prev, "gx", -1)
+    y_corner = (NARR, 2 * NEAR, edge)
+    made = pltpu.VMEM((NEAR, length), jnp.float32)
+    corner_left, corner_right = call(pack_corner, (y_corner, y_corner), 2, 2)(edge_b, edge_a)
+    corner_left, corner_right, mid_prev, mid_next = lax.optimization_barrier(
+        (corner_left, corner_right, mid_prev, mid_next)
+    )
+    corner_l = shifted(corner_right, "gy", 1)
+    corner_r = shifted(corner_left, "gy", -1)
+    mid_b = shifted(mid_next, "gx", 1)
+    mid_a = shifted(mid_prev, "gx", -1)
 
     own = (electric, magnetic, permittivity, aux)
     x_far = (NARR // 2, 2 * FAR, FARW * LANES)
@@ -458,21 +512,12 @@
     state = call(run_inside, held, 7, 15, in_specs=[smem] + [vmem] * 6, scratch_shapes=[tags])(
         waves, *own, left, right
     )
-    state, near_b, near_a = lax.optimization_barrier((state, near_b, near_a))
-
-    y_corner = (NARR, 2 * NEAR, edge)
-    made = pltpu.VMEM((NEAR, length), jnp.float32)
-    corner_left, corner_right = call(
-        pack_corner, (y_corner, y_corner), 2, 2, scratch_shapes=[made]
-    )(near_b, near_a)
-    corner_l = shifted(corner_right, "gy", 1)
-    corner_r = shifted(corner_left, "gy", -1)
-
     far_prev, far_next, corner_l, corner_r = lax.optimization_barrier(
         (far_prev, far_next, corner_l, corner_r)
     )
     far_b = shifted(far_next, "gx", 1)
     far_a = shifted(far_prev, "gx", -1)
+    state, mid_b, mid_a = lax.optimization_barrier((state, mid_b, mid_a))
 
     count = ROWS // BROWS
     owner = block_owner[0, 0, :, 0]
@@ -497,13 +542,13 @@
     state = call(
         run_near,
         (field, field) + held,
-        10,
         12,
-        in_specs=[smem] + [vmem] * 9,
+        12,
+        in_specs=[smem] + [vmem] * 11,
         out_specs=(hbm,) * 2 + (vmem,) * 5,
         scratch_shapes=[tags, made, pltpu.VMEM((12, 16, length), jnp.float32), copy_sem((12,))],
         input_output_aliases={1 + k: 2 + k for k in range(5)},
-    )(waves, *state, near_b, near_a, corner_l, corner_r)
+    )(waves, *state, edge_b, edge_a, mid_b, mid_a, corner_l, corner_r)
     stage = pltpu.VMEM((12, 8, length), jnp.float32)
     out = call(
         run_far,

time: 120 us -> 135 us (1.12)
  blocking collectives: 11.9 us -> 39.3 us
  waiting for transfers between devices: 31.7 us -> 14.8 us
  starting transfers between devices: 18.6 us -> 25.3 us
  local copies, waits for them, and re-layouts: 1.9 us -> 0.07 us
    all_to_all x1, blocking collectives: 11.9 us -> 39.3 us  [per_device(): lax.all_to_all(packed.reshape(owners, 3, LANES), 'gy', split_axis=0, conc...]
    ppermute x8 -> x10, waiting for transfers between devices: 31.7 us -> 14.8 us  [shifted(): lax.ppermute(array, axis, [(i, (i + by) % count) for i in range(count)])]
    ppermute x8 -> x10, starting transfers between devices: 18.6 us -> 25.3 us  [shifted(): lax.ppermute(array, axis, [(i, (i + by) % count) for i in range(count)])]
    unnamed x18 -> x14, local copies, waits for them, and re-layouts: 1.87 us -> 0.04 us
  transfers between devices with their start and end apart: 8 -> 10, of which waited for: 8 -> 4; matrix products, arithmetic and copies ran while one was open for 0% -> 0% of each run, Pallas kernels for 34% -> 30%
where the time goes in v4:
time: 135 us
  Pallas kernels  54.3 us (40%)
  blocking collectives  39.3 us (29%)
  starting transfers between devices  25.3 us (19%)
  waiting for transfers between devices  14.8 us (11%)
    all_to_all x1, blocking collectives, per_device(): lax.all_to_all(packed.reshape(owners, 3, LANES), 'gy', split_axis=0, conc...  39.3 us
    ppermute x10, starting transfers between devices, shifted(): lax.ppermute(array, axis, [(i, (i + by) % count) for i in range(count)])  25.3 us
    pallas_call x1, Pallas kernels, per_device(): call(run_inside, held, 7, 15, in_specs=[smem] + [vmem] * 6, scratch_shape...  21.5 us
    pallas_call x1, Pallas kernels, per_device(): call(run_near, (field, field) + held, 12, 12, in_specs=[smem] + [vmem] *...  16.5 us
    ppermute x10, waiting for transfers between devices, shifted(): lax.ppermute(array, axis, [(i, (i + by) % count) for i in range(count)])  14.8 us
    pallas_call x1, Pallas kernels, per_device(): call(run_far, (field, field, (3 * owners, LANES)) + held, 12, 8, in_specs...  10.4 us
  transfers between devices with their start and end apart: 10, of which 4 were waited for; matrix products, arithmetic and copies ran while one was open for 0% of the time, Pallas kernels for 30%

profile of v4, /device:TPU:1, one launch (start us, length us, event | category | flops | bytes accessed | tf_op | source)
XLA Modules:
  0.0 135.1 jit_solution(2033631291926623324)
XLA Ops:
  0.6 2.2 %pack_near.1 = (f32[8,10240]{1,0:T(8,128)S(1)}, f32[8,10240]{1,0:T(8,128)S(1)}, f32[8,16640]{1,0:T(8,128)S(1)}, f32[8,16640]{1,0:T(8,128)S(1)}) custom-call(f32[2,3,32,2048]{3,2,1,0:T(8,128)} %e.6, f32[2,3,32,2048]{3,2,1,0:T(8,128)} %h.6, f32[32,2048]{1,0:T(8,128)} %eps.6, f32[2,32,64]{2,1,0:T(8,128)} %profile.2, s32[2,32]{1,0:T(2,128)} %plane.2), custom_call_target="tpu_custom_call" | custom-call | bytes 6000000 | tf_op jit(solution)/shard_map/pack_near/pallas_call | solution.py:470
  2.8 0.0 copy-start.5
  2.8 0.0 copy-start
  2.8 0.0 copy-start.1
  2.8 0.0 copy-start.2
  2.8 3.7 %collective-permute-start = (f32[8,10240]{1,0:T(8,128)S(1)}, f32[8,10240]{1,0:T(8,128)S(1)}, u32[]{:S(2)}, u32[]{:S(2)}) collective-permute-start(f32[8,10240]{1,0:T(8,128)S(1)} %get-tuple-element.67), channel_id=1, source_target_pairs={{0,16},{16,32},{32,48},{48,64},{64,80},{80,96},{96,112},{112,128},... | collective-permute-start | bytes 983048 | tf_op jit(solution)/shard_map/ppermute | solution.py:36
  6.5 5.4 %collective-permute-start.1 = (f32[8,10240]{1,0:T(8,128)S(1)}, f32[8,10240]{1,0:T(8,128)S(1)}, u32[]{:S(2)}, u32[]{:S(2)}) collective-permute-start(f32[8,10240]{1,0:T(8,128)S(1)} %get-tuple-element.68), channel_id=1, source_target_pairs={{0,240},{16,0},{32,16},{48,32},{64,48},{80,64},{96,80},{112,96},{1... | collective-permute-start | bytes 983048 | tf_op jit(solution)/shard_map/ppermute | solution.py:36
  11.9 1.8 %pack_side.1 = (f32[14,32,384]{2,1,0:T(8,128)S(1)}, f32[14,32,384]{2,1,0:T(8,128)S(1)}, f32[32,2048]{1,0:T(8,128)S(1)}) custom-call(f32[2,3,32,2048]{3,2,1,0:T(8,128)} %e.6, f32[2,3,32,2048]{3,2,1,0:T(8,128)} %h.6, f32[32,2048]{1,0:T(8,128)} %eps.6, f32[2,32,64]{2,1,0:T(8,128)} %profile.2, s32[2,32]{1,0:T(2,128)} %plane.2), custom_call_target="tpu_custom_call" | custom-call | bytes 9000000 | tf_op jit(solution)/shard_map/pack_side/pallas_call | solution.py:478
  13.7 6.2 %collective-permute-done.behind.edge_b = f32[8,10240]{1,0:T(8,128)S(1)} collective-permute-done((f32[8,10240]{1,0:T(8,128)S(1)}, f32[8,10240]{1,0:T(8,128)S(1)}, u32[]{:S(2)}, u32[]{:S(2)}) %collective-permute-start) | collective-permute-done | bytes 327712 | tf_op jit(solution)/shard_map/ppermute | solution.py:36
  19.9 3.4 %collective-permute-done.1.ahead.edge_a = f32[8,10240]{1,0:T(8,128)S(1)} collective-permute-done((f32[8,10240]{1,0:T(8,128)S(1)}, f32[8,10240]{1,0:T(8,128)S(1)}, u32[]{:S(2)}, u32[]{:S(2)}) %collective-permute-start.1) | collective-permute-done | bytes 327712 | tf_op jit(solution)/shard_map/ppermute | solution.py:36
  23.3 3.0 %collective-permute-start.2 = (f32[14,32,384]{2,1,0:T(8,128)S(1)}, f32[14,32,384]{2,1,0:T(8,128)S(1)}, u32[]{:S(2)}, u32[]{:S(2)}) collective-permute-start(f32[14,32,384]{2,1,0:T(8,128)S(1)} %get-tuple-element.71), channel_id=1, source_target_pairs={{0,1},{1,2},{2,3},{3,4},{4,5},{5,6},{6,7},{7,8},{8,9},{9,10},{10,1... | collective-permute-start | bytes 2064392 | tf_op jit(solution)/shard_map/ppermute | solution.py:36
  26.3 0.0 collective-permute-start.3
  26.3 0.5 pack_corner.1
  26.8 1.8 %collective-permute-start.6 = (f32[14,16,384]{2,1,0:T(8,128)S(1)}, f32[14,16,384]{2,1,0:T(8,128)S(1)}, u32[]{:S(2)}, u32[]{:S(2)}) collective-permute-start(f32[14,16,384]{2,1,0:T(8,128)S(1)} %get-tuple-element.99), channel_id=1, source_target_pairs={{0,1},{1,2},{2,3},{3,4},{4,5},{5,6},{6,7},{7,8},{8,9},{9,10},{10,1... | collective-permute-start | bytes 1032200 | tf_op jit(solution)/shard_map/ppermute | solution.py:36
  28.6 1.0 collective-permute-start.7
  29.6 0.0 copy-done.5
  29.6 0.2 convert_reduce_fusion
  29.8 0.1 collective-permute-start.4
  29.9 4.3 %collective-permute-done.2.left = f32[14,32,384]{2,1,0:T(8,128)S(1)} collective-permute-done((f32[14,32,384]{2,1,0:T(8,128)S(1)}, f32[14,32,384]{2,1,0:T(8,128)S(1)}, u32[]{:S(2)}, u32[]{:S(2)}) %collective-permute-start.2) | collective-permute-done | bytes 688160 | tf_op jit(solution)/shard_map/ppermute | solution.py:36
  34.2 5.3 %collective-permute-start.5 = (f32[8,16640]{1,0:T(8,128)S(1)}, f32[8,16640]{1,0:T(8,128)S(1)}, u32[]{:S(2)}, u32[]{:S(2)}) collective-permute-start(f32[8,16640]{1,0:T(8,128)S(1)} %get-tuple-element.89), channel_id=1, source_target_pairs={{0,240},{16,0},{32,16},{48,32},{64,48},{80,64},{96,80},{112,96},{1... | collective-permute-start | bytes 1597448 | tf_op jit(solution)/shard_map/ppermute | solution.py:36
  39.5 0.0 collective-permute-done.3.right
  39.5 0.0 copy-done
  39.5 0.0 copy-done.1
  39.5 0.0 copy-done.2
  39.5 0.0 copy-start.6
  39.5 0.0 copy-start.4
  39.6 0.2 pack_far.1
  39.8 0.0 collective-permute-done.6.corner_l
  39.8 0.9 collective-permute-done.7.corner_r
  40.7 0.0 collective-permute-start.8
  40.7 5.1 %collective-permute-start.9 = (f32[7,8,2560]{2,1,0:T(8,128)S(1)}, f32[7,8,2560]{2,1,0:T(8,128)S(1)}, u32[]{:S(2)}, u32[]{:S(2)}) collective-permute-start(f32[7,8,2560]{2,1,0:T(8,128)S(1)} %get-tuple-element.111), channel_id=1, source_target_pairs={{0,240},{16,0},{32,16},{48,32},{64,48},{80,64},{96,80},{112,96},{1... | collective-permute-start | bytes 1720328 | tf_op jit(solution)/shard_map/ppermute | solution.py:36
  45.8 0.0 copy-done.6
  45.8 0.2 fusion.1.marks
  46.0 0.0 copy-done.4
  46.0 21.5 %run_inside.1 = (f32[8096,128]{1,0:T(8,128)S(1)}, f32[8096,128]{1,0:T(8,128)S(1)}, f32[1376,128]{1,0:T(8,128)S(1)}, f32[2720,128]{1,0:T(8,128)S(1)}, f32[1376,128]{1,0:T(8,128)S(1)}) custom-call(f32[12]{0:T(128)S(1)} %copy-done.4, f32[2,3,32,2048]{3,2,1,0:T(8,128)S(1)} %copy-done, f32[2,3,32,2048]{3,2,1,0:T(8,128)S(1)} %copy-done.1, ...), custom_call_target="tpu_custom_call" | custom-call | bytes 45000000 | tf_op jit(solution)/shard_map/run_inside/pallas_call | solution.py:512
  67.5 0.0 collective-permute-done.4.mid_b
  67.5 0.0 collective-permute-done.5.mid_a
  67.5 16.5 %run_near.1 = (f32[2,3,32,2048]{3,2,1,0:T(8,128)}, f32[2,3,32,2048]{3,2,1,0:T(8,128)}, f32[8096,128]{1,0:T(8,128)S(1)}, f32[8096,128]{1,0:T(8,128)S(1)}, f32[137...) custom-call(f32[12]{0:T(128)S(1)} %copy-done.4, ...), custom_call_target="tpu_custom_call", output_to_operand_aliasing={{2}: (1, {}), {3}: (2, {}), {4}: (3, {}), {5}: (4, {}), {6}... | custom-call | bytes 36000000 | tf_op jit(solution)/shard_map/run_near/pallas_call | solution.py:542
  84.0 0.0 collective-permute-done.8.far_b
  84.0 0.0 collective-permute-done.9.far_a
  84.0 0.0 copy-start.3
  84.1 10.4 %run_far.1 = (f32[2,3,32,2048]{3,2,1,0:T(8,128)}, f32[2,3,32,2048]{3,2,1,0:T(8,128)}, f32[48,128]{1,0:T(8,128)S(1)}, f32[8096,128]{1,0:T(8,128)S(1)}, f32[8096,1...) custom-call(f32[12]{0:T(128)S(1)} %copy-done.4, ...), custom_call_target="tpu_custom_call", output_to_operand_aliasing={{0}: (6, {}), {1}: (7, {}), {3}: (1, {}), {4}: (2, {}), {5}... | custom-call | bytes 24000000 | tf_op jit(solution)/shard_map/run_far/pallas_call | solution.py:553
  94.5 39.3 %all_to_all.5 = f32[16,3,128]{2,1,0:T(4,128)S(1)} all-to-all(f32[16,3,128]{2,1,0:T(4,128)S(1)} %reshape.36), channel_id=1, replica_groups=mesh['gx'=16,'gy'=16] {'gy'}, dimensions={0} | all-to-all | bytes 49152 | tf_op jit(solution)/shard_map/all_to_all | solution.py:564
  133.9 0.0 copy-done.3
  133.9 1.2 collect.1
  (5 shorter events, 0.0 us)
Async XLA Ops:
  2.8 26.8 %copy-start.5 = (s32[1,1,16,1]{2,3,1,0:T(1,128)S(1)}, s32[1,1,16,1]{2,3,1,0:T(1,128)}, u32[]{:S(2)}) copy-start(s32[1,1,16,1]{2,3,1,0:T(1,128)} %param.14) | copy-start | bytes 196
  2.8 36.7 %copy-start = (f32[2,3,32,2048]{3,2,1,0:T(8,128)S(1)}, f32[2,3,32,2048]{3,2,1,0:T(8,128)}, u32[]{:S(2)}) copy-start(f32[2,3,32,2048]{3,2,1,0:T(8,128)} %e.6) | copy-start | bytes 4718596
  2.8 36.7 %copy-start.1 = (f32[2,3,32,2048]{3,2,1,0:T(8,128)S(1)}, f32[2,3,32,2048]{3,2,1,0:T(8,128)}, u32[]{:S(2)}) copy-start(f32[2,3,32,2048]{3,2,1,0:T(8,128)} %h.6) | copy-start | bytes 4718596
  2.8 36.7 %copy-start.2 = (f32[32,2048]{1,0:T(8,128)S(1)}, f32[32,2048]{1,0:T(8,128)}, u32[]{:S(2)}) copy-start(f32[32,2048]{1,0:T(8,128)} %eps.6) | copy-start | bytes 786436
  2.8 17.1 %collective-permute-start = (f32[8,10240]{1,0:T(8,128)S(1)}, f32[8,10240]{1,0:T(8,128)S(1)}, u32[]{:S(2)}, u32[]{:S(2)}) collective-permute-start(f32[8,10240]{1,0:T(8,128)S(1)} %get-tuple-element.67), channel_id=1, source_target_pairs={{0,16},{16,32},{32,48},{48,64},{64,80},{80,96},{96,112},{112,128},... | collective-permute-start | bytes 983048 | tf_op jit(solution)/shard_map/ppermute | solution.py:36
  6.5 16.8 %collective-permute-start.1 = (f32[8,10240]{1,0:T(8,128)S(1)}, f32[8,10240]{1,0:T(8,128)S(1)}, u32[]{:S(2)}, u32[]{:S(2)}) collective-permute-start(f32[8,10240]{1,0:T(8,128)S(1)} %get-tuple-element.68), channel_id=1, source_target_pairs={{0,240},{16,0},{32,16},{48,32},{64,48},{80,64},{96,80},{112,96},{1... | collective-permute-start | bytes 983048 | tf_op jit(solution)/shard_map/ppermute | solution.py:36
  23.3 10.9 %collective-permute-start.2 = (f32[14,32,384]{2,1,0:T(8,128)S(1)}, f32[14,32,384]{2,1,0:T(8,128)S(1)}, u32[]{:S(2)}, u32[]{:S(2)}) collective-permute-start(f32[14,32,384]{2,1,0:T(8,128)S(1)} %get-tuple-element.71), channel_id=1, source_target_pairs={{0,1},{1,2},{2,3},{3,4},{4,5},{5,6},{6,7},{7,8},{8,9},{9,10},{10,1... | collective-permute-start | bytes 2064392 | tf_op jit(solution)/shard_map/ppermute | solution.py:36
  26.3 13.2 %collective-permute-start.3 = (f32[14,32,384]{2,1,0:T(8,128)S(1)}, f32[14,32,384]{2,1,0:T(8,128)S(1)}, u32[]{:S(2)}, u32[]{:S(2)}) collective-permute-start(f32[14,32,384]{2,1,0:T(8,128)S(1)} %get-tuple-element.72), channel_id=1, source_target_pairs={{0,15},{1,0},{2,1},{3,2},{4,3},{5,4},{6,5},{7,6},{8,7},{9,8},{10,9... | collective-permute-start | bytes 2064392 | tf_op jit(solution)/shard_map/ppermute | solution.py:36
  26.8 13.0 %collective-permute-start.6 = (f32[14,16,384]{2,1,0:T(8,128)S(1)}, f32[14,16,384]{2,1,0:T(8,128)S(1)}, u32[]{:S(2)}, u32[]{:S(2)}) collective-permute-start(f32[14,16,384]{2,1,0:T(8,128)S(1)} %get-tuple-element.99), channel_id=1, source_target_pairs={{0,1},{1,2},{2,3},{3,4},{4,5},{5,6},{6,7},{7,8},{8,9},{9,10},{10,1... | collective-permute-start | bytes 1032200 | tf_op jit(solution)/shard_map/ppermute | solution.py:36
  28.6 12.1 %collective-permute-start.7 = (f32[14,16,384]{2,1,0:T(8,128)S(1)}, f32[14,16,384]{2,1,0:T(8,128)S(1)}, u32[]{:S(2)}, u32[]{:S(2)}) collective-permute-start(f32[14,16,384]{2,1,0:T(8,128)S(1)} %get-tuple-element.100), channel_id=1, source_target_pairs={{0,15},{1,0},{2,1},{3,2},{4,3},{5,4},{6,5},{7,6},{8,7},{9,8},{10,9... | collective-permute-start | bytes 1032200 | tf_op jit(solution)/shard_map/ppermute | solution.py:36
  29.8 37.7 %collective-permute-start.4 = (f32[8,16640]{1,0:T(8,128)S(1)}, f32[8,16640]{1,0:T(8,128)S(1)}, u32[]{:S(2)}, u32[]{:S(2)}) collective-permute-start(f32[8,16640]{1,0:T(8,128)S(1)} %get-tuple-element.88), channel_id=1, source_target_pairs={{0,16},{16,32},{32,48},{48,64},{64,80},{80,96},{96,112},{112,128},... | collective-permute-start | bytes 1597448 | tf_op jit(solution)/shard_map/ppermute | solution.py:36
  34.2 33.3 %collective-permute-start.5 = (f32[8,16640]{1,0:T(8,128)S(1)}, f32[8,16640]{1,0:T(8,128)S(1)}, u32[]{:S(2)}, u32[]{:S(2)}) collective-permute-start(f32[8,16640]{1,0:T(8,128)S(1)} %get-tuple-element.89), channel_id=1, source_target_pairs={{0,240},{16,0},{32,16},{48,32},{64,48},{80,64},{96,80},{112,96},{1... | collective-permute-start | bytes 1597448 | tf_op jit(solution)/shard_map/ppermute | solution.py:36
  39.5 6.2 %copy-start.6 = (s32[1,1,16]{2,1,0:T(1,128)S(1)}, s32[1,1,16]{2,1,0:T(1,128)}, u32[]{:S(2)}) copy-start(s32[1,1,16]{2,1,0:T(1,128)} %param.15) | copy-start | bytes 196
  39.5 6.4 %copy-start.4 = (f32[12]{0:T(128)S(1)}, f32[12]{0:T(128)}, u32[]{:S(2)}) copy-start(f32[12]{0:T(128)} %constant.12.clone.waves) | copy-start | bytes 148
  40.7 43.4 %collective-permute-start.8 = (f32[7,8,2560]{2,1,0:T(8,128)S(1)}, f32[7,8,2560]{2,1,0:T(8,128)S(1)}, u32[]{:S(2)}, u32[]{:S(2)}) collective-permute-start(f32[7,8,2560]{2,1,0:T(8,128)S(1)} %get-tuple-element.110), channel_id=1, source_target_pairs={{0,16},{16,32},{32,48},{48,64},{64,80},{80,96},{96,112},{112,128},... | collective-permute-start | bytes 1720328 | tf_op jit(solution)/shard_map/ppermute | solution.py:36
  40.7 43.4 %collective-permute-start.9 = (f32[7,8,2560]{2,1,0:T(8,128)S(1)}, f32[7,8,2560]{2,1,0:T(8,128)S(1)}, u32[]{:S(2)}, u32[]{:S(2)}) collective-permute-start(f32[7,8,2560]{2,1,0:T(8,128)S(1)} %get-tuple-element.111), channel_id=1, source_target_pairs={{0,240},{16,0},{32,16},{48,32},{64,48},{80,64},{96,80},{112,96},{1... | collective-permute-start | bytes 1720328 | tf_op jit(solution)/shard_map/ppermute | solution.py:36
  84.0 49.8 %copy-start.3 = (f32[128,128]{1,0:T(8,128)S(1)}, f32[128,128]{1,0:T(8,128)}, u32[]{:S(2)}) copy-start(f32[128,128]{1,0:T(8,128)} %filter_matrix.1) | copy-start | bytes 196612

commit v5 on v4

--- a/solution.py
+++ b/solution.py
@@ -478,9 +478,6 @@
     to_left, to_right, aux = call(
         pack_side, (y_own, y_own, (ROWS, length)), 5, 3, **packing(2 * (NARR - 1))
     )(*raw)
-    edge_b, edge_a, to_left, to_right = lax.optimization_barrier(
-        (edge_b, edge_a, to_left, to_right)
-    )
     left = shifted(to_right, "gy", 1)
     right = shifted(to_left, "gy", -1)
 
@@ -498,7 +495,9 @@
     own = (electric, magnetic, permittivity, aux)
     x_far = (NARR // 2, 2 * FAR, FARW * LANES)
     far_prev, far_next = call(pack_far, (x_far, x_far), 6, 2)(*own, left, right)
-    far_prev, far_next, left, right = lax.optimization_barrier((far_prev, far_next, left, right))
+    far_prev, far_next, left, right, corner_l, corner_r = lax.optimization_barrier(
+        (far_prev, far_next, left, right, corner_l, corner_r)
+    )
     waves = jnp.asarray(
         time_step
         * np.sin(np.arange(1, STEPS + 1).astype(np.float32) * np.float32(omega_source * time_step)),
@@ -512,12 +511,9 @@
     state = call(run_inside, held, 7, 15, in_specs=[smem] + [vmem] * 6, scratch_shapes=[tags])(
         waves, *own, left, right
     )
-    far_prev, far_next, corner_l, corner_r = lax.optimization_barrier(
-        (far_prev, far_next, corner_l, corner_r)
-    )
+    far_prev, far_next, state = lax.optimization_barrier((far_prev, far_next, state))
     far_b = shifted(far_next, "gx", 1)
     far_a = shifted(far_prev, "gx", -1)
-    state, mid_b, mid_a = lax.optimization_barrier((state, mid_b, mid_a))
 
     count = ROWS // BROWS
     owner = block_owner[0, 0, :, 0]

time: 135 us -> 126 us (0.933)
  blocking collectives: 39.3 us -> 27.7 us
  starting transfers between devices: 25.3 us -> 29.3 us
  waiting for transfers between devices: 14.8 us -> 13 us
    all_to_all x1, blocking collectives: 39.3 us -> 27.7 us  [per_device(): lax.all_to_all(packed.reshape(owners, 3, LANES), 'gy', split_axis=0, conc...]
    ppermute x10, starting transfers between devices: 25.3 us -> 29.3 us  [shifted(): lax.ppermute(array, axis, [(i, (i + by) % count) for i in range(count)])]
    ppermute x10, waiting for transfers between devices: 14.8 us -> 13 us  [shifted(): lax.ppermute(array, axis, [(i, (i + by) % count) for i in range(count)])]
  transfers between devices with their start and end apart: 10 -> 10, of which waited for: 4 -> 2; matrix products, arithmetic and copies ran while one was open for 0% -> 0% of each run, Pallas kernels for 30% -> 31%
where the time goes in v5:
time: 126 us
  Pallas kernels  54.5 us (43%)
  starting transfers between devices  29.3 us (23%)
  blocking collectives  27.7 us (22%)
  waiting for transfers between devices  13 us (10%)
    ppermute x10, starting transfers between devices, shifted(): lax.ppermute(array, axis, [(i, (i + by) % count) for i in range(count)])  29.3 us
    all_to_all x1, blocking collectives, per_device(): lax.all_to_all(packed.reshape(owners, 3, LANES), 'gy', split_axis=0, conc...  27.7 us
    pallas_call x1, Pallas kernels, per_device(): call(run_inside, held, 7, 15, in_specs=[smem] + [vmem] * 6, scratch_shape...  21.5 us
    pallas_call x1, Pallas kernels, per_device(): call(run_near, (field, field) + held, 12, 12, in_specs=[smem] + [vmem] *...  16.5 us
    ppermute x10, waiting for transfers between devices, shifted(): lax.ppermute(array, axis, [(i, (i + by) % count) for i in range(count)])  13 us
    pallas_call x1, Pallas kernels, per_device(): call(run_far, (field, field, (3 * owners, LANES)) + held, 12, 8, in_specs...  10.4 us
  transfers between devices with their start and end apart: 10, of which 2 were waited for; matrix products, arithmetic and copies ran while one was open for 0% of the time, Pallas kernels for 31%

profile of v5, /device:TPU:1, one launch (start us, length us, event | category | flops | bytes accessed | tf_op | source)
XLA Modules:
  0.0 126.1 jit_solution(10609535478969969156)
XLA Ops:
  0.6 2.2 %pack_near.1 = (f32[8,10240]{1,0:T(8,128)S(1)}, f32[8,10240]{1,0:T(8,128)S(1)}, f32[8,16640]{1,0:T(8,128)S(1)}, f32[8,16640]{1,0:T(8,128)S(1)}) custom-call(f32[2,3,32,2048]{3,2,1,0:T(8,128)} %e.6, f32[2,3,32,2048]{3,2,1,0:T(8,128)} %h.6, f32[32,2048]{1,0:T(8,128)} %eps.6, f32[2,32,64]{2,1,0:T(8,128)} %profile.2, s32[2,32]{1,0:T(2,128)} %plane.2), custom_call_target="tpu_custom_call" | custom-call | bytes 6000000 | tf_op jit(solution)/shard_map/pack_near/pallas_call | solution.py:470
  2.8 0.0 copy-start.5
  2.8 0.0 copy-start
  2.8 0.0 copy-start.1
  2.8 0.0 copy-start.2
  2.8 1.9 %pack_side.1 = (f32[14,32,384]{2,1,0:T(8,128)S(1)}, f32[14,32,384]{2,1,0:T(8,128)S(1)}, f32[32,2048]{1,0:T(8,128)S(1)}) custom-call(f32[2,3,32,2048]{3,2,1,0:T(8,128)} %e.6, f32[2,3,32,2048]{3,2,1,0:T(8,128)} %h.6, f32[32,2048]{1,0:T(8,128)} %eps.6, f32[2,32,64]{2,1,0:T(8,128)} %profile.2, s32[2,32]{1,0:T(2,128)} %plane.2), custom_call_target="tpu_custom_call" | custom-call | bytes 9000000 | tf_op jit(solution)/shard_map/pack_side/pallas_call | solution.py:478
  4.8 2.8 %collective-permute-start = (f32[14,32,384]{2,1,0:T(8,128)S(1)}, f32[14,32,384]{2,1,0:T(8,128)S(1)}, u32[]{:S(2)}, u32[]{:S(2)}) collective-permute-start(f32[14,32,384]{2,1,0:T(8,128)S(1)} %get-tuple-element.61), channel_id=1, source_target_pairs={{0,1},{1,2},{2,3},{3,4},{4,5},{5,6},{6,7},{7,8},{8,9},{9,10},{10,1... | collective-permute-start | bytes 2064392 | tf_op jit(solution)/shard_map/ppermute | solution.py:36
  7.6 0.6 collective-permute-start.1
  8.2 2.1 %collective-permute-start.2 = (f32[8,10240]{1,0:T(8,128)S(1)}, f32[8,10240]{1,0:T(8,128)S(1)}, u32[]{:S(2)}, u32[]{:S(2)}) collective-permute-start(f32[8,10240]{1,0:T(8,128)S(1)} %get-tuple-element.65), channel_id=1, source_target_pairs={{0,16},{16,32},{32,48},{48,64},{64,80},{80,96},{96,112},{112,128},... | collective-permute-start | bytes 983048 | tf_op jit(solution)/shard_map/ppermute | solution.py:36
  10.3 5.3 %collective-permute-start.3 = (f32[8,10240]{1,0:T(8,128)S(1)}, f32[8,10240]{1,0:T(8,128)S(1)}, u32[]{:S(2)}, u32[]{:S(2)}) collective-permute-start(f32[8,10240]{1,0:T(8,128)S(1)} %get-tuple-element.66), channel_id=1, source_target_pairs={{0,240},{16,0},{32,16},{48,32},{64,48},{80,64},{96,80},{112,96},{1... | collective-permute-start | bytes 983048 | tf_op jit(solution)/shard_map/ppermute | solution.py:36
  15.6 7.3 %collective-permute-done.2.behind.edge_b = f32[8,10240]{1,0:T(8,128)S(1)} collective-permute-done((f32[8,10240]{1,0:T(8,128)S(1)}, f32[8,10240]{1,0:T(8,128)S(1)}, u32[]{:S(2)}, u32[]{:S(2)}) %collective-permute-start.2) | collective-permute-done | bytes 327712 | tf_op jit(solution)/shard_map/ppermute | solution.py:36
  22.9 5.6 %collective-permute-done.3.ahead.edge_a = f32[8,10240]{1,0:T(8,128)S(1)} collective-permute-done((f32[8,10240]{1,0:T(8,128)S(1)}, f32[8,10240]{1,0:T(8,128)S(1)}, u32[]{:S(2)}, u32[]{:S(2)}) %collective-permute-start.3) | collective-permute-done | bytes 327712 | tf_op jit(solution)/shard_map/ppermute | solution.py:36
  28.6 0.5 pack_corner.1
  29.1 1.6 %collective-permute-start.4 = (f32[14,16,384]{2,1,0:T(8,128)S(1)}, f32[14,16,384]{2,1,0:T(8,128)S(1)}, u32[]{:S(2)}, u32[]{:S(2)}) collective-permute-start(f32[14,16,384]{2,1,0:T(8,128)S(1)} %get-tuple-element.71), channel_id=1, source_target_pairs={{0,1},{1,2},{2,3},{3,4},{4,5},{5,6},{6,7},{7,8},{8,9},{9,10},{10,1... | collective-permute-start | bytes 1032200 | tf_op jit(solution)/shard_map/ppermute | solution.py:36
  30.6 6.1 %collective-permute-start.5 = (f32[14,16,384]{2,1,0:T(8,128)S(1)}, f32[14,16,384]{2,1,0:T(8,128)S(1)}, u32[]{:S(2)}, u32[]{:S(2)}) collective-permute-start(f32[14,16,384]{2,1,0:T(8,128)S(1)} %get-tuple-element.72), channel_id=1, source_target_pairs={{0,15},{1,0},{2,1},{3,2},{4,3},{5,4},{6,5},{7,6},{8,7},{9,8},{10,9... | collective-permute-start | bytes 1032200 | tf_op jit(solution)/shard_map/ppermute | solution.py:36
  36.8 0.0 copy-done.5
  36.8 0.2 convert_reduce_fusion
  37.0 0.2 collective-permute-start.6
  37.2 0.0 collective-permute-done.left
  37.2 5.4 %collective-permute-start.7 = (f32[8,16640]{1,0:T(8,128)S(1)}, f32[8,16640]{1,0:T(8,128)S(1)}, u32[]{:S(2)}, u32[]{:S(2)}) collective-permute-start(f32[8,16640]{1,0:T(8,128)S(1)} %get-tuple-element.88), channel_id=1, source_target_pairs={{0,240},{16,0},{32,16},{48,32},{64,48},{80,64},{96,80},{112,96},{1... | collective-permute-start | bytes 1597448 | tf_op jit(solution)/shard_map/ppermute | solution.py:36
  42.6 0.0 collective-permute-done.1.right
  42.6 0.0 copy-done
  42.6 0.0 copy-done.1
  42.6 0.0 copy-done.2
  42.6 0.0 copy-start.4
  42.6 0.2 pack_far.1
  42.8 0.0 collective-permute-done.4.corner_l
  42.9 0.0 collective-permute-done.5.corner_r
  42.9 0.4 copy-done.4
  43.3 0.0 copy-start.6
  43.3 21.5 %run_inside.1 = (f32[8096,128]{1,0:T(8,128)S(1)}, f32[8096,128]{1,0:T(8,128)S(1)}, f32[1376,128]{1,0:T(8,128)S(1)}, f32[2720,128]{1,0:T(8,128)S(1)}, f32[1376,128]{1,0:T(8,128)S(1)}) custom-call(f32[12]{0:T(128)S(1)} %copy-done.4, f32[2,3,32,2048]{3,2,1,0:T(8,128)S(1)} %copy-done, f32[2,3,32,2048]{3,2,1,0:T(8,128)S(1)} %copy-done.1, ...), custom_call_target="tpu_custom_call" | custom-call | bytes 45000000 | tf_op jit(solution)/shard_map/run_inside/pallas_call | solution.py:511
  64.7 0.1 collective-permute-start.8
  64.8 5.1 %collective-permute-start.9 = (f32[7,8,2560]{2,1,0:T(8,128)S(1)}, f32[7,8,2560]{2,1,0:T(8,128)S(1)}, u32[]{:S(2)}, u32[]{:S(2)}) collective-permute-start(f32[7,8,2560]{2,1,0:T(8,128)S(1)} %get-tuple-element.99), channel_id=1, source_target_pairs={{0,240},{16,0},{32,16},{48,32},{64,48},{80,64},{96,80},{112,96},{1... | collective-permute-start | bytes 1720328 | tf_op jit(solution)/shard_map/ppermute | solution.py:36
  69.9 0.0 copy-done.6
  69.9 0.2 fusion.1.marks
  70.1 0.0 collective-permute-done.6.mid_b
  70.1 0.0 collective-permute-done.7.mid_a
  70.1 16.5 %run_near.1 = (f32[2,3,32,2048]{3,2,1,0:T(8,128)}, f32[2,3,32,2048]{3,2,1,0:T(8,128)}, f32[8096,128]{1,0:T(8,128)S(1)}, f32[8096,128]{1,0:T(8,128)S(1)}, f32[137...) custom-call(f32[12]{0:T(128)S(1)} %copy-done.4, ...), custom_call_target="tpu_custom_call", output_to_operand_aliasing={{2}: (1, {}), {3}: (2, {}), {4}: (3, {}), {5}: (4, {}), {6}... | custom-call | bytes 36000000 | tf_op jit(solution)/shard_map/run_near/pallas_call | solution.py:538
  86.7 0.0 collective-permute-done.8.far_b
  86.7 0.0 collective-permute-done.9.far_a
  86.7 0.0 copy-start.3
  86.7 10.4 %run_far.1 = (f32[2,3,32,2048]{3,2,1,0:T(8,128)}, f32[2,3,32,2048]{3,2,1,0:T(8,128)}, f32[48,128]{1,0:T(8,128)S(1)}, f32[8096,128]{1,0:T(8,128)S(1)}, f32[8096,1...) custom-call(f32[12]{0:T(128)S(1)} %copy-done.4, ...), custom_call_target="tpu_custom_call", output_to_operand_aliasing={{0}: (6, {}), {1}: (7, {}), {3}: (1, {}), {4}: (2, {}), {5}... | custom-call | bytes 24000000 | tf_op jit(solution)/shard_map/run_far/pallas_call | solution.py:549
  97.2 27.7 %all_to_all.5 = f32[16,3,128]{2,1,0:T(4,128)S(1)} all-to-all(f32[16,3,128]{2,1,0:T(4,128)S(1)} %reshape.36), channel_id=1, replica_groups=mesh['gx'=16,'gy'=16] {'gy'}, dimensions={0} | all-to-all | bytes 49152 | tf_op jit(solution)/shard_map/all_to_all | solution.py:560
  124.9 0.0 copy-done.3
  124.9 1.2 collect.1
  (5 shorter events, 0.0 us)
Async XLA Ops:
  2.8 34.0 %copy-start.5 = (s32[1,1,16,1]{2,3,1,0:T(1,128)S(1)}, s32[1,1,16,1]{2,3,1,0:T(1,128)}, u32[]{:S(2)}) copy-start(s32[1,1,16,1]{2,3,1,0:T(1,128)} %param.14) | copy-start | bytes 196
  2.8 39.8 %copy-start = (f32[2,3,32,2048]{3,2,1,0:T(8,128)S(1)}, f32[2,3,32,2048]{3,2,1,0:T(8,128)}, u32[]{:S(2)}) copy-start(f32[2,3,32,2048]{3,2,1,0:T(8,128)} %e.6) | copy-start | bytes 4718596
  2.8 39.8 %copy-start.1 = (f32[2,3,32,2048]{3,2,1,0:T(8,128)S(1)}, f32[2,3,32,2048]{3,2,1,0:T(8,128)}, u32[]{:S(2)}) copy-start(f32[2,3,32,2048]{3,2,1,0:T(8,128)} %h.6) | copy-start | bytes 4718596
  2.8 39.8 %copy-start.2 = (f32[32,2048]{1,0:T(8,128)S(1)}, f32[32,2048]{1,0:T(8,128)}, u32[]{:S(2)}) copy-start(f32[32,2048]{1,0:T(8,128)} %eps.6) | copy-start | bytes 786436
  4.8 32.4 %collective-permute-start = (f32[14,32,384]{2,1,0:T(8,128)S(1)}, f32[14,32,384]{2,1,0:T(8,128)S(1)}, u32[]{:S(2)}, u32[]{:S(2)}) collective-permute-start(f32[14,32,384]{2,1,0:T(8,128)S(1)} %get-tuple-element.61), channel_id=1, source_target_pairs={{0,1},{1,2},{2,3},{3,4},{4,5},{5,6},{6,7},{7,8},{8,9},{9,10},{10,1... | collective-permute-start | bytes 2064392 | tf_op jit(solution)/shard_map/ppermute | solution.py:36
  7.6 35.0 %collective-permute-start.1 = (f32[14,32,384]{2,1,0:T(8,128)S(1)}, f32[14,32,384]{2,1,0:T(8,128)S(1)}, u32[]{:S(2)}, u32[]{:S(2)}) collective-permute-start(f32[14,32,384]{2,1,0:T(8,128)S(1)} %get-tuple-element.62), channel_id=1, source_target_pairs={{0,15},{1,0},{2,1},{3,2},{4,3},{5,4},{6,5},{7,6},{8,7},{9,8},{10,9... | collective-permute-start | bytes 2064392 | tf_op jit(solution)/shard_map/ppermute | solution.py:36
  8.2 14.7 %collective-permute-start.2 = (f32[8,10240]{1,0:T(8,128)S(1)}, f32[8,10240]{1,0:T(8,128)S(1)}, u32[]{:S(2)}, u32[]{:S(2)}) collective-permute-start(f32[8,10240]{1,0:T(8,128)S(1)} %get-tuple-element.65), channel_id=1, source_target_pairs={{0,16},{16,32},{32,48},{48,64},{64,80},{80,96},{96,112},{112,128},... | collective-permute-start | bytes 983048 | tf_op jit(solution)/shard_map/ppermute | solution.py:36
  10.3 18.3 %collective-permute-start.3 = (f32[8,10240]{1,0:T(8,128)S(1)}, f32[8,10240]{1,0:T(8,128)S(1)}, u32[]{:S(2)}, u32[]{:S(2)}) collective-permute-start(f32[8,10240]{1,0:T(8,128)S(1)} %get-tuple-element.66), channel_id=1, source_target_pairs={{0,240},{16,0},{32,16},{48,32},{64,48},{80,64},{96,80},{112,96},{1... | collective-permute-start | bytes 983048 | tf_op jit(solution)/shard_map/ppermute | solution.py:36
  29.1 13.8 %collective-permute-start.4 = (f32[14,16,384]{2,1,0:T(8,128)S(1)}, f32[14,16,384]{2,1,0:T(8,128)S(1)}, u32[]{:S(2)}, u32[]{:S(2)}) collective-permute-start(f32[14,16,384]{2,1,0:T(8,128)S(1)} %get-tuple-element.71), channel_id=1, source_target_pairs={{0,1},{1,2},{2,3},{3,4},{4,5},{5,6},{6,7},{7,8},{8,9},{9,10},{10,1... | collective-permute-start | bytes 1032200 | tf_op jit(solution)/shard_map/ppermute | solution.py:36
  30.6 12.2 %collective-permute-start.5 = (f32[14,16,384]{2,1,0:T(8,128)S(1)}, f32[14,16,384]{2,1,0:T(8,128)S(1)}, u32[]{:S(2)}, u32[]{:S(2)}) collective-permute-start(f32[14,16,384]{2,1,0:T(8,128)S(1)} %get-tuple-element.72), channel_id=1, source_target_pairs={{0,15},{1,0},{2,1},{3,2},{4,3},{5,4},{6,5},{7,6},{8,7},{9,8},{10,9... | collective-permute-start | bytes 1032200 | tf_op jit(solution)/shard_map/ppermute | solution.py:36
  37.0 33.1 %collective-permute-start.6 = (f32[8,16640]{1,0:T(8,128)S(1)}, f32[8,16640]{1,0:T(8,128)S(1)}, u32[]{:S(2)}, u32[]{:S(2)}) collective-permute-start(f32[8,16640]{1,0:T(8,128)S(1)} %get-tuple-element.87), channel_id=1, source_target_pairs={{0,16},{16,32},{32,48},{48,64},{64,80},{80,96},{96,112},{112,128},... | collective-permute-start | bytes 1597448 | tf_op jit(solution)/shard_map/ppermute | solution.py:36
  37.2 32.9 %collective-permute-start.7 = (f32[8,16640]{1,0:T(8,128)S(1)}, f32[8,16640]{1,0:T(8,128)S(1)}, u32[]{:S(2)}, u32[]{:S(2)}) collective-permute-start(f32[8,16640]{1,0:T(8,128)S(1)} %get-tuple-element.88), channel_id=1, source_target_pairs={{0,240},{16,0},{32,16},{48,32},{64,48},{80,64},{96,80},{112,96},{1... | collective-permute-start | bytes 1597448 | tf_op jit(solution)/shard_map/ppermute | solution.py:36
  42.6 0.7 copy-start.4
  43.3 26.6 %copy-start.6 = (s32[1,1,16]{2,1,0:T(1,128)S(1)}, s32[1,1,16]{2,1,0:T(1,128)}, u32[]{:S(2)}) copy-start(s32[1,1,16]{2,1,0:T(1,128)} %param.15) | copy-start | bytes 196
  64.7 22.0 %collective-permute-start.8 = (f32[7,8,2560]{2,1,0:T(8,128)S(1)}, f32[7,8,2560]{2,1,0:T(8,128)S(1)}, u32[]{:S(2)}, u32[]{:S(2)}) collective-permute-start(f32[7,8,2560]{2,1,0:T(8,128)S(1)} %get-tuple-element.98), channel_id=1, source_target_pairs={{0,16},{16,32},{32,48},{48,64},{64,80},{80,96},{96,112},{112,128},... | collective-permute-start | bytes 1720328 | tf_op jit(solution)/shard_map/ppermute | solution.py:36
  64.8 21.9 %collective-permute-start.9 = (f32[7,8,2560]{2,1,0:T(8,128)S(1)}, f32[7,8,2560]{2,1,0:T(8,128)S(1)}, u32[]{:S(2)}, u32[]{:S(2)}) collective-permute-start(f32[7,8,2560]{2,1,0:T(8,128)S(1)} %get-tuple-element.99), channel_id=1, source_target_pairs={{0,240},{16,0},{32,16},{48,32},{64,48},{80,64},{96,80},{112,96},{1... | collective-permute-start | bytes 1720328 | tf_op jit(solution)/shard_map/ppermute | solution.py:36
  86.7 38.2 %copy-start.3 = (f32[128,128]{1,0:T(8,128)S(1)}, f32[128,128]{1,0:T(8,128)}, u32[]{:S(2)}) copy-start(f32[128,128]{1,0:T(8,128)} %filter_matrix.1) | copy-start | bytes 196612

commit v6 on v4

--- a/solution.py
+++ b/solution.py
@@ -487,11 +487,11 @@
     y_corner = (NARR, 2 * NEAR, edge)
     made = pltpu.VMEM((NEAR, length), jnp.float32)
     corner_left, corner_right = call(pack_corner, (y_corner, y_corner), 2, 2)(edge_b, edge_a)
-    corner_left, corner_right, mid_prev, mid_next = lax.optimization_barrier(
-        (corner_left, corner_right, mid_prev, mid_next)
-    )
     corner_l = shifted(corner_right, "gy", 1)
     corner_r = shifted(corner_left, "gy", -1)
+    corner_l, corner_r, left, right, mid_prev, mid_next = lax.optimization_barrier(
+        (corner_l, corner_r, left, right, mid_prev, mid_next)
+    )
     mid_b = shifted(mid_next, "gx", 1)
     mid_a = shifted(mid_prev, "gx", -1)
 
@@ -512,12 +512,9 @@
     state = call(run_inside, held, 7, 15, in_specs=[smem] + [vmem] * 6, scratch_shapes=[tags])(
         waves, *own, left, right
     )
-    far_prev, far_next, corner_l, corner_r = lax.optimization_barrier(
-        (far_prev, far_next, corner_l, corner_r)
-    )
+    far_prev, far_next, state = lax.optimization_barrier((far_prev, far_next, state))
     far_b = shifted(far_next, "gx", 1)
     far_a = shifted(far_prev, "gx", -1)
-    state, mid_b, mid_a = lax.optimization_barrier((state, mid_b, mid_a))
 
     count = ROWS // BROWS
     owner = block_owner[0, 0, :, 0]

time: 135 us -> 119 us (0.88)
  blocking collectives: 39.3 us -> 11.3 us
  waiting for transfers between devices: 14.8 us -> 26.2 us
    all_to_all x1, blocking collectives: 39.3 us -> 11.3 us  [per_device(): lax.all_to_all(packed.reshape(owners, 3, LANES), 'gy', split_axis=0, conc...]
    ppermute x10, waiting for transfers between devices: 14.8 us -> 26.2 us  [shifted(): lax.ppermute(array, axis, [(i, (i + by) % count) for i in range(count)])]
  transfers between devices with their start and end apart: 10 -> 10, of which waited for: 4 -> 6; matrix products, arithmetic and copies ran while one was open for 0% -> 0% of each run, Pallas kernels for 30% -> 34%
where the time goes in v6:
time: 119 us
  Pallas kernels  54.3 us (46%)
  waiting for transfers between devices  26.2 us (22%)
  starting transfers between devices  25.4 us (21%)
  blocking collectives  11.3 us (9%)
    ppermute x10, waiting for transfers between devices, shifted(): lax.ppermute(array, axis, [(i, (i + by) % count) for i in range(count)])  26.2 us
    ppermute x10, starting transfers between devices, shifted(): lax.ppermute(array, axis, [(i, (i + by) % count) for i in range(count)])  25.4 us
    pallas_call x1, Pallas kernels, per_device(): call(run_inside, held, 7, 15, in_specs=[smem] + [vmem] * 6, scratch_shape...  21.5 us
    pallas_call x1, Pallas kernels, per_device(): call(run_near, (field, field) + held, 12, 12, in_specs=[smem] + [vmem] *...  16.5 us
    all_to_all x1, blocking collectives, per_device(): lax.all_to_all(packed.reshape(owners, 3, LANES), 'gy', split_axis=0, conc...  11.3 us
    pallas_call x1, Pallas kernels, per_device(): call(run_far, (field, field, (3 * owners, LANES)) + held, 12, 8, in_specs...  10.4 us
  transfers between devices with their start and end apart: 10, of which 6 were waited for; matrix products, arithmetic and copies ran while one was open for 0% of the time, Pallas kernels for 34%

profile of v6, /device:TPU:1, one launch (start us, length us, event | category | flops | bytes accessed | tf_op | source)
XLA Modules:
  0.0 118.8 jit_solution(9477261890663150145)
XLA Ops:
  0.6 2.2 %pack_near.1 = (f32[8,10240]{1,0:T(8,128)S(1)}, f32[8,10240]{1,0:T(8,128)S(1)}, f32[8,16640]{1,0:T(8,128)S(1)}, f32[8,16640]{1,0:T(8,128)S(1)}) custom-call(f32[2,3,32,2048]{3,2,1,0:T(8,128)} %e.6, f32[2,3,32,2048]{3,2,1,0:T(8,128)} %h.6, f32[32,2048]{1,0:T(8,128)} %eps.6, f32[2,32,64]{2,1,0:T(8,128)} %profile.2, s32[2,32]{1,0:T(2,128)} %plane.2), custom_call_target="tpu_custom_call" | custom-call | bytes 6000000 | tf_op jit(solution)/shard_map/pack_near/pallas_call | solution.py:470
  2.8 0.0 copy-start.5
  2.8 0.0 copy-start
  2.8 0.0 copy-start.1
  2.8 0.0 copy-start.2
  2.8 3.7 %collective-permute-start = (f32[8,10240]{1,0:T(8,128)S(1)}, f32[8,10240]{1,0:T(8,128)S(1)}, u32[]{:S(2)}, u32[]{:S(2)}) collective-permute-start(f32[8,10240]{1,0:T(8,128)S(1)} %get-tuple-element.65), channel_id=1, source_target_pairs={{0,16},{16,32},{32,48},{48,64},{64,80},{80,96},{96,112},{112,128},... | collective-permute-start | bytes 983048 | tf_op jit(solution)/shard_map/ppermute | solution.py:36
  6.5 5.4 %collective-permute-start.1 = (f32[8,10240]{1,0:T(8,128)S(1)}, f32[8,10240]{1,0:T(8,128)S(1)}, u32[]{:S(2)}, u32[]{:S(2)}) collective-permute-start(f32[8,10240]{1,0:T(8,128)S(1)} %get-tuple-element.66), channel_id=1, source_target_pairs={{0,240},{16,0},{32,16},{48,32},{64,48},{80,64},{96,80},{112,96},{1... | collective-permute-start | bytes 983048 | tf_op jit(solution)/shard_map/ppermute | solution.py:36
  11.9 1.8 %pack_side.1 = (f32[14,32,384]{2,1,0:T(8,128)S(1)}, f32[14,32,384]{2,1,0:T(8,128)S(1)}, f32[32,2048]{1,0:T(8,128)S(1)}) custom-call(f32[2,3,32,2048]{3,2,1,0:T(8,128)} %e.6, f32[2,3,32,2048]{3,2,1,0:T(8,128)} %h.6, f32[32,2048]{1,0:T(8,128)} %eps.6, f32[2,32,64]{2,1,0:T(8,128)} %profile.2, s32[2,32]{1,0:T(2,128)} %plane.2), custom_call_target="tpu_custom_call" | custom-call | bytes 9000000 | tf_op jit(solution)/shard_map/pack_side/pallas_call | solution.py:478
  13.7 6.2 %collective-permute-done.behind.edge_b = f32[8,10240]{1,0:T(8,128)S(1)} collective-permute-done((f32[8,10240]{1,0:T(8,128)S(1)}, f32[8,10240]{1,0:T(8,128)S(1)}, u32[]{:S(2)}, u32[]{:S(2)}) %collective-permute-start) | collective-permute-done | bytes 327712 | tf_op jit(solution)/shard_map/ppermute | solution.py:36
  19.9 3.4 %collective-permute-done.1.ahead.edge_a = f32[8,10240]{1,0:T(8,128)S(1)} collective-permute-done((f32[8,10240]{1,0:T(8,128)S(1)}, f32[8,10240]{1,0:T(8,128)S(1)}, u32[]{:S(2)}, u32[]{:S(2)}) %collective-permute-start.1) | collective-permute-done | bytes 327712 | tf_op jit(solution)/shard_map/ppermute | solution.py:36
  23.3 3.0 %collective-permute-start.4 = (f32[14,32,384]{2,1,0:T(8,128)S(1)}, f32[14,32,384]{2,1,0:T(8,128)S(1)}, u32[]{:S(2)}, u32[]{:S(2)}) collective-permute-start(f32[14,32,384]{2,1,0:T(8,128)S(1)} %get-tuple-element.73), channel_id=1, source_target_pairs={{0,1},{1,2},{2,3},{3,4},{4,5},{5,6},{6,7},{7,8},{8,9},{9,10},{10,1... | collective-permute-start | bytes 2064392 | tf_op jit(solution)/shard_map/ppermute | solution.py:36
  26.3 0.0 collective-permute-start.5
  26.3 0.5 pack_corner.1
  26.8 1.8 %collective-permute-start.2 = (f32[14,16,384]{2,1,0:T(8,128)S(1)}, f32[14,16,384]{2,1,0:T(8,128)S(1)}, u32[]{:S(2)}, u32[]{:S(2)}) collective-permute-start(f32[14,16,384]{2,1,0:T(8,128)S(1)} %get-tuple-element.71), channel_id=1, source_target_pairs={{0,1},{1,2},{2,3},{3,4},{4,5},{5,6},{6,7},{7,8},{8,9},{9,10},{10,1... | collective-permute-start | bytes 1032200 | tf_op jit(solution)/shard_map/ppermute | solution.py:36
  28.6 1.0 collective-permute-start.3
  29.6 0.0 copy-done.5
  29.6 0.2 convert_reduce_fusion
  29.8 8.1 %collective-permute-done.2.corner_l = f32[14,16,384]{2,1,0:T(8,128)S(1)} collective-permute-done((f32[14,16,384]{2,1,0:T(8,128)S(1)}, f32[14,16,384]{2,1,0:T(8,128)S(1)}, u32[]{:S(2)}, u32[]{:S(2)}) %collective-permute-start.2) | collective-permute-done | bytes 344096 | tf_op jit(solution)/shard_map/ppermute | solution.py:36
  37.9 2.8 %collective-permute-done.3.corner_r = f32[14,16,384]{2,1,0:T(8,128)S(1)} collective-permute-done((f32[14,16,384]{2,1,0:T(8,128)S(1)}, f32[14,16,384]{2,1,0:T(8,128)S(1)}, u32[]{:S(2)}, u32[]{:S(2)}) %collective-permute-start.3) | collective-permute-done | bytes 344096 | tf_op jit(solution)/shard_map/ppermute | solution.py:36
  40.7 0.0 collective-permute-done.4.left
  40.7 0.0 collective-permute-done.5.right
  40.7 0.0 collective-permute-start.6
  40.7 5.4 %collective-permute-start.7 = (f32[8,16640]{1,0:T(8,128)S(1)}, f32[8,16640]{1,0:T(8,128)S(1)}, u32[]{:S(2)}, u32[]{:S(2)}) collective-permute-start(f32[8,16640]{1,0:T(8,128)S(1)} %get-tuple-element.96), channel_id=1, source_target_pairs={{0,240},{16,0},{32,16},{48,32},{64,48},{80,64},{96,80},{112,96},{1... | collective-permute-start | bytes 1597448 | tf_op jit(solution)/shard_map/ppermute | solution.py:36
  46.1 0.0 copy-done
  46.1 0.0 copy-done.1
  46.1 0.0 copy-done.2
  46.1 0.0 copy-start.4
  46.1 0.2 pack_far.1
  46.3 0.4 copy-done.4
  46.7 0.0 copy-start.6
  46.7 21.5 %run_inside.1 = (f32[8096,128]{1,0:T(8,128)S(1)}, f32[8096,128]{1,0:T(8,128)S(1)}, f32[1376,128]{1,0:T(8,128)S(1)}, f32[2720,128]{1,0:T(8,128)S(1)}, f32[1376,128]{1,0:T(8,128)S(1)}) custom-call(f32[12]{0:T(128)S(1)} %copy-done.4, f32[2,3,32,2048]{3,2,1,0:T(8,128)S(1)} %copy-done, f32[2,3,32,2048]{3,2,1,0:T(8,128)S(1)} %copy-done.1, ...), custom_call_target="tpu_custom_call" | custom-call | bytes 45000000 | tf_op jit(solution)/shard_map/run_inside/pallas_call | solution.py:512
  68.2 0.1 collective-permute-start.8
  68.3 5.1 %collective-permute-start.9 = (f32[7,8,2560]{2,1,0:T(8,128)S(1)}, f32[7,8,2560]{2,1,0:T(8,128)S(1)}, u32[]{:S(2)}, u32[]{:S(2)}) collective-permute-start(f32[7,8,2560]{2,1,0:T(8,128)S(1)} %get-tuple-element.107), channel_id=1, source_target_pairs={{0,240},{16,0},{32,16},{48,32},{64,48},{80,64},{96,80},{112,96},{1... | collective-permute-start | bytes 1720328 | tf_op jit(solution)/shard_map/ppermute | solution.py:36
  73.3 0.0 copy-done.6
  73.4 0.2 fusion.1.marks
  73.6 0.0 collective-permute-done.6.mid_b
  73.6 0.0 collective-permute-done.7.mid_a
  73.6 16.5 %run_near.1 = (f32[2,3,32,2048]{3,2,1,0:T(8,128)}, f32[2,3,32,2048]{3,2,1,0:T(8,128)}, f32[8096,128]{1,0:T(8,128)S(1)}, f32[8096,128]{1,0:T(8,128)S(1)}, f32[137...) custom-call(f32[12]{0:T(128)S(1)} %copy-done.4, ...), custom_call_target="tpu_custom_call", output_to_operand_aliasing={{2}: (1, {}), {3}: (2, {}), {4}: (3, {}), {5}: (4, {}), {6}... | custom-call | bytes 36000000 | tf_op jit(solution)/shard_map/run_near/pallas_call | solution.py:539
  90.1 2.0 %collective-permute-done.8.far_b = f32[7,8,2560]{2,1,0:T(8,128)S(1)} collective-permute-done((f32[7,8,2560]{2,1,0:T(8,128)S(1)}, f32[7,8,2560]{2,1,0:T(8,128)S(1)}, u32[]{:S(2)}, u32[]{:S(2)}) %collective-permute-start.8) | collective-permute-done | bytes 573472 | tf_op jit(solution)/shard_map/ppermute | solution.py:36
  92.2 3.6 %collective-permute-done.9.far_a = f32[7,8,2560]{2,1,0:T(8,128)S(1)} collective-permute-done((f32[7,8,2560]{2,1,0:T(8,128)S(1)}, f32[7,8,2560]{2,1,0:T(8,128)S(1)}, u32[]{:S(2)}, u32[]{:S(2)}) %collective-permute-start.9) | collective-permute-done | bytes 573472 | tf_op jit(solution)/shard_map/ppermute | solution.py:36
  95.8 0.0 copy-start.3
  95.8 10.4 %run_far.1 = (f32[2,3,32,2048]{3,2,1,0:T(8,128)}, f32[2,3,32,2048]{3,2,1,0:T(8,128)}, f32[48,128]{1,0:T(8,128)S(1)}, f32[8096,128]{1,0:T(8,128)S(1)}, f32[8096,1...) custom-call(f32[12]{0:T(128)S(1)} %copy-done.4, ...), custom_call_target="tpu_custom_call", output_to_operand_aliasing={{0}: (6, {}), {1}: (7, {}), {3}: (1, {}), {4}: (2, {}), {5}... | custom-call | bytes 24000000 | tf_op jit(solution)/shard_map/run_far/pallas_call | solution.py:550
  106.2 11.3 %all_to_all.5 = f32[16,3,128]{2,1,0:T(4,128)S(1)} all-to-all(f32[16,3,128]{2,1,0:T(4,128)S(1)} %reshape.36), channel_id=1, replica_groups=mesh['gx'=16,'gy'=16] {'gy'}, dimensions={0} | all-to-all | bytes 49152 | tf_op jit(solution)/shard_map/all_to_all | solution.py:561
  117.6 0.0 copy-done.3
  117.6 1.2 %collect.1 = f32[4,128]{1,0:T(4,128)} custom-call(f32[48,128]{1,0:T(8,128)S(1)} %reshape.37.received, f32[128,128]{1,0:T(8,128)S(1)} %copy-done.3), custom_call_target="tpu_custom_call" | custom-call | bytes 3000000 | tf_op jit(solution)/shard_map/collect/pallas_call | solution.py:564
  (5 shorter events, 0.0 us)
Async XLA Ops:
  2.8 26.8 %copy-start.5 = (s32[1,1,16,1]{2,3,1,0:T(1,128)S(1)}, s32[1,1,16,1]{2,3,1,0:T(1,128)}, u32[]{:S(2)}) copy-start(s32[1,1,16,1]{2,3,1,0:T(1,128)} %param.14) | copy-start | bytes 196
  2.8 43.3 %copy-start = (f32[2,3,32,2048]{3,2,1,0:T(8,128)S(1)}, f32[2,3,32,2048]{3,2,1,0:T(8,128)}, u32[]{:S(2)}) copy-start(f32[2,3,32,2048]{3,2,1,0:T(8,128)} %e.6) | copy-start | bytes 4718596
  2.8 43.2 %copy-start.1 = (f32[2,3,32,2048]{3,2,1,0:T(8,128)S(1)}, f32[2,3,32,2048]{3,2,1,0:T(8,128)}, u32[]{:S(2)}) copy-start(f32[2,3,32,2048]{3,2,1,0:T(8,128)} %h.6) | copy-start | bytes 4718596
  2.8 43.2 %copy-start.2 = (f32[32,2048]{1,0:T(8,128)S(1)}, f32[32,2048]{1,0:T(8,128)}, u32[]{:S(2)}) copy-start(f32[32,2048]{1,0:T(8,128)} %eps.6) | copy-start | bytes 786436
  2.8 17.1 %collective-permute-start = (f32[8,10240]{1,0:T(8,128)S(1)}, f32[8,10240]{1,0:T(8,128)S(1)}, u32[]{:S(2)}, u32[]{:S(2)}) collective-permute-start(f32[8,10240]{1,0:T(8,128)S(1)} %get-tuple-element.65), channel_id=1, source_target_pairs={{0,16},{16,32},{32,48},{48,64},{64,80},{80,96},{96,112},{112,128},... | collective-permute-start | bytes 983048 | tf_op jit(solution)/shard_map/ppermute | solution.py:36
  6.5 16.8 %collective-permute-start.1 = (f32[8,10240]{1,0:T(8,128)S(1)}, f32[8,10240]{1,0:T(8,128)S(1)}, u32[]{:S(2)}, u32[]{:S(2)}) collective-permute-start(f32[8,10240]{1,0:T(8,128)S(1)} %get-tuple-element.66), channel_id=1, source_target_pairs={{0,240},{16,0},{32,16},{48,32},{64,48},{80,64},{96,80},{112,96},{1... | collective-permute-start | bytes 983048 | tf_op jit(solution)/shard_map/ppermute | solution.py:36
  23.3 17.4 %collective-permute-start.4 = (f32[14,32,384]{2,1,0:T(8,128)S(1)}, f32[14,32,384]{2,1,0:T(8,128)S(1)}, u32[]{:S(2)}, u32[]{:S(2)}) collective-permute-start(f32[14,32,384]{2,1,0:T(8,128)S(1)} %get-tuple-element.73), channel_id=1, source_target_pairs={{0,1},{1,2},{2,3},{3,4},{4,5},{5,6},{6,7},{7,8},{8,9},{9,10},{10,1... | collective-permute-start | bytes 2064392 | tf_op jit(solution)/shard_map/ppermute | solution.py:36
  26.3 14.3 %collective-permute-start.5 = (f32[14,32,384]{2,1,0:T(8,128)S(1)}, f32[14,32,384]{2,1,0:T(8,128)S(1)}, u32[]{:S(2)}, u32[]{:S(2)}) collective-permute-start(f32[14,32,384]{2,1,0:T(8,128)S(1)} %get-tuple-element.74), channel_id=1, source_target_pairs={{0,15},{1,0},{2,1},{3,2},{4,3},{5,4},{6,5},{7,6},{8,7},{9,8},{10,9... | collective-permute-start | bytes 2064392 | tf_op jit(solution)/shard_map/ppermute | solution.py:36
  26.8 11.1 %collective-permute-start.2 = (f32[14,16,384]{2,1,0:T(8,128)S(1)}, f32[14,16,384]{2,1,0:T(8,128)S(1)}, u32[]{:S(2)}, u32[]{:S(2)}) collective-permute-start(f32[14,16,384]{2,1,0:T(8,128)S(1)} %get-tuple-element.71), channel_id=1, source_target_pairs={{0,1},{1,2},{2,3},{3,4},{4,5},{5,6},{6,7},{7,8},{8,9},{9,10},{10,1... | collective-permute-start | bytes 1032200 | tf_op jit(solution)/shard_map/ppermute | solution.py:36
  28.6 12.1 %collective-permute-start.3 = (f32[14,16,384]{2,1,0:T(8,128)S(1)}, f32[14,16,384]{2,1,0:T(8,128)S(1)}, u32[]{:S(2)}, u32[]{:S(2)}) collective-permute-start(f32[14,16,384]{2,1,0:T(8,128)S(1)} %get-tuple-element.72), channel_id=1, source_target_pairs={{0,15},{1,0},{2,1},{3,2},{4,3},{5,4},{6,5},{7,6},{8,7},{9,8},{10,9... | collective-permute-start | bytes 1032200 | tf_op jit(solution)/shard_map/ppermute | solution.py:36
  40.7 32.9 %collective-permute-start.6 = (f32[8,16640]{1,0:T(8,128)S(1)}, f32[8,16640]{1,0:T(8,128)S(1)}, u32[]{:S(2)}, u32[]{:S(2)}) collective-permute-start(f32[8,16640]{1,0:T(8,128)S(1)} %get-tuple-element.95), channel_id=1, source_target_pairs={{0,16},{16,32},{32,48},{48,64},{64,80},{80,96},{96,112},{112,128},... | collective-permute-start | bytes 1597448 | tf_op jit(solution)/shard_map/ppermute | solution.py:36
  40.7 32.9 %collective-permute-start.7 = (f32[8,16640]{1,0:T(8,128)S(1)}, f32[8,16640]{1,0:T(8,128)S(1)}, u32[]{:S(2)}, u32[]{:S(2)}) collective-permute-start(f32[8,16640]{1,0:T(8,128)S(1)} %get-tuple-element.96), channel_id=1, source_target_pairs={{0,240},{16,0},{32,16},{48,32},{64,48},{80,64},{96,80},{112,96},{1... | collective-permute-start | bytes 1597448 | tf_op jit(solution)/shard_map/ppermute | solution.py:36
  46.1 0.7 copy-start.4
  46.7 26.6 %copy-start.6 = (s32[1,1,16]{2,1,0:T(1,128)S(1)}, s32[1,1,16]{2,1,0:T(1,128)}, u32[]{:S(2)}) copy-start(s32[1,1,16]{2,1,0:T(1,128)} %param.15) | copy-start | bytes 196
  68.2 24.0 %collective-permute-start.8 = (f32[7,8,2560]{2,1,0:T(8,128)S(1)}, f32[7,8,2560]{2,1,0:T(8,128)S(1)}, u32[]{:S(2)}, u32[]{:S(2)}) collective-permute-start(f32[7,8,2560]{2,1,0:T(8,128)S(1)} %get-tuple-element.106), channel_id=1, source_target_pairs={{0,16},{16,32},{32,48},{48,64},{64,80},{80,96},{96,112},{112,128},... | collective-permute-start | bytes 1720328 | tf_op jit(solution)/shard_map/ppermute | solution.py:36
  68.3 27.5 %collective-permute-start.9 = (f32[7,8,2560]{2,1,0:T(8,128)S(1)}, f32[7,8,2560]{2,1,0:T(8,128)S(1)}, u32[]{:S(2)}, u32[]{:S(2)}) collective-permute-start(f32[7,8,2560]{2,1,0:T(8,128)S(1)} %get-tuple-element.107), channel_id=1, source_target_pairs={{0,240},{16,0},{32,16},{48,32},{64,48},{80,64},{96,80},{112,96},{1... | collective-permute-start | bytes 1720328 | tf_op jit(solution)/shard_map/ppermute | solution.py:36
  95.8 21.8 %copy-start.3 = (f32[128,128]{1,0:T(8,128)S(1)}, f32[128,128]{1,0:T(8,128)}, u32[]{:S(2)}) copy-start(f32[128,128]{1,0:T(8,128)} %filter_matrix.1) | copy-start | bytes 196612

commit v7 on v6

--- a/solution.py
+++ b/solution.py
@@ -189,16 +189,20 @@
     ref[pl.ds(pl.multiple_of(at(a, x), 8), YV), :] = value
 
 
-def fill_sources(wa, ws, x, count):
-    size = count * YV
-    level = iota((size, LANES), 1) % NZ
-    held = wa[pl.ds(at(0, x), size), :]
+def fill_sources(wa, ws, spans):
+    held = jnp.concatenate([wa[pl.ds(at(0, x), n * YV), :] for x, n in spans], axis=0)
+    level = iota(held.shape, 1) % NZ
     held = jnp.where(level < 4, held, 0.0)
-    i, j = iota((LANES, LANES), 0), iota((LANES, LANES), 1)
+    i, j = iota((LANES, 4 * LANES), 0), iota((LANES, 4 * LANES), 1)
+    spread = dot(held, (i == (j % LANES) // NZ * NZ + j // LANES).astype(jnp.float32))
     for r in range(2):
-        strength = dot(held, (i == (j // NZ) * NZ + r).astype(jnp.float32))
-        where = dot(held, (i == (j // NZ) * NZ + 2 + r).astype(jnp.float32))
-        ws[pl.ds(at(r, x), size), :] = jnp.where(level.astype(jnp.float32) == where, strength, 0.0)
+        strength = spread[:, r * LANES : (r + 1) * LANES]
+        where = spread[:, (2 + r) * LANES : (3 + r) * LANES]
+        term = jnp.where(level.astype(jnp.float32) == where, strength, 0.0)
+        begin = 0
+        for x, n in spans:
+            ws[pl.ds(at(r, x), n * YV), :] = term[begin : begin + n * YV]
+            begin += n * YV
 
 
 def kinds(we, wh, wc, wa):
@@ -282,7 +286,7 @@
 
         lax.fori_loop(0, STEPS, step, 0)
 
-    def inside(self, low, high):
+    def inside(self, low, high, begin, end):
         def sweep(one, x, count):
             def group(g, _):
                 for i in range(8):
@@ -291,12 +295,12 @@
 
             lax.fori_loop(0, count // 8, group, 0)
             for size in (4, 2, 1):
-                begin = x + count // (2 * size) * (2 * size)
+                start = x + count // (2 * size) * (2 * size)
 
                 @pl.when(count % (2 * size) >= size)
-                def _(size=size, begin=begin):
+                def _(size=size, start=start):
                     for i in range(size):
-                        one(begin + i)
+                        one(start + i)
 
         def step(n, _):
             wave = self.waves[n]
@@ -304,7 +308,7 @@
             sweep(lambda x: self.electric(x, wave), low + 1 + n, high - low - 1 - 2 * n)
             return 0
 
-        lax.fori_loop(0, STEPS, step, 0)
+        lax.fori_loop(begin, end, step, 0)
 
 
 def run_inside(waves, e, h, eps, aux, left, right, we, wh, wc, ws, acc, wa):
@@ -318,9 +322,13 @@
                 cols = pl.ds(j * LANES, LANES)
                 place(dst, a, HALO + 8 * i, j, fix(left[n, rows, cols]))
                 place(dst, a, HALO + 8 * i, HT + TILES + j, fix(right[n, rows, cols]))
-    fill_sources(wa, ws, HALO, ROWS)
+    fill_sources(wa, ws, ((HALO, ROWS),))
     acc[...] = jnp.zeros_like(acc)
-    Stepper(waves, we, wh, wc, ws, acc).inside(HALO, HALO + ROWS - 1)
+    Stepper(waves, we, wh, wc, ws, acc).inside(HALO, HALO + ROWS - 1, 0, STEPS // 2)
+
+
+def run_inside_rest(waves, _e, _h, _c, _s, _t, we, wh, wc, ws, acc):
+    Stepper(waves, we, wh, wc, ws, acc).inside(HALO, HALO + ROWS - 1, STEPS // 2, STEPS)
 
 
 def store_rows(we, wh, stage, e_out, h_out, sems, x, count):
@@ -364,7 +372,7 @@
                 cols = pl.ds(j * LANES, LANES)
                 place(dst, a, x, j, fix(corner_l[n, rows, cols]))
                 place(dst, a, x, HT + TILES + j, fix(corner_r[n, rows, cols]))
-        fill_sources(wa, ws, x, NEAR)
+    fill_sources(wa, ws, ((FAR, NEAR), (HALO + ROWS, NEAR)))
     Stepper(waves, we, wh, wc, ws, acc).edges(FAR, HALO + ROWS - 1, NEAR)
     for copy in store_rows(we, wh, stage, e_out, h_out, sems, 8, 16):
         copy.wait()
@@ -379,12 +387,12 @@
             cols = pl.ds(j * LANES, LANES)
             place(dst, a, 0, HT - 1 + j, fix(far_b[n // 2, q, cols]))
             place(dst, a, XR - FAR, j, fix(far_a[n // 2, q, cols]))
-    fill_sources(wa, ws, 0, FAR)
-    fill_sources(wa, ws, XR - FAR, FAR)
+    fill_sources(wa, ws, ((0, FAR), (XR - FAR, FAR)))
     Stepper(waves, we, wh, wc, ws, acc).edges(0, XR - FAR - 1, FAR)
 
     stores = store_rows(we, wh, stage_lo, e_out, h_out, sems, 0, 8)
     stores += store_rows(we, wh, stage_hi, e_out, h_out, sems.at[pl.ds(12, 12)], 24, 8)
+
     i, j = iota((LANES, LANES), 0), iota((LANES, LANES), 1)
     sums = dot(acc[pl.ds(at(0, HALO), ROWS * YV), :], (i // NZ == j % 4).astype(jnp.float32))
     per = BROWS * YV
@@ -509,12 +517,21 @@
     tail = PAD + YV
     held = tuple((k * many + tail, LANES) for k in (6, 6, 1, 2, 1))
     tags = pltpu.VMEM((many + tail, LANES), jnp.float32)
-    state = call(run_inside, held, 7, 15, in_specs=[smem] + [vmem] * 6, scratch_shapes=[tags])(
+    state = call(run_inside, held, 7, 30, in_specs=[smem] + [vmem] * 6, scratch_shapes=[tags])(
         waves, *own, left, right
     )
     far_prev, far_next, state = lax.optimization_barrier((far_prev, far_next, state))
     far_b = shifted(far_next, "gx", 1)
     far_a = shifted(far_prev, "gx", -1)
+    keep = {1 + k: k for k in range(5)}
+    state = call(
+        run_inside_rest,
+        held,
+        6,
+        1,
+        in_specs=[smem] + [vmem] * 5,
+        input_output_aliases=keep,
+    )(waves, *state)
 
     count = ROWS // BROWS
     owner = block_owner[0, 0, :, 0]

time: 119 us -> 120 us (level)
  blocking collectives: 11.3 us -> 16.8 us
  waiting for transfers between devices: 26.2 us -> 20.8 us
    all_to_all x1, blocking collectives: 11.3 us -> 16.8 us  [per_device(): lax.all_to_all(packed.reshape(owners, 3, LANES), 'gy', split_axis=0, conc...]
    ppermute x10, waiting for transfers between devices: 26.2 us -> 20.8 us  [shifted(): lax.ppermute(array, axis, [(i, (i + by) % count) for i in range(count)])]
    pallas_call x1 -> x2, Pallas kernels: 21.5 us -> 22 us  [the longest x1 14.7 us: per_device(): call(run_inside, held, 7, 30, in_specs=[smem] + [vmem] * 6, scratch_shape...]
  transfers between devices with their start and end apart: 10 -> 10, of which waited for: 6 -> 5; matrix products, arithmetic and copies ran while one was open for 0% -> 0% of each run, Pallas kernels for 34% -> 34%
where the time goes in v7:
time: 120 us; the launch traced here: 119 us
  Pallas kernels  54.7 us (46%)
  starting transfers between devices  25.4 us (21%)
  waiting for transfers between devices  20.8 us (17%)
  blocking collectives  16.8 us (14%)
    ppermute x10, starting transfers between devices, shifted(): lax.ppermute(array, axis, [(i, (i + by) % count) for i in range(count)])  25.4 us
    ppermute x10, waiting for transfers between devices, shifted(): lax.ppermute(array, axis, [(i, (i + by) % count) for i in range(count)])  20.8 us
    all_to_all x1, blocking collectives, per_device(): lax.all_to_all(packed.reshape(owners, 3, LANES), 'gy', split_axis=0, conc...  16.8 us
    pallas_call x1, Pallas kernels, per_device(): call(run_near, (field, field) + held, 12, 12, in_specs=[smem] + [vmem] *...  16.5 us
    pallas_call x1, Pallas kernels, per_device(): call(run_inside, held, 7, 30, in_specs=[smem] + [vmem] * 6, scratch_shape...  14.7 us
    pallas_call x1, Pallas kernels, per_device(): call(run_far, (field, field, (3 * owners, LANES)) + held, 12, 8, in_specs...  10.4 us
    pallas_call x1, Pallas kernels, per_device(): call(run_inside_rest, held, 6, 1, in_specs=[smem] + [vmem] * 5, input_out...  7.31 us
  transfers between devices with their start and end apart: 10, of which 5 were waited for; matrix products, arithmetic and copies ran while one was open for 0% of the time, Pallas kernels for 34%

profile of v7, /device:TPU:1, one launch (start us, length us, event | category | flops | bytes accessed | tf_op | source)
XLA Modules:
  0.0 119.4 jit_solution(10814212102916080888)
XLA Ops:
  0.6 2.2 %pack_near.1 = (f32[8,10240]{1,0:T(8,128)S(1)}, f32[8,10240]{1,0:T(8,128)S(1)}, f32[8,16640]{1,0:T(8,128)S(1)}, f32[8,16640]{1,0:T(8,128)S(1)}) custom-call(f32[2,3,32,2048]{3,2,1,0:T(8,128)} %e.6, f32[2,3,32,2048]{3,2,1,0:T(8,128)} %h.6, f32[32,2048]{1,0:T(8,128)} %eps.6, f32[2,32,64]{2,1,0:T(8,128)} %profile.2, s32[2,32]{1,0:T(2,128)} %plane.2), custom_call_target="tpu_custom_call" | custom-call | bytes 6000000 | tf_op jit(solution)/shard_map/pack_near/pallas_call | solution.py:478
  2.8 0.0 copy-start.5
  2.8 0.0 copy-start
  2.8 0.0 copy-start.1
  2.8 0.0 copy-start.2
  2.8 3.7 %collective-permute-start = (f32[8,10240]{1,0:T(8,128)S(1)}, f32[8,10240]{1,0:T(8,128)S(1)}, u32[]{:S(2)}, u32[]{:S(2)}) collective-permute-start(f32[8,10240]{1,0:T(8,128)S(1)} %get-tuple-element.70), channel_id=1, source_target_pairs={{0,16},{16,32},{32,48},{48,64},{64,80},{80,96},{96,112},{112,128},... | collective-permute-start | bytes 983048 | tf_op jit(solution)/shard_map/ppermute | solution.py:36
  6.5 5.4 %collective-permute-start.1 = (f32[8,10240]{1,0:T(8,128)S(1)}, f32[8,10240]{1,0:T(8,128)S(1)}, u32[]{:S(2)}, u32[]{:S(2)}) collective-permute-start(f32[8,10240]{1,0:T(8,128)S(1)} %get-tuple-element.71), channel_id=1, source_target_pairs={{0,240},{16,0},{32,16},{48,32},{64,48},{80,64},{96,80},{112,96},{1... | collective-permute-start | bytes 983048 | tf_op jit(solution)/shard_map/ppermute | solution.py:36
  11.9 1.8 %pack_side.1 = (f32[14,32,384]{2,1,0:T(8,128)S(1)}, f32[14,32,384]{2,1,0:T(8,128)S(1)}, f32[32,2048]{1,0:T(8,128)S(1)}) custom-call(f32[2,3,32,2048]{3,2,1,0:T(8,128)} %e.6, f32[2,3,32,2048]{3,2,1,0:T(8,128)} %h.6, f32[32,2048]{1,0:T(8,128)} %eps.6, f32[2,32,64]{2,1,0:T(8,128)} %profile.2, s32[2,32]{1,0:T(2,128)} %plane.2), custom_call_target="tpu_custom_call" | custom-call | bytes 9000000 | tf_op jit(solution)/shard_map/pack_side/pallas_call | solution.py:486
  13.7 6.2 %collective-permute-done.behind.edge_b = f32[8,10240]{1,0:T(8,128)S(1)} collective-permute-done((f32[8,10240]{1,0:T(8,128)S(1)}, f32[8,10240]{1,0:T(8,128)S(1)}, u32[]{:S(2)}, u32[]{:S(2)}) %collective-permute-start) | collective-permute-done | bytes 327712 | tf_op jit(solution)/shard_map/ppermute | solution.py:36
  19.9 3.4 %collective-permute-done.1.ahead.edge_a = f32[8,10240]{1,0:T(8,128)S(1)} collective-permute-done((f32[8,10240]{1,0:T(8,128)S(1)}, f32[8,10240]{1,0:T(8,128)S(1)}, u32[]{:S(2)}, u32[]{:S(2)}) %collective-permute-start.1) | collective-permute-done | bytes 327712 | tf_op jit(solution)/shard_map/ppermute | solution.py:36
  23.3 3.0 %collective-permute-start.4 = (f32[14,32,384]{2,1,0:T(8,128)S(1)}, f32[14,32,384]{2,1,0:T(8,128)S(1)}, u32[]{:S(2)}, u32[]{:S(2)}) collective-permute-start(f32[14,32,384]{2,1,0:T(8,128)S(1)} %get-tuple-element.78), channel_id=1, source_target_pairs={{0,1},{1,2},{2,3},{3,4},{4,5},{5,6},{6,7},{7,8},{8,9},{9,10},{10,1... | collective-permute-start | bytes 2064392 | tf_op jit(solution)/shard_map/ppermute | solution.py:36
  26.3 0.0 collective-permute-start.5
  26.3 0.5 pack_corner.1
  26.8 1.8 %collective-permute-start.2 = (f32[14,16,384]{2,1,0:T(8,128)S(1)}, f32[14,16,384]{2,1,0:T(8,128)S(1)}, u32[]{:S(2)}, u32[]{:S(2)}) collective-permute-start(f32[14,16,384]{2,1,0:T(8,128)S(1)} %get-tuple-element.76), channel_id=1, source_target_pairs={{0,1},{1,2},{2,3},{3,4},{4,5},{5,6},{6,7},{7,8},{8,9},{9,10},{10,1... | collective-permute-start | bytes 1032200 | tf_op jit(solution)/shard_map/ppermute | solution.py:36
  28.6 1.0 collective-permute-start.3
  29.6 0.0 copy-done.5
  29.6 0.2 convert_reduce_fusion
  29.8 8.1 %collective-permute-done.2.corner_l = f32[14,16,384]{2,1,0:T(8,128)S(1)} collective-permute-done((f32[14,16,384]{2,1,0:T(8,128)S(1)}, f32[14,16,384]{2,1,0:T(8,128)S(1)}, u32[]{:S(2)}, u32[]{:S(2)}) %collective-permute-start.2) | collective-permute-done | bytes 344096 | tf_op jit(solution)/shard_map/ppermute | solution.py:36
  37.9 2.8 %collective-permute-done.3.corner_r = f32[14,16,384]{2,1,0:T(8,128)S(1)} collective-permute-done((f32[14,16,384]{2,1,0:T(8,128)S(1)}, f32[14,16,384]{2,1,0:T(8,128)S(1)}, u32[]{:S(2)}, u32[]{:S(2)}) %collective-permute-start.3) | collective-permute-done | bytes 344096 | tf_op jit(solution)/shard_map/ppermute | solution.py:36
  40.7 0.0 collective-permute-done.4.left
  40.7 0.0 collective-permute-done.5.right
  40.7 0.0 collective-permute-start.6
  40.7 5.4 %collective-permute-start.7 = (f32[8,16640]{1,0:T(8,128)S(1)}, f32[8,16640]{1,0:T(8,128)S(1)}, u32[]{:S(2)}, u32[]{:S(2)}) collective-permute-start(f32[8,16640]{1,0:T(8,128)S(1)} %get-tuple-element.106), channel_id=1, source_target_pairs={{0,240},{16,0},{32,16},{48,32},{64,48},{80,64},{96,80},{112,96},{1... | collective-permute-start | bytes 1597448 | tf_op jit(solution)/shard_map/ppermute | solution.py:36
  46.1 0.0 copy-done
  46.1 0.0 copy-done.1
  46.1 0.0 copy-done.2
  46.1 0.0 copy-start.4
  46.1 0.2 pack_far.1
  46.3 0.4 copy-done.4
  46.7 0.0 copy-start.6
  46.7 14.7 %run_inside.1 = (f32[8096,128]{1,0:T(8,128)S(1)}, f32[8096,128]{1,0:T(8,128)S(1)}, f32[1376,128]{1,0:T(8,128)S(1)}, f32[2720,128]{1,0:T(8,128)S(1)}, f32[1376,128]{1,0:T(8,128)S(1)}) custom-call(f32[12]{0:T(128)S(1)} %copy-done.4, f32[2,3,32,2048]{3,2,1,0:T(8,128)S(1)} %copy-done, f32[2,3,32,2048]{3,2,1,0:T(8,128)S(1)} %copy-done.1, ...), custom_call_target="tpu_custom_call" | custom-call | bytes 90000000 | tf_op jit(solution)/shard_map/run_inside/pallas_call | solution.py:520
  61.4 0.1 collective-permute-start.8
  61.5 5.1 %collective-permute-start.9 = (f32[7,8,2560]{2,1,0:T(8,128)S(1)}, f32[7,8,2560]{2,1,0:T(8,128)S(1)}, u32[]{:S(2)}, u32[]{:S(2)}) collective-permute-start(f32[7,8,2560]{2,1,0:T(8,128)S(1)} %get-tuple-element.117), channel_id=1, source_target_pairs={{0,240},{16,0},{32,16},{48,32},{64,48},{80,64},{96,80},{112,96},{1... | collective-permute-start | bytes 1720328 | tf_op jit(solution)/shard_map/ppermute | solution.py:36
  66.6 0.0 copy-done.6
  66.6 0.2 fusion.1.marks
  66.8 7.3 %run_inside_rest.1 = (f32[8096,128]{1,0:T(8,128)S(1)}, f32[8096,128]{1,0:T(8,128)S(1)}, f32[1376,128]{1,0:T(8,128)S(1)}, f32[2720,128]{1,0:T(8,128)S(1)}, f32[1376,128]{1,0:T(8,128)S(1)}) custom-call(f32[12]{0:T(128)S(1)} %copy-done.4, ...), custom_call_target="tpu_custom_call", output_to_operand_aliasing={{0}: (1, {}), {1}: (2, {}), {2}: (3, {}), {3}: (4, {}), {4}... | custom-call | bytes 3000000 | tf_op jit(solution)/shard_map/run_inside_rest/pallas_call | solution.py:527
  74.1 0.0 collective-permute-done.6.mid_b
  74.2 0.0 collective-permute-done.7.mid_a
  74.2 16.5 %run_near.1 = (f32[2,3,32,2048]{3,2,1,0:T(8,128)}, f32[2,3,32,2048]{3,2,1,0:T(8,128)}, f32[8096,128]{1,0:T(8,128)S(1)}, f32[8096,128]{1,0:T(8,128)S(1)}, f32[137...) custom-call(f32[12]{0:T(128)S(1)} %copy-done.4, ...), custom_call_target="tpu_custom_call", output_to_operand_aliasing={{2}: (1, {}), {3}: (2, {}), {4}: (3, {}), {5}: (4, {}), {6}... | custom-call | bytes 36000000 | tf_op jit(solution)/shard_map/run_near/pallas_call | solution.py:556
  90.7 0.0 collective-permute-done.8.far_b
  90.7 0.3 collective-permute-done.9.far_a
  91.0 0.0 copy-start.3
  91.0 10.4 %run_far.1 = (f32[2,3,32,2048]{3,2,1,0:T(8,128)}, f32[2,3,32,2048]{3,2,1,0:T(8,128)}, f32[48,128]{1,0:T(8,128)S(1)}, f32[8096,128]{1,0:T(8,128)S(1)}, f32[8096,1...) custom-call(f32[12]{0:T(128)S(1)} %copy-done.4, ...), custom_call_target="tpu_custom_call", output_to_operand_aliasing={{0}: (6, {}), {1}: (7, {}), {3}: (1, {}), {4}: (2, {}), {5}... | custom-call | bytes 24000000 | tf_op jit(solution)/shard_map/run_far/pallas_call | solution.py:567
  101.4 16.8 %all_to_all.5 = f32[16,3,128]{2,1,0:T(4,128)S(1)} all-to-all(f32[16,3,128]{2,1,0:T(4,128)S(1)} %reshape.36), channel_id=1, replica_groups=mesh['gx'=16,'gy'=16] {'gy'}, dimensions={0} | all-to-all | bytes 49152 | tf_op jit(solution)/shard_map/all_to_all | solution.py:578
  118.2 0.0 copy-done.3
  118.2 1.2 %collect.1 = f32[4,128]{1,0:T(4,128)} custom-call(f32[48,128]{1,0:T(8,128)S(1)} %reshape.37.received, f32[128,128]{1,0:T(8,128)S(1)} %copy-done.3), custom_call_target="tpu_custom_call" | custom-call | bytes 3000000 | tf_op jit(solution)/shard_map/collect/pallas_call | solution.py:581
  (5 shorter events, 0.0 us)
Async XLA Ops:
  2.8 26.8 %copy-start.5 = (s32[1,1,16,1]{2,3,1,0:T(1,128)S(1)}, s32[1,1,16,1]{2,3,1,0:T(1,128)}, u32[]{:S(2)}) copy-start(s32[1,1,16,1]{2,3,1,0:T(1,128)} %param.14) | copy-start | bytes 196
  2.8 43.3 %copy-start = (f32[2,3,32,2048]{3,2,1,0:T(8,128)S(1)}, f32[2,3,32,2048]{3,2,1,0:T(8,128)}, u32[]{:S(2)}) copy-start(f32[2,3,32,2048]{3,2,1,0:T(8,128)} %e.6) | copy-start | bytes 4718596
  2.8 43.2 %copy-start.1 = (f32[2,3,32,2048]{3,2,1,0:T(8,128)S(1)}, f32[2,3,32,2048]{3,2,1,0:T(8,128)}, u32[]{:S(2)}) copy-start(f32[2,3,32,2048]{3,2,1,0:T(8,128)} %h.6) | copy-start | bytes 4718596
  2.8 43.2 %copy-start.2 = (f32[32,2048]{1,0:T(8,128)S(1)}, f32[32,2048]{1,0:T(8,128)}, u32[]{:S(2)}) copy-start(f32[32,2048]{1,0:T(8,128)} %eps.6) | copy-start | bytes 786436
  2.8 17.1 %collective-permute-start = (f32[8,10240]{1,0:T(8,128)S(1)}, f32[8,10240]{1,0:T(8,128)S(1)}, u32[]{:S(2)}, u32[]{:S(2)}) collective-permute-start(f32[8,10240]{1,0:T(8,128)S(1)} %get-tuple-element.70), channel_id=1, source_target_pairs={{0,16},{16,32},{32,48},{48,64},{64,80},{80,96},{96,112},{112,128},... | collective-permute-start | bytes 983048 | tf_op jit(solution)/shard_map/ppermute | solution.py:36
  6.5 16.8 %collective-permute-start.1 = (f32[8,10240]{1,0:T(8,128)S(1)}, f32[8,10240]{1,0:T(8,128)S(1)}, u32[]{:S(2)}, u32[]{:S(2)}) collective-permute-start(f32[8,10240]{1,0:T(8,128)S(1)} %get-tuple-element.71), channel_id=1, source_target_pairs={{0,240},{16,0},{32,16},{48,32},{64,48},{80,64},{96,80},{112,96},{1... | collective-permute-start | bytes 983048 | tf_op jit(solution)/shard_map/ppermute | solution.py:36
  23.3 17.4 %collective-permute-start.4 = (f32[14,32,384]{2,1,0:T(8,128)S(1)}, f32[14,32,384]{2,1,0:T(8,128)S(1)}, u32[]{:S(2)}, u32[]{:S(2)}) collective-permute-start(f32[14,32,384]{2,1,0:T(8,128)S(1)} %get-tuple-element.78), channel_id=1, source_target_pairs={{0,1},{1,2},{2,3},{3,4},{4,5},{5,6},{6,7},{7,8},{8,9},{9,10},{10,1... | collective-permute-start | bytes 2064392 | tf_op jit(solution)/shard_map/ppermute | solution.py:36
  26.3 14.3 %collective-permute-start.5 = (f32[14,32,384]{2,1,0:T(8,128)S(1)}, f32[14,32,384]{2,1,0:T(8,128)S(1)}, u32[]{:S(2)}, u32[]{:S(2)}) collective-permute-start(f32[14,32,384]{2,1,0:T(8,128)S(1)} %get-tuple-element.79), channel_id=1, source_target_pairs={{0,15},{1,0},{2,1},{3,2},{4,3},{5,4},{6,5},{7,6},{8,7},{9,8},{10,9... | collective-permute-start | bytes 2064392 | tf_op jit(solution)/shard_map/ppermute | solution.py:36
  26.8 11.1 %collective-permute-start.2 = (f32[14,16,384]{2,1,0:T(8,128)S(1)}, f32[14,16,384]{2,1,0:T(8,128)S(1)}, u32[]{:S(2)}, u32[]{:S(2)}) collective-permute-start(f32[14,16,384]{2,1,0:T(8,128)S(1)} %get-tuple-element.76), channel_id=1, source_target_pairs={{0,1},{1,2},{2,3},{3,4},{4,5},{5,6},{6,7},{7,8},{8,9},{9,10},{10,1... | collective-permute-start | bytes 1032200 | tf_op jit(solution)/shard_map/ppermute | solution.py:36
  28.6 12.1 %collective-permute-start.3 = (f32[14,16,384]{2,1,0:T(8,128)S(1)}, f32[14,16,384]{2,1,0:T(8,128)S(1)}, u32[]{:S(2)}, u32[]{:S(2)}) collective-permute-start(f32[14,16,384]{2,1,0:T(8,128)S(1)} %get-tuple-element.77), channel_id=1, source_target_pairs={{0,15},{1,0},{2,1},{3,2},{4,3},{5,4},{6,5},{7,6},{8,7},{9,8},{10,9... | collective-permute-start | bytes 1032200 | tf_op jit(solution)/shard_map/ppermute | solution.py:36
  40.7 33.5 %collective-permute-start.6 = (f32[8,16640]{1,0:T(8,128)S(1)}, f32[8,16640]{1,0:T(8,128)S(1)}, u32[]{:S(2)}, u32[]{:S(2)}) collective-permute-start(f32[8,16640]{1,0:T(8,128)S(1)} %get-tuple-element.105), channel_id=1, source_target_pairs={{0,16},{16,32},{32,48},{48,64},{64,80},{80,96},{96,112},{112,128},... | collective-permute-start | bytes 1597448 | tf_op jit(solution)/shard_map/ppermute | solution.py:36
  40.7 33.5 %collective-permute-start.7 = (f32[8,16640]{1,0:T(8,128)S(1)}, f32[8,16640]{1,0:T(8,128)S(1)}, u32[]{:S(2)}, u32[]{:S(2)}) collective-permute-start(f32[8,16640]{1,0:T(8,128)S(1)} %get-tuple-element.106), channel_id=1, source_target_pairs={{0,240},{16,0},{32,16},{48,32},{64,48},{80,64},{96,80},{112,96},{1... | collective-permute-start | bytes 1597448 | tf_op jit(solution)/shard_map/ppermute | solution.py:36
  46.1 0.7 copy-start.4
  46.7 19.9 %copy-start.6 = (s32[1,1,16]{2,1,0:T(1,128)S(1)}, s32[1,1,16]{2,1,0:T(1,128)}, u32[]{:S(2)}) copy-start(s32[1,1,16]{2,1,0:T(1,128)} %param.15) | copy-start | bytes 196
  61.4 29.2 %collective-permute-start.8 = (f32[7,8,2560]{2,1,0:T(8,128)S(1)}, f32[7,8,2560]{2,1,0:T(8,128)S(1)}, u32[]{:S(2)}, u32[]{:S(2)}) collective-permute-start(f32[7,8,2560]{2,1,0:T(8,128)S(1)} %get-tuple-element.116), channel_id=1, source_target_pairs={{0,16},{16,32},{32,48},{48,64},{64,80},{80,96},{96,112},{112,128},... | collective-permute-start | bytes 1720328 | tf_op jit(solution)/shard_map/ppermute | solution.py:36
  61.5 29.4 %collective-permute-start.9 = (f32[7,8,2560]{2,1,0:T(8,128)S(1)}, f32[7,8,2560]{2,1,0:T(8,128)S(1)}, u32[]{:S(2)}, u32[]{:S(2)}) collective-permute-start(f32[7,8,2560]{2,1,0:T(8,128)S(1)} %get-tuple-element.117), channel_id=1, source_target_pairs={{0,240},{16,0},{32,16},{48,32},{64,48},{80,64},{96,80},{112,96},{1... | collective-permute-start | bytes 1720328 | tf_op jit(solution)/shard_map/ppermute | solution.py:36
  91.0 27.3 %copy-start.3 = (f32[128,128]{1,0:T(8,128)S(1)}, f32[128,128]{1,0:T(8,128)}, u32[]{:S(2)}) copy-start(f32[128,128]{1,0:T(8,128)} %filter_matrix.1) | copy-start | bytes 196612

commit v8 on v7

--- a/solution.py
+++ b/solution.py
@@ -29,6 +29,7 @@
 FARW = TILES + HT + 1
 LANES = 128
 HIGH = lax.Precision.HIGHEST
+CUT = 8
 
 
 def shifted(array, axis, by):
@@ -156,12 +157,13 @@
         to_next[p, q, LANES + length :] = right[a, hi : hi + FAR, :]
 
 
-def pack_corner(behind, ahead, to_left, to_right):
+def pack_corner(behind, ahead, to_left, to_right, aux):
     edge = HT * LANES
     length = TILES * LANES
     for k, src in enumerate((behind, ahead)):
         made = near_source(src)
         rows = pl.ds(NEAR * k, NEAR)
+        aux[rows, :] = made
         to_left[NARR - 1, rows, :] = made[:, 0:edge]
         to_right[NARR - 1, rows, :] = made[:, length - edge : length]
         for a in range(NARR - 1):
@@ -324,11 +326,11 @@
                 place(dst, a, HALO + 8 * i, HT + TILES + j, fix(right[n, rows, cols]))
     fill_sources(wa, ws, ((HALO, ROWS),))
     acc[...] = jnp.zeros_like(acc)
-    Stepper(waves, we, wh, wc, ws, acc).inside(HALO, HALO + ROWS - 1, 0, STEPS // 2)
+    Stepper(waves, we, wh, wc, ws, acc).inside(HALO, HALO + ROWS - 1, 0, CUT)
 
 
 def run_inside_rest(waves, _e, _h, _c, _s, _t, we, wh, wc, ws, acc):
-    Stepper(waves, we, wh, wc, ws, acc).inside(HALO, HALO + ROWS - 1, STEPS // 2, STEPS)
+    Stepper(waves, we, wh, wc, ws, acc).inside(HALO, HALO + ROWS - 1, CUT, STEPS)
 
 
 def store_rows(we, wh, stage, e_out, h_out, sems, x, count):
@@ -348,13 +350,13 @@
     return copies
 
 
-def run_near(waves, _e, _h, _c, _s, _t, edge_b, edge_a, mid_b, mid_a, corner_l, corner_r, e_out, h_out, we, wh, wc, ws, acc, wa, made, stage, sems):
+def run_near(waves, _e, _h, _c, _s, _t, edge_b, edge_a, mid_b, mid_a, corner_l, corner_r, aux_near, e_out, h_out, we, wh, wc, ws, acc, wa, stage, sems):
     edge = HT * LANES
     inner = (TILES - 2 * HT) * LANES
 
-    def near_tile(side, middle, n, j):
+    def near_tile(side, middle, n, j, rows):
         if n == NARR - 1:
-            return made[:, pl.ds(j * LANES, LANES)]
+            return aux_near[rows, pl.ds(j * LANES, LANES)]
         if HT <= j < TILES - HT:
             return middle[:, pl.ds(n * inner + (j - HT) * LANES, LANES)]
         j = j if j < HT else j - (TILES - 2 * HT)
@@ -363,11 +365,10 @@
     for k, (side, middle, x) in enumerate(
         ((edge_b, mid_b, FAR), (edge_a, mid_a, HALO + ROWS))
     ):
-        made[...] = near_source(side)
         rows = pl.ds(NEAR * k, NEAR)
         for n, (dst, a, fix) in enumerate(kinds(we, wh, wc, wa)):
             for j in range(TILES):
-                place(dst, a, x, HT + j, fix(near_tile(side, middle, n, j)))
+                place(dst, a, x, HT + j, fix(near_tile(side, middle, n, j, rows)))
             for j in range(HT):
                 cols = pl.ds(j * LANES, LANES)
                 place(dst, a, x, j, fix(corner_l[n, rows, cols]))
@@ -493,8 +494,9 @@
     right = shifted(to_left, "gy", -1)
 
     y_corner = (NARR, 2 * NEAR, edge)
-    made = pltpu.VMEM((NEAR, length), jnp.float32)
-    corner_left, corner_right = call(pack_corner, (y_corner, y_corner), 2, 2)(edge_b, edge_a)
+    corner_left, corner_right, aux_near = call(
+        pack_corner, (y_corner, y_corner, (2 * NEAR, length)), 2, 2
+    )(edge_b, edge_a)
     corner_l = shifted(corner_right, "gy", 1)
     corner_r = shifted(corner_left, "gy", -1)
     corner_l, corner_r, left, right, mid_prev, mid_next = lax.optimization_barrier(
@@ -556,13 +558,13 @@
     state = call(
         run_near,
         (field, field) + held,
+        13,
         12,
-        12,
-        in_specs=[smem] + [vmem] * 11,
+        in_specs=[smem] + [vmem] * 12,
         out_specs=(hbm,) * 2 + (vmem,) * 5,
-        scratch_shapes=[tags, made, pltpu.VMEM((12, 16, length), jnp.float32), copy_sem((12,))],
+        scratch_shapes=[tags, pltpu.VMEM((12, 16, length), jnp.float32), copy_sem((12,))],
         input_output_aliases={1 + k: 2 + k for k in range(5)},
-    )(waves, *state, edge_b, edge_a, mid_b, mid_a, corner_l, corner_r)
+    )(waves, *state, edge_b, edge_a, mid_b, mid_a, corner_l, corner_r, aux_near)
     stage = pltpu.VMEM((12, 8, length), jnp.float32)
     out = call(
         run_far,

time: 120 us -> 117 us (0.975); the launches traced: 119 us -> 115 us
  blocking collectives: 16.8 us -> 11.3 us
    all_to_all x1, blocking collectives: 16.8 us -> 11.3 us  [per_device(): lax.all_to_all(packed.reshape(owners, 3, LANES), 'gy', split_axis=0, conc...]
    pallas_call x1, Pallas kernels: 14.7 us -> 17.5 us  [per_device(): call(run_inside, held, 7, 30, in_specs=[smem] + [vmem] * 6, scratch_shape...]
    pallas_call x1, Pallas kernels: 7.31 us -> 4.53 us  [per_device(): call(run_inside_rest, held, 6, 1, in_specs=[smem] + [vmem] * 5, input_out...]
  transfers between devices with their start and end apart: 10 -> 10, of which waited for: 5 -> 5; matrix products, arithmetic and copies ran while one was open for 0% -> 0% of each run, Pallas kernels for 34% -> 36%
where the time goes in v8:
time: 117 us; the launch traced here: 115 us
  Pallas kernels  54.5 us (47%)
  starting transfers between devices  25.5 us (22%)
  waiting for transfers between devices  21.8 us (19%)
  blocking collectives  11.3 us (10%)
    ppermute x10, starting transfers between devices, shifted(): lax.ppermute(array, axis, [(i, (i + by) % count) for i in range(count)])  25.5 us
    ppermute x10, waiting for transfers between devices, shifted(): lax.ppermute(array, axis, [(i, (i + by) % count) for i in range(count)])  21.8 us
    pallas_call x1, Pallas kernels, per_device(): call(run_inside, held, 7, 30, in_specs=[smem] + [vmem] * 6, scratch_shape...  17.5 us
    pallas_call x1, Pallas kernels, per_device(): call(run_near, (field, field) + held, 13, 12, in_specs=[smem] + [vmem] *...  15.9 us
    all_to_all x1, blocking collectives, per_device(): lax.all_to_all(packed.reshape(owners, 3, LANES), 'gy', split_axis=0, conc...  11.3 us
    pallas_call x1, Pallas kernels, per_device(): call(run_far, (field, field, (3 * owners, LANES)) + held, 12, 8, in_specs...  10.4 us
    pallas_call x1, Pallas kernels, per_device(): call(run_inside_rest, held, 6, 1, in_specs=[smem] + [vmem] * 5, input_out...  4.53 us
  transfers between devices with their start and end apart: 10, of which 5 were waited for; matrix products, arithmetic and copies ran while one was open for 0% of the time, Pallas kernels for 36%

profile of v8, /device:TPU:1, one launch (start us, length us, event | category | flops | bytes accessed | tf_op | source)
XLA Modules:
  0.0 114.8 jit_solution(4090479697625918896)
XLA Ops:
  0.6 2.2 %pack_near.1 = (f32[8,10240]{1,0:T(8,128)S(1)}, f32[8,10240]{1,0:T(8,128)S(1)}, f32[8,16640]{1,0:T(8,128)S(1)}, f32[8,16640]{1,0:T(8,128)S(1)}) custom-call(f32[2,3,32,2048]{3,2,1,0:T(8,128)} %e.6, f32[2,3,32,2048]{3,2,1,0:T(8,128)} %h.6, f32[32,2048]{1,0:T(8,128)} %eps.6, f32[2,32,64]{2,1,0:T(8,128)} %profile.2, s32[2,32]{1,0:T(2,128)} %plane.2), custom_call_target="tpu_custom_call" | custom-call | bytes 6000000 | tf_op jit(solution)/shard_map/pack_near/pallas_call | solution.py:479
  2.8 0.0 copy-start.5
  2.8 0.0 copy-start
  2.8 0.0 copy-start.1
  2.8 0.0 copy-start.2
  2.8 3.7 %collective-permute-start = (f32[8,10240]{1,0:T(8,128)S(1)}, f32[8,10240]{1,0:T(8,128)S(1)}, u32[]{:S(2)}, u32[]{:S(2)}) collective-permute-start(f32[8,10240]{1,0:T(8,128)S(1)} %get-tuple-element.71), channel_id=1, source_target_pairs={{0,16},{16,32},{32,48},{48,64},{64,80},{80,96},{96,112},{112,128},... | collective-permute-start | bytes 983048 | tf_op jit(solution)/shard_map/ppermute | solution.py:37
  6.5 5.4 %collective-permute-start.1 = (f32[8,10240]{1,0:T(8,128)S(1)}, f32[8,10240]{1,0:T(8,128)S(1)}, u32[]{:S(2)}, u32[]{:S(2)}) collective-permute-start(f32[8,10240]{1,0:T(8,128)S(1)} %get-tuple-element.72), channel_id=1, source_target_pairs={{0,240},{16,0},{32,16},{48,32},{64,48},{80,64},{96,80},{112,96},{1... | collective-permute-start | bytes 983048 | tf_op jit(solution)/shard_map/ppermute | solution.py:37
  11.9 1.8 %pack_side.1 = (f32[14,32,384]{2,1,0:T(8,128)S(1)}, f32[14,32,384]{2,1,0:T(8,128)S(1)}, f32[32,2048]{1,0:T(8,128)S(1)}) custom-call(f32[2,3,32,2048]{3,2,1,0:T(8,128)} %e.6, f32[2,3,32,2048]{3,2,1,0:T(8,128)} %h.6, f32[32,2048]{1,0:T(8,128)} %eps.6, f32[2,32,64]{2,1,0:T(8,128)} %profile.2, s32[2,32]{1,0:T(2,128)} %plane.2), custom_call_target="tpu_custom_call" | custom-call | bytes 9000000 | tf_op jit(solution)/shard_map/pack_side/pallas_call | solution.py:487
  13.7 6.2 %collective-permute-done.behind.edge_b = f32[8,10240]{1,0:T(8,128)S(1)} collective-permute-done((f32[8,10240]{1,0:T(8,128)S(1)}, f32[8,10240]{1,0:T(8,128)S(1)}, u32[]{:S(2)}, u32[]{:S(2)}) %collective-permute-start) | collective-permute-done | bytes 327712 | tf_op jit(solution)/shard_map/ppermute | solution.py:37
  19.9 3.4 %collective-permute-done.1.ahead.edge_a = f32[8,10240]{1,0:T(8,128)S(1)} collective-permute-done((f32[8,10240]{1,0:T(8,128)S(1)}, f32[8,10240]{1,0:T(8,128)S(1)}, u32[]{:S(2)}, u32[]{:S(2)}) %collective-permute-start.1) | collective-permute-done | bytes 327712 | tf_op jit(solution)/shard_map/ppermute | solution.py:37
  23.3 3.0 %collective-permute-start.4 = (f32[14,32,384]{2,1,0:T(8,128)S(1)}, f32[14,32,384]{2,1,0:T(8,128)S(1)}, u32[]{:S(2)}, u32[]{:S(2)}) collective-permute-start(f32[14,32,384]{2,1,0:T(8,128)S(1)} %get-tuple-element.79), channel_id=1, source_target_pairs={{0,1},{1,2},{2,3},{3,4},{4,5},{5,6},{6,7},{7,8},{8,9},{9,10},{10,1... | collective-permute-start | bytes 2064392 | tf_op jit(solution)/shard_map/ppermute | solution.py:37
  26.3 0.0 collective-permute-start.5
  26.3 0.8 pack_corner.1
  27.2 1.8 %collective-permute-start.2 = (f32[14,16,384]{2,1,0:T(8,128)S(1)}, f32[14,16,384]{2,1,0:T(8,128)S(1)}, u32[]{:S(2)}, u32[]{:S(2)}) collective-permute-start(f32[14,16,384]{2,1,0:T(8,128)S(1)} %get-tuple-element.77), channel_id=1, source_target_pairs={{0,1},{1,2},{2,3},{3,4},{4,5},{5,6},{6,7},{7,8},{8,9},{9,10},{10,1... | collective-permute-start | bytes 1032200 | tf_op jit(solution)/shard_map/ppermute | solution.py:37
  28.9 1.0 collective-permute-start.3
  29.9 0.0 copy-done.5
  29.9 0.2 convert_reduce_fusion
  30.1 7.8 %collective-permute-done.2.corner_l = f32[14,16,384]{2,1,0:T(8,128)S(1)} collective-permute-done((f32[14,16,384]{2,1,0:T(8,128)S(1)}, f32[14,16,384]{2,1,0:T(8,128)S(1)}, u32[]{:S(2)}, u32[]{:S(2)}) %collective-permute-start.2) | collective-permute-done | bytes 344096 | tf_op jit(solution)/shard_map/ppermute | solution.py:37
  37.9 2.8 %collective-permute-done.3.corner_r = f32[14,16,384]{2,1,0:T(8,128)S(1)} collective-permute-done((f32[14,16,384]{2,1,0:T(8,128)S(1)}, f32[14,16,384]{2,1,0:T(8,128)S(1)}, u32[]{:S(2)}, u32[]{:S(2)}) %collective-permute-start.3) | collective-permute-done | bytes 344096 | tf_op jit(solution)/shard_map/ppermute | solution.py:37
  40.7 0.0 collective-permute-done.4.left
  40.7 0.0 collective-permute-done.5.right
  40.7 0.0 collective-permute-start.6
  40.7 5.4 %collective-permute-start.7 = (f32[8,16640]{1,0:T(8,128)S(1)}, f32[8,16640]{1,0:T(8,128)S(1)}, u32[]{:S(2)}, u32[]{:S(2)}) collective-permute-start(f32[8,16640]{1,0:T(8,128)S(1)} %get-tuple-element.107), channel_id=1, source_target_pairs={{0,240},{16,0},{32,16},{48,32},{64,48},{80,64},{96,80},{112,96},{1... | collective-permute-start | bytes 1597448 | tf_op jit(solution)/shard_map/ppermute | solution.py:37
  46.1 0.0 copy-done
  46.1 0.0 copy-done.1
  46.1 0.0 copy-done.2
  46.1 0.0 copy-start.4
  46.1 0.2 pack_far.1
  46.3 0.4 copy-done.4
  46.7 0.0 copy-start.6
  46.7 17.5 %run_inside.1 = (f32[8096,128]{1,0:T(8,128)S(1)}, f32[8096,128]{1,0:T(8,128)S(1)}, f32[1376,128]{1,0:T(8,128)S(1)}, f32[2720,128]{1,0:T(8,128)S(1)}, f32[1376,128]{1,0:T(8,128)S(1)}) custom-call(f32[12]{0:T(128)S(1)} %copy-done.4, f32[2,3,32,2048]{3,2,1,0:T(8,128)S(1)} %copy-done, f32[2,3,32,2048]{3,2,1,0:T(8,128)S(1)} %copy-done.1, ...), custom_call_target="tpu_custom_call" | custom-call | bytes 90000000 | tf_op jit(solution)/shard_map/run_inside/pallas_call | solution.py:522
  64.2 0.3 collective-permute-start.8
  64.5 5.1 %collective-permute-start.9 = (f32[7,8,2560]{2,1,0:T(8,128)S(1)}, f32[7,8,2560]{2,1,0:T(8,128)S(1)}, u32[]{:S(2)}, u32[]{:S(2)}) collective-permute-start(f32[7,8,2560]{2,1,0:T(8,128)S(1)} %get-tuple-element.119), channel_id=1, source_target_pairs={{0,240},{16,0},{32,16},{48,32},{64,48},{80,64},{96,80},{112,96},{1... | collective-permute-start | bytes 1720328 | tf_op jit(solution)/shard_map/ppermute | solution.py:37
  69.6 0.0 copy-done.6
  69.6 0.2 fusion.1.marks
  69.8 4.5 %run_inside_rest.1 = (f32[8096,128]{1,0:T(8,128)S(1)}, f32[8096,128]{1,0:T(8,128)S(1)}, f32[1376,128]{1,0:T(8,128)S(1)}, f32[2720,128]{1,0:T(8,128)S(1)}, f32[1376,128]{1,0:T(8,128)S(1)}) custom-call(f32[12]{0:T(128)S(1)} %copy-done.4, ...), custom_call_target="tpu_custom_call", output_to_operand_aliasing={{0}: (1, {}), {1}: (2, {}), {2}: (3, {}), {3}: (4, {}), {4}... | custom-call | bytes 3000000 | tf_op jit(solution)/shard_map/run_inside_rest/pallas_call | solution.py:529
  74.3 0.0 collective-permute-done.6.mid_b
  74.3 0.0 collective-permute-done.7.mid_a
  74.4 15.9 %run_near.1 = (f32[2,3,32,2048]{3,2,1,0:T(8,128)}, f32[2,3,32,2048]{3,2,1,0:T(8,128)}, f32[8096,128]{1,0:T(8,128)S(1)}, f32[8096,128]{1,0:T(8,128)S(1)}, f32[137...) custom-call(f32[12]{0:T(128)S(1)} %copy-done.4, ...), custom_call_target="tpu_custom_call", output_to_operand_aliasing={{2}: (1, {}), {3}: (2, {}), {4}: (3, {}), {5}: (4, {}), {6}... | custom-call | bytes 36000000 | tf_op jit(solution)/shard_map/run_near/pallas_call | solution.py:558
  90.3 0.0 collective-permute-done.8.far_b
  90.3 1.6 %collective-permute-done.9.far_a = f32[7,8,2560]{2,1,0:T(8,128)S(1)} collective-permute-done((f32[7,8,2560]{2,1,0:T(8,128)S(1)}, f32[7,8,2560]{2,1,0:T(8,128)S(1)}, u32[]{:S(2)}, u32[]{:S(2)}) %collective-permute-start.9) | collective-permute-done | bytes 573472 | tf_op jit(solution)/shard_map/ppermute | solution.py:37
  91.8 0.0 copy-start.3
  91.8 10.4 %run_far.1 = (f32[2,3,32,2048]{3,2,1,0:T(8,128)}, f32[2,3,32,2048]{3,2,1,0:T(8,128)}, f32[48,128]{1,0:T(8,128)S(1)}, f32[8096,128]{1,0:T(8,128)S(1)}, f32[8096,1...) custom-call(f32[12]{0:T(128)S(1)} %copy-done.4, ...), custom_call_target="tpu_custom_call", output_to_operand_aliasing={{0}: (6, {}), {1}: (7, {}), {3}: (1, {}), {4}: (2, {}), {5}... | custom-call | bytes 24000000 | tf_op jit(solution)/shard_map/run_far/pallas_call | solution.py:569
  102.3 11.3 %all_to_all.5 = f32[16,3,128]{2,1,0:T(4,128)S(1)} all-to-all(f32[16,3,128]{2,1,0:T(4,128)S(1)} %reshape.36), channel_id=1, replica_groups=mesh['gx'=16,'gy'=16] {'gy'}, dimensions={0} | all-to-all | bytes 49152 | tf_op jit(solution)/shard_map/all_to_all | solution.py:580
  113.6 0.0 copy-done.3
  113.6 1.2 %collect.1 = f32[4,128]{1,0:T(4,128)} custom-call(f32[48,128]{1,0:T(8,128)S(1)} %reshape.37.received, f32[128,128]{1,0:T(8,128)S(1)} %copy-done.3), custom_call_target="tpu_custom_call" | custom-call | bytes 3000000 | tf_op jit(solution)/shard_map/collect/pallas_call | solution.py:583
  (5 shorter events, 0.0 us)
Async XLA Ops:
  2.8 27.1 %copy-start.5 = (s32[1,1,16,1]{2,3,1,0:T(1,128)S(1)}, s32[1,1,16,1]{2,3,1,0:T(1,128)}, u32[]{:S(2)}) copy-start(s32[1,1,16,1]{2,3,1,0:T(1,128)} %param.14) | copy-start | bytes 196
  2.8 43.3 %copy-start = (f32[2,3,32,2048]{3,2,1,0:T(8,128)S(1)}, f32[2,3,32,2048]{3,2,1,0:T(8,128)}, u32[]{:S(2)}) copy-start(f32[2,3,32,2048]{3,2,1,0:T(8,128)} %e.6) | copy-start | bytes 4718596
  2.8 43.2 %copy-start.1 = (f32[2,3,32,2048]{3,2,1,0:T(8,128)S(1)}, f32[2,3,32,2048]{3,2,1,0:T(8,128)}, u32[]{:S(2)}) copy-start(f32[2,3,32,2048]{3,2,1,0:T(8,128)} %h.6) | copy-start | bytes 4718596
  2.8 43.2 %copy-start.2 = (f32[32,2048]{1,0:T(8,128)S(1)}, f32[32,2048]{1,0:T(8,128)}, u32[]{:S(2)}) copy-start(f32[32,2048]{1,0:T(8,128)} %eps.6) | copy-start | bytes 786436
  2.8 17.1 %collective-permute-start = (f32[8,10240]{1,0:T(8,128)S(1)}, f32[8,10240]{1,0:T(8,128)S(1)}, u32[]{:S(2)}, u32[]{:S(2)}) collective-permute-start(f32[8,10240]{1,0:T(8,128)S(1)} %get-tuple-element.71), channel_id=1, source_target_pairs={{0,16},{16,32},{32,48},{48,64},{64,80},{80,96},{96,112},{112,128},... | collective-permute-start | bytes 983048 | tf_op jit(solution)/shard_map/ppermute | solution.py:37
  6.5 16.8 %collective-permute-start.1 = (f32[8,10240]{1,0:T(8,128)S(1)}, f32[8,10240]{1,0:T(8,128)S(1)}, u32[]{:S(2)}, u32[]{:S(2)}) collective-permute-start(f32[8,10240]{1,0:T(8,128)S(1)} %get-tuple-element.72), channel_id=1, source_target_pairs={{0,240},{16,0},{32,16},{48,32},{64,48},{80,64},{96,80},{112,96},{1... | collective-permute-start | bytes 983048 | tf_op jit(solution)/shard_map/ppermute | solution.py:37
  23.3 17.4 %collective-permute-start.4 = (f32[14,32,384]{2,1,0:T(8,128)S(1)}, f32[14,32,384]{2,1,0:T(8,128)S(1)}, u32[]{:S(2)}, u32[]{:S(2)}) collective-permute-start(f32[14,32,384]{2,1,0:T(8,128)S(1)} %get-tuple-element.79), channel_id=1, source_target_pairs={{0,1},{1,2},{2,3},{3,4},{4,5},{5,6},{6,7},{7,8},{8,9},{9,10},{10,1... | collective-permute-start | bytes 2064392 | tf_op jit(solution)/shard_map/ppermute | solution.py:37
  26.3 14.3 %collective-permute-start.5 = (f32[14,32,384]{2,1,0:T(8,128)S(1)}, f32[14,32,384]{2,1,0:T(8,128)S(1)}, u32[]{:S(2)}, u32[]{:S(2)}) collective-permute-start(f32[14,32,384]{2,1,0:T(8,128)S(1)} %get-tuple-element.80), channel_id=1, source_target_pairs={{0,15},{1,0},{2,1},{3,2},{4,3},{5,4},{6,5},{7,6},{8,7},{9,8},{10,9... | collective-permute-start | bytes 2064392 | tf_op jit(solution)/shard_map/ppermute | solution.py:37
  27.2 10.7 %collective-permute-start.2 = (f32[14,16,384]{2,1,0:T(8,128)S(1)}, f32[14,16,384]{2,1,0:T(8,128)S(1)}, u32[]{:S(2)}, u32[]{:S(2)}) collective-permute-start(f32[14,16,384]{2,1,0:T(8,128)S(1)} %get-tuple-element.77), channel_id=1, source_target_pairs={{0,1},{1,2},{2,3},{3,4},{4,5},{5,6},{6,7},{7,8},{8,9},{9,10},{10,1... | collective-permute-start | bytes 1032200 | tf_op jit(solution)/shard_map/ppermute | solution.py:37
  28.9 11.8 %collective-permute-start.3 = (f32[14,16,384]{2,1,0:T(8,128)S(1)}, f32[14,16,384]{2,1,0:T(8,128)S(1)}, u32[]{:S(2)}, u32[]{:S(2)}) collective-permute-start(f32[14,16,384]{2,1,0:T(8,128)S(1)} %get-tuple-element.78), channel_id=1, source_target_pairs={{0,15},{1,0},{2,1},{3,2},{4,3},{5,4},{6,5},{7,6},{8,7},{9,8},{10,9... | collective-permute-start | bytes 1032200 | tf_op jit(solution)/shard_map/ppermute | solution.py:37
  40.7 33.7 %collective-permute-start.6 = (f32[8,16640]{1,0:T(8,128)S(1)}, f32[8,16640]{1,0:T(8,128)S(1)}, u32[]{:S(2)}, u32[]{:S(2)}) collective-permute-start(f32[8,16640]{1,0:T(8,128)S(1)} %get-tuple-element.106), channel_id=1, source_target_pairs={{0,16},{16,32},{32,48},{48,64},{64,80},{80,96},{96,112},{112,128},... | collective-permute-start | bytes 1597448 | tf_op jit(solution)/shard_map/ppermute | solution.py:37
  40.7 33.7 %collective-permute-start.7 = (f32[8,16640]{1,0:T(8,128)S(1)}, f32[8,16640]{1,0:T(8,128)S(1)}, u32[]{:S(2)}, u32[]{:S(2)}) collective-permute-start(f32[8,16640]{1,0:T(8,128)S(1)} %get-tuple-element.107), channel_id=1, source_target_pairs={{0,240},{16,0},{32,16},{48,32},{64,48},{80,64},{96,80},{112,96},{1... | collective-permute-start | bytes 1597448 | tf_op jit(solution)/shard_map/ppermute | solution.py:37
  46.1 0.7 copy-start.4
  46.7 22.8 %copy-start.6 = (s32[1,1,16]{2,1,0:T(1,128)S(1)}, s32[1,1,16]{2,1,0:T(1,128)}, u32[]{:S(2)}) copy-start(s32[1,1,16]{2,1,0:T(1,128)} %param.15) | copy-start | bytes 196
  64.2 26.0 %collective-permute-start.8 = (f32[7,8,2560]{2,1,0:T(8,128)S(1)}, f32[7,8,2560]{2,1,0:T(8,128)S(1)}, u32[]{:S(2)}, u32[]{:S(2)}) collective-permute-start(f32[7,8,2560]{2,1,0:T(8,128)S(1)} %get-tuple-element.118), channel_id=1, source_target_pairs={{0,16},{16,32},{32,48},{48,64},{64,80},{80,96},{96,112},{112,128},... | collective-permute-start | bytes 1720328 | tf_op jit(solution)/shard_map/ppermute | solution.py:37
  64.5 27.3 %collective-permute-start.9 = (f32[7,8,2560]{2,1,0:T(8,128)S(1)}, f32[7,8,2560]{2,1,0:T(8,128)S(1)}, u32[]{:S(2)}, u32[]{:S(2)}) collective-permute-start(f32[7,8,2560]{2,1,0:T(8,128)S(1)} %get-tuple-element.119), channel_id=1, source_target_pairs={{0,240},{16,0},{32,16},{48,32},{64,48},{80,64},{96,80},{112,96},{1... | collective-permute-start | bytes 1720328 | tf_op jit(solution)/shard_map/ppermute | solution.py:37
  91.8 21.8 %copy-start.3 = (f32[128,128]{1,0:T(8,128)S(1)}, f32[128,128]{1,0:T(8,128)}, u32[]{:S(2)}) copy-start(f32[128,128]{1,0:T(8,128)} %filter_matrix.1) | copy-start | bytes 196612

commit v9 on v8

--- a/solution.py
+++ b/solution.py
@@ -29,6 +29,8 @@
 FARW = TILES + HT + 1
 LANES = 128
 HIGH = lax.Precision.HIGHEST
+PART = NARR // 2
+EXTRA = 6 * LANES
 CUT = 8
 
 
@@ -84,16 +86,19 @@
     return copies
 
 
-def pack_side(e, h, eps, profile, plane, to_left, to_right, aux, pv, lv, sems):
+def pack_side(e, h, eps, profile, plane, left_lo, left_hi, right_lo, right_hi, aux, pv, lv, sems):
     edge = HT * LANES
     length = TILES * LANES
     tags = fetch_tags(profile, plane, pv, lv, sems)
     copies = []
-    for part, begin in ((to_left, 0), (to_right, length - edge)):
+    sides = (((left_lo, left_hi), 0), ((right_lo, right_hi), length - edge))
+    for parts, begin in sides:
         for a, src in enumerate(planes(e, h, eps)):
             copies.append(
                 pltpu.make_async_copy(
-                    src.at[:, pl.ds(begin, edge)], part.at[a], sems.at[2 + len(copies)]
+                    src.at[:, pl.ds(begin, edge)],
+                    parts[a // PART].at[a % PART],
+                    sems.at[2 + len(copies)],
                 )
             )
             copies[-1].start()
@@ -101,8 +106,8 @@
         copy.wait()
     made = source_rows(*source_tags(pv, lv))
     aux[...] = made
-    to_left[NARR - 1] = made[:, 0:edge]
-    to_right[NARR - 1] = made[:, length - edge : length]
+    left_hi[PART - 1] = made[:, 0:edge]
+    right_hi[PART - 1] = made[:, length - edge : length]
     for copy in copies:
         copy.wait()
 
@@ -143,18 +148,19 @@
     return source_rows(ref[:, base : base + LANES], ref[:, base + LANES : base + 2 * LANES])
 
 
-def pack_far(e, h, eps, aux, left, right, to_prev, to_next):
+def pack_far(e, h, eps, aux, left_lo, left_hi, right_lo, right_hi, to_prev, to_next):
     edge = HT * LANES
     length = TILES * LANES
     lo, hi = NEAR, ROWS - NEAR - FAR
     for a, src in enumerate(planes(e, h, eps, aux)):
+        left, right = ((left_lo, right_lo), (left_hi, right_hi))[a // PART]
         p, q = a // 2, pl.ds(FAR * (a % 2), FAR)
-        to_prev[p, q, 0:edge] = left[a, lo : lo + FAR, :]
+        to_prev[p, q, 0:edge] = left[a % PART, lo : lo + FAR, :]
         to_prev[p, q, edge : edge + length] = src[lo : lo + FAR, :]
-        to_prev[p, q, edge + length :] = right[a, lo : lo + FAR, 0:LANES]
-        to_next[p, q, 0:LANES] = left[a, hi : hi + FAR, edge - LANES : edge]
+        to_prev[p, q, edge + length :] = right[a % PART, lo : lo + FAR, 0:LANES]
+        to_next[p, q, 0:LANES] = left[a % PART, hi : hi + FAR, edge - LANES : edge]
         to_next[p, q, LANES : LANES + length] = src[hi : hi + FAR, :]
-        to_next[p, q, LANES + length :] = right[a, hi : hi + FAR, :]
+        to_next[p, q, LANES + length :] = right[a % PART, hi : hi + FAR, :]
 
 
 def pack_corner(behind, ahead, to_left, to_right, aux):
@@ -313,17 +319,18 @@
         lax.fori_loop(begin, end, step, 0)
 
 
-def run_inside(waves, e, h, eps, aux, left, right, we, wh, wc, ws, acc, wa):
+def run_inside(waves, e, h, eps, aux, left_lo, left_hi, right_lo, right_hi, we, wh, wc, ws, acc, wa):
     own = planes(e, h, eps, aux)
     for n, (dst, a, fix) in enumerate(kinds(we, wh, wc, wa)):
+        left, right = ((left_lo, right_lo), (left_hi, right_hi))[n // PART]
         for i in range(ROWS // 8):
             rows = pl.ds(8 * i, 8)
             for j in range(TILES):
                 place(dst, a, HALO + 8 * i, HT + j, fix(own[n][rows, pl.ds(j * LANES, LANES)]))
             for j in range(HT):
                 cols = pl.ds(j * LANES, LANES)
-                place(dst, a, HALO + 8 * i, j, fix(left[n, rows, cols]))
-                place(dst, a, HALO + 8 * i, HT + TILES + j, fix(right[n, rows, cols]))
+                place(dst, a, HALO + 8 * i, j, fix(left[n % PART, rows, cols]))
+                place(dst, a, HALO + 8 * i, HT + TILES + j, fix(right[n % PART, rows, cols]))
     fill_sources(wa, ws, ((HALO, ROWS),))
     acc[...] = jnp.zeros_like(acc)
     Stepper(waves, we, wh, wc, ws, acc).inside(HALO, HALO + ROWS - 1, 0, CUT)
@@ -474,7 +481,7 @@
             ],
         )
 
-    x_edge = (NEAR, (NARR - 1) * 2 * edge + 2 * LANES)
+    x_edge = (NEAR, (NARR - 1) * 2 * edge + 2 * LANES + EXTRA)
     x_mid = (NEAR, (NARR - 1) * (length - 2 * edge))
     edge_prev, edge_next, mid_prev, mid_next = call(
         pack_near, (x_edge, x_edge, x_mid, x_mid), 5, 2, **packing(6 * (NARR - 1))
@@ -483,15 +490,11 @@
     edge_b = shifted(edge_next, "gx", 1)
     edge_a = shifted(edge_prev, "gx", -1)
 
-    y_own = (NARR, ROWS, edge)
-    to_left, to_right, aux = call(
-        pack_side, (y_own, y_own, (ROWS, length)), 5, 3, **packing(2 * (NARR - 1))
+    y_own = (PART, ROWS, edge)
+    *sides, aux = call(
+        pack_side, (y_own,) * 4 + ((ROWS, length),), 5, 3, **packing(2 * (NARR - 1))
     )(*raw)
-    edge_b, edge_a, to_left, to_right = lax.optimization_barrier(
-        (edge_b, edge_a, to_left, to_right)
-    )
-    left = shifted(to_right, "gy", 1)
-    right = shifted(to_left, "gy", -1)
+    side = [shifted(t, "gy", 1) for t in sides[2:]] + [shifted(t, "gy", -1) for t in sides[:2]]
 
     y_corner = (NARR, 2 * NEAR, edge)
     corner_left, corner_right, aux_near = call(
@@ -499,16 +502,16 @@
     )(edge_b, edge_a)
     corner_l = shifted(corner_right, "gy", 1)
     corner_r = shifted(corner_left, "gy", -1)
-    corner_l, corner_r, left, right, mid_prev, mid_next = lax.optimization_barrier(
-        (corner_l, corner_r, left, right, mid_prev, mid_next)
+    corner_l, corner_r, side, mid_prev, mid_next = lax.optimization_barrier(
+        (corner_l, corner_r, side, mid_prev, mid_next)
     )
     mid_b = shifted(mid_next, "gx", 1)
     mid_a = shifted(mid_prev, "gx", -1)
 
     own = (electric, magnetic, permittivity, aux)
     x_far = (NARR // 2, 2 * FAR, FARW * LANES)
-    far_prev, far_next = call(pack_far, (x_far, x_far), 6, 2)(*own, left, right)
-    far_prev, far_next, left, right = lax.optimization_barrier((far_prev, far_next, left, right))
+    far_prev, far_next = call(pack_far, (x_far, x_far), 8, 2)(*own, *side)
+    far_prev, far_next, side = lax.optimization_barrier((far_prev, far_next, side))
     waves = jnp.asarray(
         time_step
         * np.sin(np.arange(1, STEPS + 1).astype(np.float32) * np.float32(omega_source * time_step)),
@@ -519,8 +522,8 @@
     tail = PAD + YV
     held = tuple((k * many + tail, LANES) for k in (6, 6, 1, 2, 1))
     tags = pltpu.VMEM((many + tail, LANES), jnp.float32)
-    state = call(run_inside, held, 7, 30, in_specs=[smem] + [vmem] * 6, scratch_shapes=[tags])(
-        waves, *own, left, right
+    state = call(run_inside, held, 9, 30, in_specs=[smem] + [vmem] * 8, scratch_shapes=[tags])(
+        waves, *own, *side
     )
     far_prev, far_next, state = lax.optimization_barrier((far_prev, far_next, state))
     far_b = shifted(far_next, "gx", 1)

time: 117 us -> 111 us (0.949); the launches traced: 115 us -> 110 us
  waiting for transfers between devices: 21.8 us -> 12.6 us
  starting transfers between devices: 25.5 us -> 29.4 us
    ppermute x10 -> x12, waiting for transfers between devices: 21.8 us -> 12.6 us  [shifted(): lax.ppermute(array, axis, [(i, (i + by) % count) for i in range(count)])]
    ppermute x10 -> x12, starting transfers between devices: 25.5 us -> 29.4 us  [shifted(): lax.ppermute(array, axis, [(i, (i + by) % count) for i in range(count)])]
  transfers between devices with their start and end apart: 10 -> 12, of which waited for: 5 -> 5; matrix products, arithmetic and copies ran while one was open for 0% -> 0% of each run, Pallas kernels for 36% -> 37%
where the time goes in v9:
time: 111 us; the launch traced here: 110 us
  Pallas kernels  54.5 us (49%)
  starting transfers between devices  29.4 us (26%)
  waiting for transfers between devices  12.6 us (11%)
  blocking collectives  12.2 us (11%)
    ppermute x12, starting transfers between devices, shifted(): lax.ppermute(array, axis, [(i, (i + by) % count) for i in range(count)])  29.4 us
    pallas_call x1, Pallas kernels, per_device(): call(run_inside, held, 9, 30, in_specs=[smem] + [vmem] * 8, scratch_shape...  17.5 us
    pallas_call x1, Pallas kernels, per_device(): call(run_near, (field, field) + held, 13, 12, in_specs=[smem] + [vmem] *...  15.9 us
    ppermute x12, waiting for transfers between devices, shifted(): lax.ppermute(array, axis, [(i, (i + by) % count) for i in range(count)])  12.6 us
    all_to_all x1, blocking collectives, per_device(): lax.all_to_all(packed.reshape(owners, 3, LANES), 'gy', split_axis=0, conc...  12.2 us
    pallas_call x1, Pallas kernels, per_device(): call(run_far, (field, field, (3 * owners, LANES)) + held, 12, 8, in_specs...  10.4 us
    pallas_call x1, Pallas kernels, per_device(): call(run_inside_rest, held, 6, 1, in_specs=[smem] + [vmem] * 5, input_out...  4.53 us
  transfers between devices with their start and end apart: 12, of which 5 were waited for; matrix products, arithmetic and copies ran while one was open for 0% of the time, Pallas kernels for 37%

profile of v9, /device:TPU:1, one launch (start us, length us, event | category | flops | bytes accessed | tf_op | source)
XLA Modules:
  0.0 110.4 jit_solution(18105682583637609431)
XLA Ops:
  0.6 2.2 %pack_near.1 = (f32[8,11008]{1,0:T(8,128)S(1)}, f32[8,11008]{1,0:T(8,128)S(1)}, f32[8,16640]{1,0:T(8,128)S(1)}, f32[8,16640]{1,0:T(8,128)S(1)}) custom-call(f32[2,3,32,2048]{3,2,1,0:T(8,128)} %e.6, f32[2,3,32,2048]{3,2,1,0:T(8,128)} %h.6, f32[32,2048]{1,0:T(8,128)} %eps.6, f32[2,32,64]{2,1,0:T(8,128)} %profile.2, s32[2,32]{1,0:T(2,128)} %plane.2), custom_call_target="tpu_custom_call" | custom-call | bytes 6000000 | tf_op jit(solution)/shard_map/pack_near/pallas_call | solution.py:486
  2.8 0.0 copy-start.5
  2.8 0.0 copy-start
  2.8 0.0 copy-start.1
  2.8 0.0 copy-start.2
  2.8 3.7 %collective-permute-start = (f32[8,11008]{1,0:T(8,128)S(1)}, f32[8,11008]{1,0:T(8,128)S(1)}, u32[]{:S(2)}, u32[]{:S(2)}) collective-permute-start(f32[8,11008]{1,0:T(8,128)S(1)} %get-tuple-element.73), channel_id=1, source_target_pairs={{0,16},{16,32},{32,48},{48,64},{64,80},{80,96},{96,112},{112,128},... | collective-permute-start | bytes 1056776 | tf_op jit(solution)/shard_map/ppermute | solution.py:39
  6.5 5.4 %collective-permute-start.1 = (f32[8,11008]{1,0:T(8,128)S(1)}, f32[8,11008]{1,0:T(8,128)S(1)}, u32[]{:S(2)}, u32[]{:S(2)}) collective-permute-start(f32[8,11008]{1,0:T(8,128)S(1)} %get-tuple-element.74), channel_id=1, source_target_pairs={{0,240},{16,0},{32,16},{48,32},{64,48},{80,64},{96,80},{112,96},{1... | collective-permute-start | bytes 1056776 | tf_op jit(solution)/shard_map/ppermute | solution.py:39
  11.9 1.8 %pack_side.1 = (f32[7,32,384]{2,1,0:T(8,128)S(1)}, f32[7,32,384]{2,1,0:T(8,128)S(1)}, f32[7,32,384]{2,1,0:T(8,128)S(1)}, f32[7,32,384]{2,1,0:T(8,128)S(1)}, f32[32,2048]{1,0:T(8,128)S(1)}) custom-call(f32[2,3,32,2048]{3,2,1,0:T(8,128)} %e.6, f32[2,3,32,2048]{3,2,1,0:T(8,128)} %h.6, f32[32,2048]{1,0:T(8,128)} %eps.6, f32[2,32,64]{2,1,0:T(8,128)} %profile.2, ...), custom_call_target="tpu_custom_call" | custom-call | bytes 9000000 | tf_op jit(solution)/shard_map/pack_side/pallas_call | solution.py:494
  13.7 2.2 %collective-permute-start.4 = (f32[7,32,384]{2,1,0:T(8,128)S(1)}, f32[7,32,384]{2,1,0:T(8,128)S(1)}, u32[]{:S(2)}, u32[]{:S(2)}) collective-permute-start(f32[7,32,384]{2,1,0:T(8,128)S(1)} %get-tuple-element.77), channel_id=1, source_target_pairs={{0,1},{1,2},{2,3},{3,4},{4,5},{5,6},{6,7},{7,8},{8,9},{9,10},{10,1... | collective-permute-start | bytes 1032200 | tf_op jit(solution)/shard_map/ppermute | solution.py:39
  15.9 0.1 collective-permute-start.5
  16.0 0.4 collective-permute-start.6
  16.4 4.6 %collective-permute-done.behind.edge_b = f32[8,11008]{1,0:T(8,128)S(1)} collective-permute-done((f32[8,11008]{1,0:T(8,128)S(1)}, f32[8,11008]{1,0:T(8,128)S(1)}, u32[]{:S(2)}, u32[]{:S(2)}) %collective-permute-start) | collective-permute-done | bytes 352288 | tf_op jit(solution)/shard_map/ppermute | solution.py:39
  20.9 1.5 %collective-permute-start.7 = (f32[7,32,384]{2,1,0:T(8,128)S(1)}, f32[7,32,384]{2,1,0:T(8,128)S(1)}, u32[]{:S(2)}, u32[]{:S(2)}) collective-permute-start(f32[7,32,384]{2,1,0:T(8,128)S(1)} %get-tuple-element.80), channel_id=1, source_target_pairs={{0,15},{1,0},{2,1},{3,2},{4,3},{5,4},{6,5},{7,6},{8,7},{9,8},{10,9... | collective-permute-start | bytes 1032200 | tf_op jit(solution)/shard_map/ppermute | solution.py:39
  22.5 1.8 %collective-permute-done.1.ahead.edge_a = f32[8,11008]{1,0:T(8,128)S(1)} collective-permute-done((f32[8,11008]{1,0:T(8,128)S(1)}, f32[8,11008]{1,0:T(8,128)S(1)}, u32[]{:S(2)}, u32[]{:S(2)}) %collective-permute-start.1) | collective-permute-done | bytes 352288 | tf_op jit(solution)/shard_map/ppermute | solution.py:39
  24.3 0.8 pack_corner.1
  25.2 3.1 %collective-permute-start.2 = (f32[14,16,384]{2,1,0:T(8,128)S(1)}, f32[14,16,384]{2,1,0:T(8,128)S(1)}, u32[]{:S(2)}, u32[]{:S(2)}) collective-permute-start(f32[14,16,384]{2,1,0:T(8,128)S(1)} %get-tuple-element.75), channel_id=1, source_target_pairs={{0,1},{1,2},{2,3},{3,4},{4,5},{5,6},{6,7},{7,8},{8,9},{9,10},{10,1... | collective-permute-start | bytes 1032200 | tf_op jit(solution)/shard_map/ppermute | solution.py:39
  28.2 0.0 collective-permute-done.4.left_lo
  28.2 1.5 %collective-permute-start.3 = (f32[14,16,384]{2,1,0:T(8,128)S(1)}, f32[14,16,384]{2,1,0:T(8,128)S(1)}, u32[]{:S(2)}, u32[]{:S(2)}) collective-permute-start(f32[14,16,384]{2,1,0:T(8,128)S(1)} %get-tuple-element.76), channel_id=1, source_target_pairs={{0,15},{1,0},{2,1},{3,2},{4,3},{5,4},{6,5},{7,6},{8,7},{9,8},{10,9... | collective-permute-start | bytes 1032200 | tf_op jit(solution)/shard_map/ppermute | solution.py:39
  29.7 0.0 copy-done.5
  29.7 0.2 convert_reduce_fusion
  29.9 0.0 collective-permute-done.5.left_hi
  29.9 0.0 collective-permute-done.6.right_lo
  29.9 0.0 collective-permute-done.7.right_hi
  29.9 2.5 %collective-permute-done.2.corner_l = f32[14,16,384]{2,1,0:T(8,128)S(1)} collective-permute-done((f32[14,16,384]{2,1,0:T(8,128)S(1)}, f32[14,16,384]{2,1,0:T(8,128)S(1)}, u32[]{:S(2)}, u32[]{:S(2)}) %collective-permute-start.2) | collective-permute-done | bytes 344096 | tf_op jit(solution)/shard_map/ppermute | solution.py:39
  32.4 2.8 %collective-permute-done.3.corner_r = f32[14,16,384]{2,1,0:T(8,128)S(1)} collective-permute-done((f32[14,16,384]{2,1,0:T(8,128)S(1)}, f32[14,16,384]{2,1,0:T(8,128)S(1)}, u32[]{:S(2)}, u32[]{:S(2)}) %collective-permute-start.3) | collective-permute-done | bytes 344096 | tf_op jit(solution)/shard_map/ppermute | solution.py:39
  35.2 1.1 collective-permute-start.8
  36.3 5.3 %collective-permute-start.9 = (f32[8,16640]{1,0:T(8,128)S(1)}, f32[8,16640]{1,0:T(8,128)S(1)}, u32[]{:S(2)}, u32[]{:S(2)}) collective-permute-start(f32[8,16640]{1,0:T(8,128)S(1)} %get-tuple-element.111), channel_id=1, source_target_pairs={{0,240},{16,0},{32,16},{48,32},{64,48},{80,64},{96,80},{112,96},{1... | collective-permute-start | bytes 1597448 | tf_op jit(solution)/shard_map/ppermute | solution.py:39
  41.6 0.0 copy-done
  41.6 0.0 copy-done.1
  41.6 0.0 copy-done.2
  41.6 0.0 copy-start.4
  41.6 0.2 pack_far.1
  41.8 0.4 copy-done.4
  42.3 0.0 copy-start.6
  42.3 17.5 %run_inside.1 = (f32[8096,128]{1,0:T(8,128)S(1)}, f32[8096,128]{1,0:T(8,128)S(1)}, f32[1376,128]{1,0:T(8,128)S(1)}, f32[2720,128]{1,0:T(8,128)S(1)}, f32[1376,128]{1,0:T(8,128)S(1)}) custom-call(f32[12]{0:T(128)S(1)} %copy-done.4, f32[2,3,32,2048]{3,2,1,0:T(8,128)S(1)} %copy-done, f32[2,3,32,2048]{3,2,1,0:T(8,128)S(1)} %copy-done.1, ...), custom_call_target="tpu_custom_call" | custom-call | bytes 90000000 | tf_op jit(solution)/shard_map/run_inside/pallas_call | solution.py:525
  59.8 0.1 collective-permute-start.10
  59.9 5.1 %collective-permute-start.11 = (f32[7,8,2560]{2,1,0:T(8,128)S(1)}, f32[7,8,2560]{2,1,0:T(8,128)S(1)}, u32[]{:S(2)}, u32[]{:S(2)}) collective-permute-start(f32[7,8,2560]{2,1,0:T(8,128)S(1)} %get-tuple-element.123), channel_id=1, source_target_pairs={{0,240},{16,0},{32,16},{48,32},{64,48},{80,64},{96,80},{112,96},{1... | collective-permute-start | bytes 1720328 | tf_op jit(solution)/shard_map/ppermute | solution.py:39
  64.9 0.0 copy-done.6
  64.9 0.2 fusion.1.marks
  65.2 4.5 %run_inside_rest.1 = (f32[8096,128]{1,0:T(8,128)S(1)}, f32[8096,128]{1,0:T(8,128)S(1)}, f32[1376,128]{1,0:T(8,128)S(1)}, f32[2720,128]{1,0:T(8,128)S(1)}, f32[1376,128]{1,0:T(8,128)S(1)}) custom-call(f32[12]{0:T(128)S(1)} %copy-done.4, ...), custom_call_target="tpu_custom_call", output_to_operand_aliasing={{0}: (1, {}), {1}: (2, {}), {2}: (3, {}), {3}: (4, {}), {4}... | custom-call | bytes 3000000 | tf_op jit(solution)/shard_map/run_inside_rest/pallas_call | solution.py:532
  69.7 0.0 collective-permute-done.8.mid_b
  69.7 0.0 collective-permute-done.9.mid_a
  69.7 15.9 %run_near.1 = (f32[2,3,32,2048]{3,2,1,0:T(8,128)}, f32[2,3,32,2048]{3,2,1,0:T(8,128)}, f32[8096,128]{1,0:T(8,128)S(1)}, f32[8096,128]{1,0:T(8,128)S(1)}, f32[137...) custom-call(f32[12]{0:T(128)S(1)} %copy-done.4, ...), custom_call_target="tpu_custom_call", output_to_operand_aliasing={{2}: (1, {}), {3}: (2, {}), {4}: (3, {}), {5}: (4, {}), {6}... | custom-call | bytes 36000000 | tf_op jit(solution)/shard_map/run_near/pallas_call | solution.py:561
  85.6 0.0 collective-permute-done.10.far_b
  85.6 0.9 collective-permute-done.11.far_a
  86.6 0.0 copy-start.3
  86.6 10.4 %run_far.1 = (f32[2,3,32,2048]{3,2,1,0:T(8,128)}, f32[2,3,32,2048]{3,2,1,0:T(8,128)}, f32[48,128]{1,0:T(8,128)S(1)}, f32[8096,128]{1,0:T(8,128)S(1)}, f32[8096,1...) custom-call(f32[12]{0:T(128)S(1)} %copy-done.4, ...), custom_call_target="tpu_custom_call", output_to_operand_aliasing={{0}: (6, {}), {1}: (7, {}), {3}: (1, {}), {4}: (2, {}), {5}... | custom-call | bytes 24000000 | tf_op jit(solution)/shard_map/run_far/pallas_call | solution.py:572
  97.0 12.2 %all_to_all.5 = f32[16,3,128]{2,1,0:T(4,128)S(1)} all-to-all(f32[16,3,128]{2,1,0:T(4,128)S(1)} %reshape.36), channel_id=1, replica_groups=mesh['gx'=16,'gy'=16] {'gy'}, dimensions={0} | all-to-all | bytes 49152 | tf_op jit(solution)/shard_map/all_to_all | solution.py:583
  109.2 0.0 copy-done.3
  109.2 1.2 %collect.1 = f32[4,128]{1,0:T(4,128)} custom-call(f32[48,128]{1,0:T(8,128)S(1)} %reshape.37.received, f32[128,128]{1,0:T(8,128)S(1)} %copy-done.3), custom_call_target="tpu_custom_call" | custom-call | bytes 3000000 | tf_op jit(solution)/shard_map/collect/pallas_call | solution.py:586
  (5 shorter events, 0.0 us)
Async XLA Ops:
  2.8 26.9 %copy-start.5 = (s32[1,1,16,1]{2,3,1,0:T(1,128)S(1)}, s32[1,1,16,1]{2,3,1,0:T(1,128)}, u32[]{:S(2)}) copy-start(s32[1,1,16,1]{2,3,1,0:T(1,128)} %param.14) | copy-start | bytes 196
  2.8 38.8 %copy-start = (f32[2,3,32,2048]{3,2,1,0:T(8,128)S(1)}, f32[2,3,32,2048]{3,2,1,0:T(8,128)}, u32[]{:S(2)}) copy-start(f32[2,3,32,2048]{3,2,1,0:T(8,128)} %e.6) | copy-start | bytes 4718596
  2.8 38.8 %copy-start.1 = (f32[2,3,32,2048]{3,2,1,0:T(8,128)S(1)}, f32[2,3,32,2048]{3,2,1,0:T(8,128)}, u32[]{:S(2)}) copy-start(f32[2,3,32,2048]{3,2,1,0:T(8,128)} %h.6) | copy-start | bytes 4718596
  2.8 38.8 %copy-start.2 = (f32[32,2048]{1,0:T(8,128)S(1)}, f32[32,2048]{1,0:T(8,128)}, u32[]{:S(2)}) copy-start(f32[32,2048]{1,0:T(8,128)} %eps.6) | copy-start | bytes 786436
  2.8 18.1 %collective-permute-start = (f32[8,11008]{1,0:T(8,128)S(1)}, f32[8,11008]{1,0:T(8,128)S(1)}, u32[]{:S(2)}, u32[]{:S(2)}) collective-permute-start(f32[8,11008]{1,0:T(8,128)S(1)} %get-tuple-element.73), channel_id=1, source_target_pairs={{0,16},{16,32},{32,48},{48,64},{64,80},{80,96},{96,112},{112,128},... | collective-permute-start | bytes 1056776 | tf_op jit(solution)/shard_map/ppermute | solution.py:39
  6.5 17.8 %collective-permute-start.1 = (f32[8,11008]{1,0:T(8,128)S(1)}, f32[8,11008]{1,0:T(8,128)S(1)}, u32[]{:S(2)}, u32[]{:S(2)}) collective-permute-start(f32[8,11008]{1,0:T(8,128)S(1)} %get-tuple-element.74), channel_id=1, source_target_pairs={{0,240},{16,0},{32,16},{48,32},{64,48},{80,64},{96,80},{112,96},{1... | collective-permute-start | bytes 1056776 | tf_op jit(solution)/shard_map/ppermute | solution.py:39
  13.7 14.6 %collective-permute-start.4 = (f32[7,32,384]{2,1,0:T(8,128)S(1)}, f32[7,32,384]{2,1,0:T(8,128)S(1)}, u32[]{:S(2)}, u32[]{:S(2)}) collective-permute-start(f32[7,32,384]{2,1,0:T(8,128)S(1)} %get-tuple-element.77), channel_id=1, source_target_pairs={{0,1},{1,2},{2,3},{3,4},{4,5},{5,6},{6,7},{7,8},{8,9},{9,10},{10,1... | collective-permute-start | bytes 1032200 | tf_op jit(solution)/shard_map/ppermute | solution.py:39
  15.9 14.0 %collective-permute-start.5 = (f32[7,32,384]{2,1,0:T(8,128)S(1)}, f32[7,32,384]{2,1,0:T(8,128)S(1)}, u32[]{:S(2)}, u32[]{:S(2)}) collective-permute-start(f32[7,32,384]{2,1,0:T(8,128)S(1)} %get-tuple-element.78), channel_id=1, source_target_pairs={{0,1},{1,2},{2,3},{3,4},{4,5},{5,6},{6,7},{7,8},{8,9},{9,10},{10,1... | collective-permute-start | bytes 1032200 | tf_op jit(solution)/shard_map/ppermute | solution.py:39
  16.0 13.9 %collective-permute-start.6 = (f32[7,32,384]{2,1,0:T(8,128)S(1)}, f32[7,32,384]{2,1,0:T(8,128)S(1)}, u32[]{:S(2)}, u32[]{:S(2)}) collective-permute-start(f32[7,32,384]{2,1,0:T(8,128)S(1)} %get-tuple-element.79), channel_id=1, source_target_pairs={{0,15},{1,0},{2,1},{3,2},{4,3},{5,4},{6,5},{7,6},{8,7},{9,8},{10,9... | collective-permute-start | bytes 1032200 | tf_op jit(solution)/shard_map/ppermute | solution.py:39
  20.9 8.9 %collective-permute-start.7 = (f32[7,32,384]{2,1,0:T(8,128)S(1)}, f32[7,32,384]{2,1,0:T(8,128)S(1)}, u32[]{:S(2)}, u32[]{:S(2)}) collective-permute-start(f32[7,32,384]{2,1,0:T(8,128)S(1)} %get-tuple-element.80), channel_id=1, source_target_pairs={{0,15},{1,0},{2,1},{3,2},{4,3},{5,4},{6,5},{7,6},{8,7},{9,8},{10,9... | collective-permute-start | bytes 1032200 | tf_op jit(solution)/shard_map/ppermute | solution.py:39
  25.2 7.3 %collective-permute-start.2 = (f32[14,16,384]{2,1,0:T(8,128)S(1)}, f32[14,16,384]{2,1,0:T(8,128)S(1)}, u32[]{:S(2)}, u32[]{:S(2)}) collective-permute-start(f32[14,16,384]{2,1,0:T(8,128)S(1)} %get-tuple-element.75), channel_id=1, source_target_pairs={{0,1},{1,2},{2,3},{3,4},{4,5},{5,6},{6,7},{7,8},{8,9},{9,10},{10,1... | collective-permute-start | bytes 1032200 | tf_op jit(solution)/shard_map/ppermute | solution.py:39
  28.2 7.0 %collective-permute-start.3 = (f32[14,16,384]{2,1,0:T(8,128)S(1)}, f32[14,16,384]{2,1,0:T(8,128)S(1)}, u32[]{:S(2)}, u32[]{:S(2)}) collective-permute-start(f32[14,16,384]{2,1,0:T(8,128)S(1)} %get-tuple-element.76), channel_id=1, source_target_pairs={{0,15},{1,0},{2,1},{3,2},{4,3},{5,4},{6,5},{7,6},{8,7},{9,8},{10,9... | collective-permute-start | bytes 1032200 | tf_op jit(solution)/shard_map/ppermute | solution.py:39
  35.2 34.5 %collective-permute-start.8 = (f32[8,16640]{1,0:T(8,128)S(1)}, f32[8,16640]{1,0:T(8,128)S(1)}, u32[]{:S(2)}, u32[]{:S(2)}) collective-permute-start(f32[8,16640]{1,0:T(8,128)S(1)} %get-tuple-element.110), channel_id=1, source_target_pairs={{0,16},{16,32},{32,48},{48,64},{64,80},{80,96},{96,112},{112,128},... | collective-permute-start | bytes 1597448 | tf_op jit(solution)/shard_map/ppermute | solution.py:39
  36.3 33.4 %collective-permute-start.9 = (f32[8,16640]{1,0:T(8,128)S(1)}, f32[8,16640]{1,0:T(8,128)S(1)}, u32[]{:S(2)}, u32[]{:S(2)}) collective-permute-start(f32[8,16640]{1,0:T(8,128)S(1)} %get-tuple-element.111), channel_id=1, source_target_pairs={{0,240},{16,0},{32,16},{48,32},{64,48},{80,64},{96,80},{112,96},{1... | collective-permute-start | bytes 1597448 | tf_op jit(solution)/shard_map/ppermute | solution.py:39
  41.6 0.7 copy-start.4
  42.3 22.7 %copy-start.6 = (s32[1,1,16]{2,1,0:T(1,128)S(1)}, s32[1,1,16]{2,1,0:T(1,128)}, u32[]{:S(2)}) copy-start(s32[1,1,16]{2,1,0:T(1,128)} %param.15) | copy-start | bytes 196
  59.8 25.8 %collective-permute-start.10 = (f32[7,8,2560]{2,1,0:T(8,128)S(1)}, f32[7,8,2560]{2,1,0:T(8,128)S(1)}, u32[]{:S(2)}, u32[]{:S(2)}) collective-permute-start(f32[7,8,2560]{2,1,0:T(8,128)S(1)} %get-tuple-element.122), channel_id=1, source_target_pairs={{0,16},{16,32},{32,48},{48,64},{64,80},{80,96},{96,112},{112,128},... | collective-permute-start | bytes 1720328 | tf_op jit(solution)/shard_map/ppermute | solution.py:39
  59.9 26.7 %collective-permute-start.11 = (f32[7,8,2560]{2,1,0:T(8,128)S(1)}, f32[7,8,2560]{2,1,0:T(8,128)S(1)}, u32[]{:S(2)}, u32[]{:S(2)}) collective-permute-start(f32[7,8,2560]{2,1,0:T(8,128)S(1)} %get-tuple-element.123), channel_id=1, source_target_pairs={{0,240},{16,0},{32,16},{48,32},{64,48},{80,64},{96,80},{112,96},{1... | collective-permute-start | bytes 1720328 | tf_op jit(solution)/shard_map/ppermute | solution.py:39
  86.6 22.6 %copy-start.3 = (f32[128,128]{1,0:T(8,128)S(1)}, f32[128,128]{1,0:T(8,128)}, u32[]{:S(2)}) copy-start(f32[128,128]{1,0:T(8,128)} %filter_matrix.1) | copy-start | bytes 196612

commit v10 on v9

--- a/solution.py
+++ b/solution.py
@@ -31,7 +31,7 @@
 HIGH = lax.Precision.HIGHEST
 PART = NARR // 2
 EXTRA = 6 * LANES
-CUT = 8
+CUT = 9
 
 
 def shifted(array, axis, by):
@@ -302,11 +302,11 @@
                 return 0
 
             lax.fori_loop(0, count // 8, group, 0)
-            for size in (4, 2, 1):
-                start = x + count // (2 * size) * (2 * size)
-
-                @pl.when(count % (2 * size) >= size)
-                def _(size=size, start=start):
+            start = x + count // 8 * 8
+            for size in range(1, 8):
+
+                @pl.when(count % 8 == size)
+                def _(size=size):
                     for i in range(size):
                         one(start + i)
 

time: 111 us -> 112 us (level)
  waiting for transfers between devices: 12.6 us -> 14.4 us
    ppermute x12, waiting for transfers between devices: 12.6 us -> 14.4 us  [shifted(): lax.ppermute(array, axis, [(i, (i + by) % count) for i in range(count)])]
    pallas_call x1, Pallas kernels: 4.53 us -> 3.2 us  [per_device(): call(run_inside_rest, held, 6, 1, in_specs=[smem] + [vmem] * 5, input_out...]
  transfers between devices with their start and end apart: 12 -> 12, of which waited for: 5 -> 5; matrix products, arithmetic and copies ran while one was open for 0% -> 0% of each run, Pallas kernels for 37% -> 36%
where the time goes in v10:
time: 112 us; the launch traced here: 111 us
  Pallas kernels  53.8 us (48%)
  starting transfers between devices  29.4 us (26%)
  waiting for transfers between devices  14.4 us (13%)
  blocking collectives  12 us (11%)
    ppermute x12, starting transfers between devices, shifted(): lax.ppermute(array, axis, [(i, (i + by) % count) for i in range(count)])  29.4 us
    pallas_call x1, Pallas kernels, per_device(): call(run_inside, held, 9, 30, in_specs=[smem] + [vmem] * 8, scratch_shape...  18.2 us
    pallas_call x1, Pallas kernels, per_device(): call(run_near, (field, field) + held, 13, 12, in_specs=[smem] + [vmem] *...  15.9 us
    ppermute x12, waiting for transfers between devices, shifted(): lax.ppermute(array, axis, [(i, (i + by) % count) for i in range(count)])  14.4 us
    all_to_all x1, blocking collectives, per_device(): lax.all_to_all(packed.reshape(owners, 3, LANES), 'gy', split_axis=0, conc...  12 us
    pallas_call x1, Pallas kernels, per_device(): call(run_far, (field, field, (3 * owners, LANES)) + held, 12, 8, in_specs...  10.4 us
    pallas_call x1, Pallas kernels, per_device(): call(run_inside_rest, held, 6, 1, in_specs=[smem] + [vmem] * 5, input_out...  3.2 us
  transfers between devices with their start and end apart: 12, of which 5 were waited for; matrix products, arithmetic and copies ran while one was open for 0% of the time, Pallas kernels for 36%

profile of v10, /device:TPU:1, one launch (start us, length us, event | category | flops | bytes accessed | tf_op | source)
XLA Modules:
  0.0 111.3 jit_solution(1440747375080122046)
XLA Ops:
  0.6 2.2 %pack_near.1 = (f32[8,11008]{1,0:T(8,128)S(1)}, f32[8,11008]{1,0:T(8,128)S(1)}, f32[8,16640]{1,0:T(8,128)S(1)}, f32[8,16640]{1,0:T(8,128)S(1)}) custom-call(f32[2,3,32,2048]{3,2,1,0:T(8,128)} %e.6, f32[2,3,32,2048]{3,2,1,0:T(8,128)} %h.6, f32[32,2048]{1,0:T(8,128)} %eps.6, f32[2,32,64]{2,1,0:T(8,128)} %profile.2, s32[2,32]{1,0:T(2,128)} %plane.2), custom_call_target="tpu_custom_call" | custom-call | bytes 6000000 | tf_op jit(solution)/shard_map/pack_near/pallas_call | solution.py:486
  2.8 0.0 copy-start.5
  2.8 0.0 copy-start
  2.8 0.0 copy-start.1
  2.8 0.0 copy-start.2
  2.8 3.7 %collective-permute-start = (f32[8,11008]{1,0:T(8,128)S(1)}, f32[8,11008]{1,0:T(8,128)S(1)}, u32[]{:S(2)}, u32[]{:S(2)}) collective-permute-start(f32[8,11008]{1,0:T(8,128)S(1)} %get-tuple-element.73), channel_id=1, source_target_pairs={{0,16},{16,32},{32,48},{48,64},{64,80},{80,96},{96,112},{112,128},... | collective-permute-start | bytes 1056776 | tf_op jit(solution)/shard_map/ppermute | solution.py:39
  6.5 5.4 %collective-permute-start.1 = (f32[8,11008]{1,0:T(8,128)S(1)}, f32[8,11008]{1,0:T(8,128)S(1)}, u32[]{:S(2)}, u32[]{:S(2)}) collective-permute-start(f32[8,11008]{1,0:T(8,128)S(1)} %get-tuple-element.74), channel_id=1, source_target_pairs={{0,240},{16,0},{32,16},{48,32},{64,48},{80,64},{96,80},{112,96},{1... | collective-permute-start | bytes 1056776 | tf_op jit(solution)/shard_map/ppermute | solution.py:39
  11.9 1.8 %pack_side.1 = (f32[7,32,384]{2,1,0:T(8,128)S(1)}, f32[7,32,384]{2,1,0:T(8,128)S(1)}, f32[7,32,384]{2,1,0:T(8,128)S(1)}, f32[7,32,384]{2,1,0:T(8,128)S(1)}, f32[32,2048]{1,0:T(8,128)S(1)}) custom-call(f32[2,3,32,2048]{3,2,1,0:T(8,128)} %e.6, f32[2,3,32,2048]{3,2,1,0:T(8,128)} %h.6, f32[32,2048]{1,0:T(8,128)} %eps.6, f32[2,32,64]{2,1,0:T(8,128)} %profile.2, ...), custom_call_target="tpu_custom_call" | custom-call | bytes 9000000 | tf_op jit(solution)/shard_map/pack_side/pallas_call | solution.py:494
  13.7 2.2 %collective-permute-start.4 = (f32[7,32,384]{2,1,0:T(8,128)S(1)}, f32[7,32,384]{2,1,0:T(8,128)S(1)}, u32[]{:S(2)}, u32[]{:S(2)}) collective-permute-start(f32[7,32,384]{2,1,0:T(8,128)S(1)} %get-tuple-element.77), channel_id=1, source_target_pairs={{0,1},{1,2},{2,3},{3,4},{4,5},{5,6},{6,7},{7,8},{8,9},{9,10},{10,1... | collective-permute-start | bytes 1032200 | tf_op jit(solution)/shard_map/ppermute | solution.py:39
  15.9 0.1 collective-permute-start.5
  16.0 0.4 collective-permute-start.6
  16.4 4.6 %collective-permute-done.behind.edge_b = f32[8,11008]{1,0:T(8,128)S(1)} collective-permute-done((f32[8,11008]{1,0:T(8,128)S(1)}, f32[8,11008]{1,0:T(8,128)S(1)}, u32[]{:S(2)}, u32[]{:S(2)}) %collective-permute-start) | collective-permute-done | bytes 352288 | tf_op jit(solution)/shard_map/ppermute | solution.py:39
  20.9 1.5 %collective-permute-start.7 = (f32[7,32,384]{2,1,0:T(8,128)S(1)}, f32[7,32,384]{2,1,0:T(8,128)S(1)}, u32[]{:S(2)}, u32[]{:S(2)}) collective-permute-start(f32[7,32,384]{2,1,0:T(8,128)S(1)} %get-tuple-element.80), channel_id=1, source_target_pairs={{0,15},{1,0},{2,1},{3,2},{4,3},{5,4},{6,5},{7,6},{8,7},{9,8},{10,9... | collective-permute-start | bytes 1032200 | tf_op jit(solution)/shard_map/ppermute | solution.py:39
  22.5 1.8 %collective-permute-done.1.ahead.edge_a = f32[8,11008]{1,0:T(8,128)S(1)} collective-permute-done((f32[8,11008]{1,0:T(8,128)S(1)}, f32[8,11008]{1,0:T(8,128)S(1)}, u32[]{:S(2)}, u32[]{:S(2)}) %collective-permute-start.1) | collective-permute-done | bytes 352288 | tf_op jit(solution)/shard_map/ppermute | solution.py:39
  24.3 0.8 pack_corner.1
  25.2 3.1 %collective-permute-start.2 = (f32[14,16,384]{2,1,0:T(8,128)S(1)}, f32[14,16,384]{2,1,0:T(8,128)S(1)}, u32[]{:S(2)}, u32[]{:S(2)}) collective-permute-start(f32[14,16,384]{2,1,0:T(8,128)S(1)} %get-tuple-element.75), channel_id=1, source_target_pairs={{0,1},{1,2},{2,3},{3,4},{4,5},{5,6},{6,7},{7,8},{8,9},{9,10},{10,1... | collective-permute-start | bytes 1032200 | tf_op jit(solution)/shard_map/ppermute | solution.py:39
  28.2 0.0 collective-permute-done.4.left_lo
  28.2 1.5 %collective-permute-start.3 = (f32[14,16,384]{2,1,0:T(8,128)S(1)}, f32[14,16,384]{2,1,0:T(8,128)S(1)}, u32[]{:S(2)}, u32[]{:S(2)}) collective-permute-start(f32[14,16,384]{2,1,0:T(8,128)S(1)} %get-tuple-element.76), channel_id=1, source_target_pairs={{0,15},{1,0},{2,1},{3,2},{4,3},{5,4},{6,5},{7,6},{8,7},{9,8},{10,9... | collective-permute-start | bytes 1032200 | tf_op jit(solution)/shard_map/ppermute | solution.py:39
  29.7 0.0 copy-done.5
  29.7 0.2 convert_reduce_fusion
  29.9 0.0 collective-permute-done.5.left_hi
  29.9 0.0 collective-permute-done.6.right_lo
  29.9 0.0 collective-permute-done.7.right_hi
  29.9 2.5 %collective-permute-done.2.corner_l = f32[14,16,384]{2,1,0:T(8,128)S(1)} collective-permute-done((f32[14,16,384]{2,1,0:T(8,128)S(1)}, f32[14,16,384]{2,1,0:T(8,128)S(1)}, u32[]{:S(2)}, u32[]{:S(2)}) %collective-permute-start.2) | collective-permute-done | bytes 344096 | tf_op jit(solution)/shard_map/ppermute | solution.py:39
  32.4 2.8 %collective-permute-done.3.corner_r = f32[14,16,384]{2,1,0:T(8,128)S(1)} collective-permute-done((f32[14,16,384]{2,1,0:T(8,128)S(1)}, f32[14,16,384]{2,1,0:T(8,128)S(1)}, u32[]{:S(2)}, u32[]{:S(2)}) %collective-permute-start.3) | collective-permute-done | bytes 344096 | tf_op jit(solution)/shard_map/ppermute | solution.py:39
  35.2 1.1 collective-permute-start.8
  36.3 5.3 %collective-permute-start.9 = (f32[8,16640]{1,0:T(8,128)S(1)}, f32[8,16640]{1,0:T(8,128)S(1)}, u32[]{:S(2)}, u32[]{:S(2)}) collective-permute-start(f32[8,16640]{1,0:T(8,128)S(1)} %get-tuple-element.111), channel_id=1, source_target_pairs={{0,240},{16,0},{32,16},{48,32},{64,48},{80,64},{96,80},{112,96},{1... | collective-permute-start | bytes 1597448 | tf_op jit(solution)/shard_map/ppermute | solution.py:39
  41.6 0.0 copy-done
  41.6 0.0 copy-done.1
  41.6 0.0 copy-done.2
  41.6 0.0 copy-start.4
  41.6 0.2 pack_far.1
  41.8 0.4 copy-done.4
  42.3 0.0 copy-start.6
  42.3 18.2 %run_inside.1 = (f32[8096,128]{1,0:T(8,128)S(1)}, f32[8096,128]{1,0:T(8,128)S(1)}, f32[1376,128]{1,0:T(8,128)S(1)}, f32[2720,128]{1,0:T(8,128)S(1)}, f32[1376,128]{1,0:T(8,128)S(1)}) custom-call(f32[12]{0:T(128)S(1)} %copy-done.4, f32[2,3,32,2048]{3,2,1,0:T(8,128)S(1)} %copy-done, f32[2,3,32,2048]{3,2,1,0:T(8,128)S(1)} %copy-done.1, ...), custom_call_target="tpu_custom_call" | custom-call | bytes 90000000 | tf_op jit(solution)/shard_map/run_inside/pallas_call | solution.py:525
  60.4 0.1 collective-permute-start.10
  60.5 5.1 %collective-permute-start.11 = (f32[7,8,2560]{2,1,0:T(8,128)S(1)}, f32[7,8,2560]{2,1,0:T(8,128)S(1)}, u32[]{:S(2)}, u32[]{:S(2)}) collective-permute-start(f32[7,8,2560]{2,1,0:T(8,128)S(1)} %get-tuple-element.123), channel_id=1, source_target_pairs={{0,240},{16,0},{32,16},{48,32},{64,48},{80,64},{96,80},{112,96},{1... | collective-permute-start | bytes 1720328 | tf_op jit(solution)/shard_map/ppermute | solution.py:39
  65.6 0.0 copy-done.6
  65.6 0.2 fusion.1.marks
  65.8 3.2 %run_inside_rest.1 = (f32[8096,128]{1,0:T(8,128)S(1)}, f32[8096,128]{1,0:T(8,128)S(1)}, f32[1376,128]{1,0:T(8,128)S(1)}, f32[2720,128]{1,0:T(8,128)S(1)}, f32[1376,128]{1,0:T(8,128)S(1)}) custom-call(f32[12]{0:T(128)S(1)} %copy-done.4, ...), custom_call_target="tpu_custom_call", output_to_operand_aliasing={{0}: (1, {}), {1}: (2, {}), {2}: (3, {}), {3}: (4, {}), {4}... | custom-call | bytes 3000000 | tf_op jit(solution)/shard_map/run_inside_rest/pallas_call | solution.py:532
  69.0 0.0 collective-permute-done.8.mid_b
  69.0 0.0 collective-permute-done.9.mid_a
  69.1 15.9 %run_near.1 = (f32[2,3,32,2048]{3,2,1,0:T(8,128)}, f32[2,3,32,2048]{3,2,1,0:T(8,128)}, f32[8096,128]{1,0:T(8,128)S(1)}, f32[8096,128]{1,0:T(8,128)S(1)}, f32[137...) custom-call(f32[12]{0:T(128)S(1)} %copy-done.4, ...), custom_call_target="tpu_custom_call", output_to_operand_aliasing={{2}: (1, {}), {3}: (2, {}), {4}: (3, {}), {5}: (4, {}), {6}... | custom-call | bytes 36000000 | tf_op jit(solution)/shard_map/run_near/pallas_call | solution.py:561
  85.0 0.0 collective-permute-done.10.far_b
  85.0 2.7 %collective-permute-done.11.far_a = f32[7,8,2560]{2,1,0:T(8,128)S(1)} collective-permute-done((f32[7,8,2560]{2,1,0:T(8,128)S(1)}, f32[7,8,2560]{2,1,0:T(8,128)S(1)}, u32[]{:S(2)}, u32[]{:S(2)}) %collective-permute-start.11) | collective-permute-done | bytes 573472 | tf_op jit(solution)/shard_map/ppermute | solution.py:39
  87.7 0.0 copy-start.3
  87.7 10.4 %run_far.1 = (f32[2,3,32,2048]{3,2,1,0:T(8,128)}, f32[2,3,32,2048]{3,2,1,0:T(8,128)}, f32[48,128]{1,0:T(8,128)S(1)}, f32[8096,128]{1,0:T(8,128)S(1)}, f32[8096,1...) custom-call(f32[12]{0:T(128)S(1)} %copy-done.4, ...), custom_call_target="tpu_custom_call", output_to_operand_aliasing={{0}: (6, {}), {1}: (7, {}), {3}: (1, {}), {4}: (2, {}), {5}... | custom-call | bytes 24000000 | tf_op jit(solution)/shard_map/run_far/pallas_call | solution.py:572
  98.1 12.0 %all_to_all.5 = f32[16,3,128]{2,1,0:T(4,128)S(1)} all-to-all(f32[16,3,128]{2,1,0:T(4,128)S(1)} %reshape.36), channel_id=1, replica_groups=mesh['gx'=16,'gy'=16] {'gy'}, dimensions={0} | all-to-all | bytes 49152 | tf_op jit(solution)/shard_map/all_to_all | solution.py:583
  110.1 0.0 copy-done.3
  110.1 1.2 %collect.1 = f32[4,128]{1,0:T(4,128)} custom-call(f32[48,128]{1,0:T(8,128)S(1)} %reshape.37.received, f32[128,128]{1,0:T(8,128)S(1)} %copy-done.3), custom_call_target="tpu_custom_call" | custom-call | bytes 3000000 | tf_op jit(solution)/shard_map/collect/pallas_call | solution.py:586
  (5 shorter events, 0.0 us)
Async XLA Ops:
  2.8 26.9 %copy-start.5 = (s32[1,1,16,1]{2,3,1,0:T(1,128)S(1)}, s32[1,1,16,1]{2,3,1,0:T(1,128)}, u32[]{:S(2)}) copy-start(s32[1,1,16,1]{2,3,1,0:T(1,128)} %param.14) | copy-start | bytes 196
  2.8 38.8 %copy-start = (f32[2,3,32,2048]{3,2,1,0:T(8,128)S(1)}, f32[2,3,32,2048]{3,2,1,0:T(8,128)}, u32[]{:S(2)}) copy-start(f32[2,3,32,2048]{3,2,1,0:T(8,128)} %e.6) | copy-start | bytes 4718596
  2.8 38.8 %copy-start.1 = (f32[2,3,32,2048]{3,2,1,0:T(8,128)S(1)}, f32[2,3,32,2048]{3,2,1,0:T(8,128)}, u32[]{:S(2)}) copy-start(f32[2,3,32,2048]{3,2,1,0:T(8,128)} %h.6) | copy-start | bytes 4718596
  2.8 38.8 %copy-start.2 = (f32[32,2048]{1,0:T(8,128)S(1)}, f32[32,2048]{1,0:T(8,128)}, u32[]{:S(2)}) copy-start(f32[32,2048]{1,0:T(8,128)} %eps.6) | copy-start | bytes 786436
  2.8 18.1 %collective-permute-start = (f32[8,11008]{1,0:T(8,128)S(1)}, f32[8,11008]{1,0:T(8,128)S(1)}, u32[]{:S(2)}, u32[]{:S(2)}) collective-permute-start(f32[8,11008]{1,0:T(8,128)S(1)} %get-tuple-element.73), channel_id=1, source_target_pairs={{0,16},{16,32},{32,48},{48,64},{64,80},{80,96},{96,112},{112,128},... | collective-permute-start | bytes 1056776 | tf_op jit(solution)/shard_map/ppermute | solution.py:39
  6.5 17.8 %collective-permute-start.1 = (f32[8,11008]{1,0:T(8,128)S(1)}, f32[8,11008]{1,0:T(8,128)S(1)}, u32[]{:S(2)}, u32[]{:S(2)}) collective-permute-start(f32[8,11008]{1,0:T(8,128)S(1)} %get-tuple-element.74), channel_id=1, source_target_pairs={{0,240},{16,0},{32,16},{48,32},{64,48},{80,64},{96,80},{112,96},{1... | collective-permute-start | bytes 1056776 | tf_op jit(solution)/shard_map/ppermute | solution.py:39
  13.7 14.6 %collective-permute-start.4 = (f32[7,32,384]{2,1,0:T(8,128)S(1)}, f32[7,32,384]{2,1,0:T(8,128)S(1)}, u32[]{:S(2)}, u32[]{:S(2)}) collective-permute-start(f32[7,32,384]{2,1,0:T(8,128)S(1)} %get-tuple-element.77), channel_id=1, source_target_pairs={{0,1},{1,2},{2,3},{3,4},{4,5},{5,6},{6,7},{7,8},{8,9},{9,10},{10,1... | collective-permute-start | bytes 1032200 | tf_op jit(solution)/shard_map/ppermute | solution.py:39
  15.9 14.0 %collective-permute-start.5 = (f32[7,32,384]{2,1,0:T(8,128)S(1)}, f32[7,32,384]{2,1,0:T(8,128)S(1)}, u32[]{:S(2)}, u32[]{:S(2)}) collective-permute-start(f32[7,32,384]{2,1,0:T(8,128)S(1)} %get-tuple-element.78), channel_id=1, source_target_pairs={{0,1},{1,2},{2,3},{3,4},{4,5},{5,6},{6,7},{7,8},{8,9},{9,10},{10,1... | collective-permute-start | bytes 1032200 | tf_op jit(solution)/shard_map/ppermute | solution.py:39
  16.0 13.9 %collective-permute-start.6 = (f32[7,32,384]{2,1,0:T(8,128)S(1)}, f32[7,32,384]{2,1,0:T(8,128)S(1)}, u32[]{:S(2)}, u32[]{:S(2)}) collective-permute-start(f32[7,32,384]{2,1,0:T(8,128)S(1)} %get-tuple-element.79), channel_id=1, source_target_pairs={{0,15},{1,0},{2,1},{3,2},{4,3},{5,4},{6,5},{7,6},{8,7},{9,8},{10,9... | collective-permute-start | bytes 1032200 | tf_op jit(solution)/shard_map/ppermute | solution.py:39
  20.9 8.9 %collective-permute-start.7 = (f32[7,32,384]{2,1,0:T(8,128)S(1)}, f32[7,32,384]{2,1,0:T(8,128)S(1)}, u32[]{:S(2)}, u32[]{:S(2)}) collective-permute-start(f32[7,32,384]{2,1,0:T(8,128)S(1)} %get-tuple-element.80), channel_id=1, source_target_pairs={{0,15},{1,0},{2,1},{3,2},{4,3},{5,4},{6,5},{7,6},{8,7},{9,8},{10,9... | collective-permute-start | bytes 1032200 | tf_op jit(solution)/shard_map/ppermute | solution.py:39
  25.2 7.3 %collective-permute-start.2 = (f32[14,16,384]{2,1,0:T(8,128)S(1)}, f32[14,16,384]{2,1,0:T(8,128)S(1)}, u32[]{:S(2)}, u32[]{:S(2)}) collective-permute-start(f32[14,16,384]{2,1,0:T(8,128)S(1)} %get-tuple-element.75), channel_id=1, source_target_pairs={{0,1},{1,2},{2,3},{3,4},{4,5},{5,6},{6,7},{7,8},{8,9},{9,10},{10,1... | collective-permute-start | bytes 1032200 | tf_op jit(solution)/shard_map/ppermute | solution.py:39
  28.2 7.0 %collective-permute-start.3 = (f32[14,16,384]{2,1,0:T(8,128)S(1)}, f32[14,16,384]{2,1,0:T(8,128)S(1)}, u32[]{:S(2)}, u32[]{:S(2)}) collective-permute-start(f32[14,16,384]{2,1,0:T(8,128)S(1)} %get-tuple-element.76), channel_id=1, source_target_pairs={{0,15},{1,0},{2,1},{3,2},{4,3},{5,4},{6,5},{7,6},{8,7},{9,8},{10,9... | collective-permute-start | bytes 1032200 | tf_op jit(solution)/shard_map/ppermute | solution.py:39
  35.2 33.8 %collective-permute-start.8 = (f32[8,16640]{1,0:T(8,128)S(1)}, f32[8,16640]{1,0:T(8,128)S(1)}, u32[]{:S(2)}, u32[]{:S(2)}) collective-permute-start(f32[8,16640]{1,0:T(8,128)S(1)} %get-tuple-element.110), channel_id=1, source_target_pairs={{0,16},{16,32},{32,48},{48,64},{64,80},{80,96},{96,112},{112,128},... | collective-permute-start | bytes 1597448 | tf_op jit(solution)/shard_map/ppermute | solution.py:39
  36.3 32.8 %collective-permute-start.9 = (f32[8,16640]{1,0:T(8,128)S(1)}, f32[8,16640]{1,0:T(8,128)S(1)}, u32[]{:S(2)}, u32[]{:S(2)}) collective-permute-start(f32[8,16640]{1,0:T(8,128)S(1)} %get-tuple-element.111), channel_id=1, source_target_pairs={{0,240},{16,0},{32,16},{48,32},{64,48},{80,64},{96,80},{112,96},{1... | collective-permute-start | bytes 1597448 | tf_op jit(solution)/shard_map/ppermute | solution.py:39
  41.6 0.7 copy-start.4
  42.3 23.3 %copy-start.6 = (s32[1,1,16]{2,1,0:T(1,128)S(1)}, s32[1,1,16]{2,1,0:T(1,128)}, u32[]{:S(2)}) copy-start(s32[1,1,16]{2,1,0:T(1,128)} %param.15) | copy-start | bytes 196
  60.4 24.5 %collective-permute-start.10 = (f32[7,8,2560]{2,1,0:T(8,128)S(1)}, f32[7,8,2560]{2,1,0:T(8,128)S(1)}, u32[]{:S(2)}, u32[]{:S(2)}) collective-permute-start(f32[7,8,2560]{2,1,0:T(8,128)S(1)} %get-tuple-element.122), channel_id=1, source_target_pairs={{0,16},{16,32},{32,48},{48,64},{64,80},{80,96},{96,112},{112,128},... | collective-permute-start | bytes 1720328 | tf_op jit(solution)/shard_map/ppermute | solution.py:39
  60.5 27.1 %collective-permute-start.11 = (f32[7,8,2560]{2,1,0:T(8,128)S(1)}, f32[7,8,2560]{2,1,0:T(8,128)S(1)}, u32[]{:S(2)}, u32[]{:S(2)}) collective-permute-start(f32[7,8,2560]{2,1,0:T(8,128)S(1)} %get-tuple-element.123), channel_id=1, source_target_pairs={{0,240},{16,0},{32,16},{48,32},{64,48},{80,64},{96,80},{112,96},{1... | collective-permute-start | bytes 1720328 | tf_op jit(solution)/shard_map/ppermute | solution.py:39
  87.7 22.4 %copy-start.3 = (f32[128,128]{1,0:T(8,128)S(1)}, f32[128,128]{1,0:T(8,128)}, u32[]{:S(2)}) copy-start(f32[128,128]{1,0:T(8,128)} %filter_matrix.1) | copy-start | bytes 196612
